TPU v7x, 128 devices: a whole 4x4x4 slice. The times are simulated.
128 devices in a mesh: dp: 4 (over y), row: 8 (over x, core), col: 4 (over z).
Axes of the slice: x: 4, y: 4, z: 4, core: 2. Of those that a mesh axis runs over, the one named last changes fastest.
Arguments:
- patches: bfloat16 [8, 128, 128, 768], P('dp', 'row', 'col'), may hold values from -64 to 64
- keep_mask: int32 [8, 128, 128], P('dp', 'row', 'col'), may hold values from 0 to 1, as said below
- mask_token: bfloat16 [768], replicated, may hold values from -6 to 6
- qkv_weight: bfloat16 [768, 2304], replicated, may hold values from -2 to 2
- out_weight: bfloat16 [768, 768], replicated, may hold values from -0.21875 to 0.21875
- up_weight: bfloat16 [768, 3072], P(None, 'dp'), may hold values from -0.21875 to 0.21875
- down_weight: bfloat16 [3072, 768], P('dp'), may hold values from -0.109375 to 0.109375
- dec_proj: bfloat16 [768, 256], replicated, may hold values from -0.21875 to 0.21875
- conv_weight: bfloat16 [2, 9, 256, 256], replicated, may hold values from -0.125 to 0.125
- head_weight: bfloat16 [256, 128], replicated, may hold values from -0.375 to 0.375
Outputs:
- recon: bfloat16 [8, 128, 128, 128], P('dp', 'row', 'col')
Inputs may be any that keep to these rules, and one draw needn't show every extreme that they name: `keep_mask`: each sample has exactly 4096 ones; in every sample the 16 x 32 tile of some device is all ones.
All inputs are finite; a program needn't handle non-finite values.
Results may differ from a plain program's by a relative error of at most 0.015.
Values may be sent and summed in bfloat16 or wider, within the bound.
No kernel may reach another device: no remote copies, remote signals or barrier semaphores. Data moves between devices by JAX's collectives and lax.ppermute only.
A program may use at most 192 MiB of HBM per device.

v0:
```python
import jax
import jax.numpy as jnp
from jax import lax
from jax.sharding import PartitionSpec as P

HEADS = 12
HD = 64


EPS = 1e-06
BLOCK = 512


def extended_2(cells, sides, width):
    for axis, dim in sides:
        count = lax.axis_size(axis)
        ends = count - 1
        head = lax.slice_in_dim(cells, 0, width, axis=dim)
        tail = lax.slice_in_dim(cells, cells.shape[dim] - width, cells.shape[dim], axis=dim)
        cells = jnp.concatenate(
            [
                lax.ppermute(tail, axis, [(i, (i + 1) % count) for i in range(ends)]),
                cells,
                lax.ppermute(head, axis, [((i + 1) % count, i) for i in range(ends)]),
            ],
            axis=dim,
        )
    return cells


def normalize(rows):
    wide = rows.astype(jnp.float32)
    mean = jnp.mean(wide, -1, keepdims=True)
    centred = wide - mean
    var = jnp.mean(centred * centred, -1, keepdims=True)
    return (centred * lax.rsqrt(var + EPS)).astype(jnp.bfloat16)


def attend(carry, query, keys, values):
    run_max, run_sum, store = carry
    scores = jnp.einsum("sqhd,skhd->shqk", query, keys, preferred_element_type=jnp.float32) * 0.125
    new_max = jnp.maximum(run_max, jnp.max(scores, -1))
    shrink = jnp.exp(run_max - new_max)
    expo = jnp.exp(scores - new_max[..., None])
    run_sum = run_sum * shrink + jnp.sum(expo, -1)
    added = jnp.einsum(
        "shqk,skhd->sqhd", expo.astype(jnp.bfloat16), values, preferred_element_type=jnp.float32
    )
    store = store * jnp.swapaxes(shrink, 1, 2)[..., None] + added
    return (new_max, run_sum, store)


def convolve(extended, taps, out_h, out_w):
    total = None
    for first in range(3):
        for second in range(3):
            term = jnp.einsum(
                "shwc,cd->shwd",
                extended[:, first : first + out_h, second : second + out_w],
                taps[first * 3 + second],
                preferred_element_type=jnp.float32,
            )
            total = term if total is None else total + term
    return total


def border(field):
    return extended_2(field, (("row", 1), ("col", 2)), 1)


def shards(
    patches,
    keep_mask,
    mask_token,
    qkv_weight,
    out_weight,
    up_weight,
    down_weight,
    dec_proj,
    conv_weight,
    head_weight,
):
    peers = lax.axis_size(("row", "col"))
    me = lax.axis_index(("row", "col"))
    samples, tile_h, tile_w, width = patches.shape
    tile = tile_h * tile_w
    cap = tile // peers
    kept_dev = tile // 4
    flat_tokens = patches.reshape(samples, tile, width)
    flat_mask = keep_mask.reshape(samples, tile)
    counts = jnp.sum(flat_mask, 1)
    every_count = lax.all_gather(counts[None, :], ("row", "col"), axis=0, tiled=True)
    ends = jnp.cumsum(every_count, 0)
    starts = ends - every_count
    my_start = lax.dynamic_index_in_dim(starts, me, 0, keepdims=False)
    running = jnp.cumsum(flat_mask, 1)
    positions = jnp.arange(tile, dtype=jnp.int32)
    kept_at = jnp.sum((running[:, None, :] <= positions[None, :, None]).astype(jnp.int32), 2)
    peer_ids = jnp.arange(peers, dtype=jnp.int32)
    slot_ids = jnp.arange(cap, dtype=jnp.int32)
    sample_ids = jnp.arange(samples, dtype=jnp.int32)[None, :, None]
    local_rank = slot_ids[None, None, :] * peers + jnp.mod(
        peer_ids[:, None, None] - my_start[None, :, None], peers
    )
    live = local_rank < counts[None, :, None]
    source_pos = kept_at[sample_ids, jnp.minimum(local_rank, tile - 1)]
    outgoing = jnp.where(
        live[..., None], flat_tokens[sample_ids, source_pos], jnp.zeros((), jnp.bfloat16)
    )
    arrived = lax.all_to_all(outgoing, ("row", "col"), split_axis=0, concat_axis=0, tiled=True)
    order_rank = jnp.arange(kept_dev, dtype=jnp.int32) * peers + me
    source_of = jnp.sum((ends[:, :, None] <= order_rank[None, None, :]).astype(jnp.int32), 0)
    start_of = jnp.take_along_axis(starts.T, source_of, 1)
    slot_of = (order_rank[None, :] - start_of) // peers
    rows_in = arrived[source_of, jnp.arange(samples, dtype=jnp.int32)[:, None], slot_of]
    flat_rows = rows_in.reshape(samples * kept_dev, width)
    normed = normalize(flat_rows)
    init_carry = (
        jnp.full((samples, HEADS, kept_dev), -1e30, jnp.float32),
        jnp.zeros((samples, HEADS, kept_dev), jnp.float32),
        jnp.zeros((samples, kept_dev, HEADS, HD), jnp.float32),
    )
    qkv = jnp.dot(normed, qkv_weight, preferred_element_type=jnp.float32).astype(jnp.bfloat16)
    query = qkv[:, :width].reshape(samples, kept_dev, HEADS, HD)
    keys_local = qkv[:, width : 2 * width].reshape(samples, kept_dev, width)
    values_local = qkv[:, 2 * width :].reshape(samples, kept_dev, width)
    carry = init_carry
    keys_piece = lax.all_gather(keys_local, ("row", "col"), axis=1, tiled=True)
    values_piece = lax.all_gather(values_local, ("row", "col"), axis=1, tiled=True)
    count = keys_piece.shape[1]
    for lower in range(0, count, BLOCK):
        upper = min(count, lower + BLOCK)
        keys_block = keys_piece[:, lower:upper].reshape(samples, upper - lower, HEADS, HD)
        values_block = values_piece[:, lower:upper].reshape(samples, upper - lower, HEADS, HD)
        carry = attend(carry, query, keys_block, values_block)
    run_max, run_sum, store = carry
    attn = (
        (store / jnp.swapaxes(run_sum, 1, 2)[..., None])
        .astype(jnp.bfloat16)
        .reshape(samples * kept_dev, width)
    )
    x_one = (
        flat_rows.astype(jnp.float32)
        + jnp.dot(attn, out_weight, preferred_element_type=jnp.float32)
    ).astype(jnp.bfloat16)
    normed_two = normalize(x_one)
    hidden = jax.nn.gelu(
        jnp.dot(
            normed_two,
            lax.all_gather(up_weight, "dp", axis=1, tiled=True),
            preferred_element_type=jnp.float32,
        ),
        approximate=False,
    ).astype(jnp.bfloat16)
    feed = jnp.dot(
        hidden,
        lax.all_gather(down_weight, "dp", axis=0, tiled=True),
        preferred_element_type=jnp.float32,
    )
    encoded = (
        (x_one.astype(jnp.float32) + feed).astype(jnp.bfloat16).reshape(samples, kept_dev, width)
    )
    back_rank = slot_ids[None, None, :] * peers + jnp.mod(me - starts[:, :, None], peers)
    back_live = back_rank < every_count[:, :, None]
    back_row = jnp.minimum((starts[:, :, None] + back_rank) // peers, kept_dev - 1)
    returning = jnp.where(
        back_live[..., None], encoded[sample_ids, back_row], jnp.zeros((), jnp.bfloat16)
    )
    home = lax.all_to_all(returning, ("row", "col"), split_axis=0, concat_axis=0, tiled=True)
    kept_rank = jnp.maximum(running - 1, 0)
    target_peer = jnp.mod(my_start[:, None] + kept_rank, peers)
    token_back = home[
        target_peer, jnp.arange(samples, dtype=jnp.int32)[:, None], kept_rank // peers
    ]
    filled = jnp.where(flat_mask[..., None] == 1, token_back, mask_token[None, None, :]).reshape(
        samples, tile_h, tile_w, width
    )
    h_zero = jnp.dot(filled, dec_proj, preferred_element_type=jnp.float32).astype(jnp.bfloat16)
    conv_one = convolve(border(h_zero), conv_weight[0], tile_h, tile_w)
    h_one = (h_zero.astype(jnp.float32) + jax.nn.gelu(conv_one, approximate=False)).astype(
        jnp.bfloat16
    )
    conv_two = convolve(border(h_one), conv_weight[1], tile_h, tile_w)
    h_two = (h_one.astype(jnp.float32) + jax.nn.gelu(conv_two, approximate=False)).astype(
        jnp.bfloat16
    )
    return jnp.dot(h_two, head_weight, preferred_element_type=jnp.float32).astype(jnp.bfloat16)


def solution(mesh):
    return jax.shard_map(
        shards,
        mesh=mesh,
        in_specs=(
            P("dp", "row", "col", None),
            P("dp", "row", "col"),
            P(),
            P(),
            P(),
            P(None, "dp"),
            P("dp", None),
            P(),
            P(),
            P(),
        ),
        out_specs=P("dp", "row", "col", None),
        check_vma=False,
    )
```

profile of v0, /device:TPU:2, one launch (start us, length us, event | category | flops | bytes accessed | tf_op | source)
XLA Modules:
  0.0 475.2 jit_solution(3876837634357682865)
XLA Ops:
  11.7 16.4 %all-reduce = s32[64]{0:T(128)} all-reduce(s32[64]{0:T(128)S(1)} %dynamic-update-slice), channel_id=2, replica_groups=mesh['dp'=4,'row'=8,'col'=4] {'row','col'}, use_global_device_ids=true, to_apply=%add | all-reduce | flops 64 | bytes 512
  41.8 9.1 %gather_fusion = s32[1024]{0:T(1024)S(1)} fusion(s32[2,512]{1,0:T(2,128)S(1)} %convert_reduce_fusion, s32[1024]{0:T(1024)S(1)} %reshape.722), kind=kCustom, calls=%fused_computation | custom fusion | bytes 16384 | tf_op jit(solution)/shard_map/gather | solution.py:106
  53.8 31.4 %gather_fusion.1 = bf16[1024,768]{1,0:T(8,128)(2,1)} fusion(bf16[2,512,768]{2,1,0:T(8,128)(2,1)} %bitcast.404, s32[1024]{0:T(1024)S(1)} %reshape.728), kind=kCustom, calls=%fused_computation.1 | custom fusion | bytes 3153920 | tf_op jit(solution)/shard_map/gather | solution.py:108
  88.0 6.6 %all-to-all-start = ((bf16[32,2,16,768]{3,2,1,0:T(8,128)(2,1)}), bf16[32,2,16,768]{3,2,1,0:T(8,128)(2,1)}, u32[]{:S(2)}, u32[]{:S(2)}) async-start(bf16[32,2,16,768]{3,2,1,0:T(8,128)(2,1)} %broadcast_select_fusion), calls=%async_computation | async-start | bytes 3145728 | tf_op jit(solution)/shard_map/all_to_all | solution.py:110
  101.5 14.8 %all-to-all-done = bf16[32,2,16,768]{3,2,1,0:T(8,128)(2,1)} async-done(((bf16[32,2,16,768]{3,2,1,0:T(8,128)(2,1)}), bf16[32,2,16,768]{3,2,1,0:T(8,128)(2,1)}, u32[]{:S(2)}, u32[]{:S(2)}) %all-to-all-start) | async-done | bytes 1572896 | tf_op jit(solution)/shard_map/all_to_all | solution.py:110
  116.2 4.2 gather_fusion.2
  128.4 59.9 %all-gather.6.cloned.1.call-done = bf16[2,4096,768]{2,1,0:T(8,128)(2,1)} async-done(((bf16[2,128,768]{2,1,0:T(8,128)(2,1)}), bf16[2,4096,768]{2,1,0:T(8,128)(2,1)}) %all-gather.6.cloned.1.call-update) | async-done | bytes 12582928 | tf_op jit(solution)/shard_map/all_gather | solution.py:128
  188.3 9.0 %fusion.404 = (bf16[2,512,768]{2,1,0:T(8,128)(2,1)}, bf16[2,512,768]{2,1,0:T(8,128)(2,1)S(1)}, bf16[2,512,768]{2,1,0:T(8,128)(2,1)}, bf16[2,512,768]{2,1,0:T(8,1...) fusion(bf16[2,4096,768]{2,1,0:T(8,128)(2,1)} %all-gather.6.clon, ...), kind=kLoop, calls=%fused_computation.479 | loop fusion | bytes 25165824 | tf_op jit(solution)/shard_map/slice | solution.py:133
  201.6 5.3 %multiply_reduce_fusion.7 = (f32[2,12,128]{2,1,0:T(8,128)S(1)}, f32[2,12,128,512]{3,2,1,0:T(8,128)}) fusion(bf16[2,512,12,64]{1,3,2,0:T(8,128)(2,1)} %bitcast.436, bf16[2,128,12,64]{1,0,3,2:T(2,128)(2,1)S(1)} %reshape.700), kind=kOutput, calls=%fused_computation.21 | convolution fusion | flops 204469248 | bytes 8269824 | tf_op jit(solution)/shard_map/sqhd,skhd->shqk/dot_general | solution.py:41
  212.2 3.7 multiply_reduce_fusion.1
  217.7 3.7 multiply_reduce_fusion.2
  242.9 6.7 %fusion.12 = (f32[2,12,128]{2,1,0:T(8,128)S(1)}, f32[2,12,128]{2,1,0:T(8,128)S(1)}) fusion(f32[2,12,128,512]{3,2,1,0:T(8,128)} %get-tuple-element.68, f32[2,12,128]{2,1,0:T(8,128)S(1)} %get-tuple-element.15, f32[2,12,128]{2,1,0:T(8,128)S(1)} %get-tuple-element.14, f32[2,12,128,512]{3,2,1,0:T(8,128)} %get-tuple-element.66), kind=kLoop, calls=%fused_computation.34 | loop fusion | flops 9431040 | bytes 12632064 | tf_op jit(solution)/shard_map/reduce_sum | solution.py:45
  249.9 4.7 fusion.8
  254.6 8.6 %fusion.403 = (bf16[2,512,768]{2,1,0:T(8,128)(2,1)}, bf16[2,512,768]{2,1,0:T(8,128)(2,1)}, bf16[2,512,768]{2,1,0:T(8,128)(2,1)S(1)}, bf16[2,512,768]{2,1,0:T(8,1...) fusion(bf16[2,4096,768]{2,1,0:T(8,128)(2,1)} %all-gather.8.clon, ...), kind=kLoop, calls=%fused_computation.478 | loop fusion | bytes 25165824 | tf_op jit(solution)/shard_map/slice | solution.py:134
  280.6 6.3 %fusion.4 = (f32[2,12,128]{2,1,0:T(8,128)S(1)}, f32[2,12,128]{2,1,0:T(8,128)S(1)}) fusion(f32[2,12,128,512]{3,2,1,0:T(8,128)} %get-tuple-element.76, f32[2,12,128]{2,1,0:T(8,128)S(1)} %get-tuple-element.19, f32[2,12,128]{2,1,0:T(8,128)S(1)} %get-tuple-element.18, f32[2,12,128,512]{3,2,1,0:T(8,128)} %get-tuple-element.74), kind=kLoop, calls=%fused_computation.26 | loop fusion | flops 9431040 | bytes 12632064 | tf_op jit(solution)/shard_map/reduce_sum | solution.py:45
  287.3 5.0 %fusion = (f32[2,12,128]{2,1,0:T(8,128)S(1)}, f32[2,12,128]{2,1,0:T(8,128)S(1)}) fusion(f32[2,12,128,512]{3,2,1,0:T(8,128)S(1)} %bitcast.416, f32[2,12,128]{2,1,0:T(8,128)S(1)} %get-tuple-element.56, f32[2,12,128]{2,1,0:T(8,128)S(1)} %get-tuple-element.20, f32[2,12,128,512]{3,2,1,0:T(8,128)} %get-tuple-element.78), kind=kLoop, calls=%fused_computation.22 | loop fusion | flops 9431040 | bytes 12632064 | tf_op jit(solution)/shard_map/reduce_sum | solution.py:45
  310.2 51.1 %all-gather.10.cloned.1.call-done = bf16[768,3072]{1,0:T(8,128)(2,1)} async-done(((bf16[768,768]{1,0:T(8,128)(2,1)}), bf16[768,3072]{1,0:T(8,128)(2,1)}) %all-gather.10.cloned.1.call-update) | async-done | bytes 4718608 | tf_op jit(solution)/shard_map/all_gather | solution.py:150
  361.3 12.8 %fusion.152 = bf16[256,768]{1,0:T(8,128)(2,1)S(1)} fusion(f32[256,768]{1,0:T(8,128)S(1)} %get-tuple-element.82, bf16[3072,768]{1,0:T(8,128)(2,1)} %all-gather.12.cloned.1.call-done, bf16[768,3072]{1,0:T(8,128)(2,1)} %all-gather.10.cloned.1.call-done, f32[256]{0:T(256)S(1)} %add_rsqrt_fusion, f32[256]{0:T(256)S(1)} %broadcast_multiply_fusion), kind=kOutput, calls=%fused_computation.136 | convolution fusion | flops 2468020224 | bytes 10618880 | tf_op jit(solution)/shard_map/dot_general | solution.py:155
  374.1 8.8 %gather_fusion.3 = bf16[1024,768]{1,0:T(8,128)(2,1)S(1)} fusion(bf16[2,128,768]{2,1,0:T(8,128)(2,1)S(1)} %bitcast.403, s32[1024]{0:T(1024)S(1)} %reshape.740), kind=kCustom, calls=%fused_computation.3 | custom fusion | bytes 3153920 | tf_op jit(solution)/shard_map/gather | solution.py:167
  384.3 7.6 %all-to-all-start.1 = ((bf16[32,2,16,768]{3,2,1,0:T(8,128)(2,1)}), bf16[32,2,16,768]{3,2,1,0:T(8,128)(2,1)S(1)}, u32[]{:S(2)}, u32[]{:S(2)}) async-start(bf16[32,2,16,768]{3,2,1,0:T(8,128)(2,1)} %broadcast_select_fusion.1), calls=%async_computation.1 | async-start | bytes 3145728 | tf_op jit(solution)/shard_map/all_to_all | solution.py:169
  392.0 21.3 %all-to-all-done.1 = bf16[32,2,16,768]{3,2,1,0:T(8,128)(2,1)S(1)} async-done(((bf16[32,2,16,768]{3,2,1,0:T(8,128)(2,1)}), bf16[32,2,16,768]{3,2,1,0:T(8,128)(2,1)S(1)}, u32[]{:S(2)}, u32[]{:S(2)}) %all-to-all-start.1) | async-done | bytes 1572896 | tf_op jit(solution)/shard_map/all_to_all | solution.py:169
  413.3 9.8 %gather_fusion.4 = bf16[1024,768]{1,0:T(8,128)(2,1)S(1)} fusion(bf16[32,2,16,768]{3,2,1,0:T(8,128)(2,1)S(1)} %all-to-all-done.1, s32[1024]{0:T(1024)S(1)} %bitcast.406), kind=kCustom, calls=%fused_computation.4 | custom fusion | bytes 3158016 | tf_op jit(solution)/shard_map/gather | solution.py:172
  436.6 3.9 collective-permute-done.3
  458.2 3.9 collective-permute-done.7
  (229 shorter events, 145.5 us)
Async XLA Ops:
  6.5 116.3 %copy-start = (bf16[768,2304]{1,0:T(8,128)(2,1)S(1)}, bf16[768,2304]{1,0:T(8,128)(2,1)}, u32[]{:S(2)}) copy-start(bf16[768,2304]{1,0:T(8,128)(2,1)} %param.13) | copy-start | bytes 10616836
  30.9 9.7 %copy-start.2 = (s32[32,2]{1,0:T(8,128)}, s32[32,2]{1,0:T(8,128)S(1)}, u32[]{:S(2)}) copy-start(s32[32,2]{1,0:T(8,128)S(1)} %get-tuple-element.6) | copy-start | bytes 772
  85.2 12.8 %copy-start.3 = (s32[32,2]{1,0:T(8,128)S(1)}, s32[32,2]{1,0:T(8,128)}, u32[]{:S(2)}) copy-start(s32[32,2]{1,0:T(8,128)} %copy-done.2) | copy-start | bytes 772
  88.0 28.2 %all-to-all-start = ((bf16[32,2,16,768]{3,2,1,0:T(8,128)(2,1)}), bf16[32,2,16,768]{3,2,1,0:T(8,128)(2,1)}, u32[]{:S(2)}, u32[]{:S(2)}) async-start(bf16[32,2,16,768]{3,2,1,0:T(8,128)(2,1)} %broadcast_select_fusion), calls=%async_computation | async-start | bytes 3145728 | tf_op jit(solution)/shard_map/all_to_all | solution.py:110
  94.6 93.7 %all-gather.6.cloned.1.call-start = ((), (), s32[]{:S(2)}) async-start(), calls=%async_computation.2 | async-start | bytes 12976128 | tf_op jit(solution)/shard_map/all_gather | solution.py:128
  125.9 128.7 %all-gather.8.cloned.1.call-start = ((), (), s32[]{:S(2)}) async-start(), calls=%async_computation.3 | async-start | bytes 12976128 | tf_op jit(solution)/shard_map/all_gather | solution.py:129
  126.7 183.5 %all-gather.12.cloned.1.call-start = ((), (), s32[]{:S(2)}) async-start(), calls=%async_computation.5 | async-start | bytes 5898240 | tf_op jit(solution)/shard_map/all_gather | solution.py:157
  127.4 233.9 %all-gather.10.cloned.1.call-start = ((), (), s32[]{:S(2)}) async-start(), calls=%async_computation.4 | async-start | bytes 5898240 | tf_op jit(solution)/shard_map/all_gather | solution.py:150
  280.6 13.6 %slice-start.14 = ((s8[6291456]{0:T(1024)(128)(4,1)}), s8[4194304]{0:T(1024)(128)(4,1)S(1)}, s32[]{:S(2)}) async-start(s8[6291456]{0:T(1024)(128)(4,1)} %bitcast.421), calls=%async_computation.20 | async-start | bytes 8388608
  287.3 8.9 %slice-start.12 = ((s8[6291456]{0:T(1024)(128)(4,1)}), s8[4194304]{0:T(1024)(128)(4,1)S(1)}, s32[]{:S(2)}) async-start(s8[6291456]{0:T(1024)(128)(4,1)} %bitcast.419), calls=%async_computation.18 | async-start | bytes 8388608
  374.1 8.8 %copy-start.17 = (pred[32,2,16]{2,1,0:T(4,128)(4,1)S(1)}, pred[32,2,16]{2,1,0:T(4,128)(4,1)}, u32[]{:S(2)}) copy-start(pred[32,2,16]{2,1,0:T(4,128)(4,1)} %get-tuple-element.61) | copy-start | bytes 3076
  382.9 9.0 %copy-start.18 = (s32[2,4,128]{2,1,0:T(4,128)S(1)}, s32[2,4,128]{2,1,0:T(4,128)}, u32[]{:S(2)}) copy-start(s32[2,4,128]{2,1,0:T(4,128)} %get-tuple-element.57) | copy-start | bytes 12292
  382.9 9.0 %copy-start.21 = (s32[2]{0:T(128)S(1)}, s32[2]{0:T(128)}, u32[]{:S(2)}) copy-start(s32[2]{0:T(128)} %copy-done.20) | copy-start | bytes 28
  382.9 9.1 %copy-start.15 = (s32[2,16,32]{2,1,0:T(8,128)S(1)}, s32[2,16,32]{2,1,0:T(8,128)}, u32[]{:S(2)}) copy-start(s32[2,16,32]{2,1,0:T(8,128)} %param.11) | copy-start | bytes 12292
  384.3 29.1 %all-to-all-start.1 = ((bf16[32,2,16,768]{3,2,1,0:T(8,128)(2,1)}), bf16[32,2,16,768]{3,2,1,0:T(8,128)(2,1)S(1)}, u32[]{:S(2)}, u32[]{:S(2)}) async-start(bf16[32,2,16,768]{3,2,1,0:T(8,128)(2,1)} %broadcast_select_fusion.1), calls=%async_computation.1 | async-start | bytes 3145728 | tf_op jit(solution)/shard_map/all_to_all | solution.py:169
  413.3 9.9 %copy-start.25 = (bf16[768]{0:T(1024)(128)(2,1)S(1)}, bf16[768]{0:T(1024)(128)(2,1)}, u32[]{:S(2)}) copy-start(bf16[768]{0:T(1024)(128)(2,1)} %param.12) | copy-start | bytes 4612
  425.0 4.7 collective-permute-start.1
  427.0 5.2 %collective-permute-start = (bf16[2,1,32,256]{3,2,1,0:T(8,128)(2,1)S(1)}, bf16[2,1,32,256]{3,2,1,0:T(8,128)(2,1)S(1)}, u32[]{:S(2)}, u32[]{:S(2)}) collective-permute-start(bf16[2,1,32,256]{3,2,1,0:T(8,128)(2,1)S(1)} %get-tuple-element.52), channel_id=1, source_target_pairs={{0,4},{4,8},{8,12},{12,16},{16,20},{20,24},{24,28},{1,5},{5,9},{9,... | collective-permute-start | bytes 98312 | tf_op jit(solution)/shard_map/ppermute | solution.py:22
  432.3 4.3 collective-permute-start.2
  434.7 5.9 %collective-permute-start.3 = (bf16[2,18,1,256]{3,2,1,0:T(2,128)(2,1)S(1)}, bf16[2,18,1,256]{3,2,1,0:T(2,128)(2,1)S(1)}, u32[]{:S(2)}, u32[]{:S(2)}) collective-permute-start(bf16[2,18,1,256]{3,2,1,0:T(2,128)(2,1)S(1)} %get-tuple-element.49), channel_id=1, source_target_pairs={{1,0},{2,1},{3,2},{5,4},{6,5},{7,6},{9,8},{10,9},{11,10},{13,12},{... | collective-permute-start | bytes 55304 | tf_op jit(solution)/shard_map/ppermute | solution.py:24
  445.7 4.6 collective-permute-start.5
  447.6 5.2 %collective-permute-start.4 = (bf16[2,1,32,256]{3,2,1,0:T(8,128)(2,1)S(1)}, bf16[2,1,32,256]{3,2,1,0:T(8,128)(2,1)S(1)}, u32[]{:S(2)}, u32[]{:S(2)}) collective-permute-start(bf16[2,1,32,256]{3,2,1,0:T(8,128)(2,1)S(1)} %get-tuple-element.50), channel_id=1, source_target_pairs={{0,4},{4,8},{8,12},{12,16},{16,20},{20,24},{24,28},{1,5},{5,9},{9,... | collective-permute-start | bytes 98312 | tf_op jit(solution)/shard_map/ppermute | solution.py:22
  452.9 5.2 %collective-permute-start.6 = (bf16[2,18,1,256]{3,2,1,0:T(2,128)(2,1)S(1)}, bf16[2,18,1,256]{3,2,1,0:T(2,128)(2,1)S(1)}, u32[]{:S(2)}, u32[]{:S(2)}) collective-permute-start(bf16[2,18,1,256]{3,2,1,0:T(2,128)(2,1)S(1)} %get-tuple-element.44), channel_id=1, source_target_pairs={{0,1},{1,2},{2,3},{4,5},{5,6},{6,7},{8,9},{9,10},{10,11},{12,13},{... | collective-permute-start | bytes 55304 | tf_op jit(solution)/shard_map/ppermute | solution.py:22
  456.2 5.9 %collective-permute-start.7 = (bf16[2,18,1,256]{3,2,1,0:T(2,128)(2,1)S(1)}, bf16[2,18,1,256]{3,2,1,0:T(2,128)(2,1)S(1)}, u32[]{:S(2)}, u32[]{:S(2)}) collective-permute-start(bf16[2,18,1,256]{3,2,1,0:T(2,128)(2,1)S(1)} %get-tuple-element.45), channel_id=1, source_target_pairs={{1,0},{2,1},{3,2},{5,4},{6,5},{7,6},{9,8},{10,9},{11,10},{13,12},{... | collective-permute-start | bytes 55304 | tf_op jit(solution)/shard_map/ppermute | solution.py:24
  (34 other events, 124.2 us)
Sparse Core Ops, SparseCore 0:
  126.1 62.2 all-gather.5
  190.6 62.3 all-gather.7
  254.7 52.0 all-gather.11
  308.3 52.9 all-gather.9
where the time goes:
time: 483 us; the launch traced here: 475 us
  waiting for transfers between devices  162 us (34%)
  local copies, waits for them, and re-layouts  130 us (27%)
  matrix products  72.5 us (15%)
  other arithmetic  48 us (10%)
  starting transfers between devices  31.7 us (7%)
  blocking collectives  16.4 us (3%)
  between operations  15.3 us (3%)
    all_gather x1, waiting for transfers between devices, shards(): keys_piece = lax.all_gather(keys_local, ('row', 'col'), axis=1, tiled=True)  59.9 us
    all_gather x1, waiting for transfers between devices, shards(): lax.all_gather(up_weight, 'dp', axis=1, tiled=True)  51.1 us
    gather x1, local copies, waits for them, and re-layouts, shards(): flat_tokens[sample_ids, source_pos]  31.4 us
    dot_general x8, matrix products, attend(): jnp.einsum('sqhd,skhd->shqk', query, keys, preferred_element_type=jnp.flo...  30.9 us
    slice x9, local copies, waits for them, and re-layouts, shards(): values_piece[:, lower:upper].reshape(samples, upper - lower, HEADS, HD)  25.9 us
    slice x9, local copies, waits for them, and re-layouts, shards(): keys_piece[:, lower:upper].reshape(samples, upper - lower, HEADS, HD)  23.6 us
    reduce_sum x4, other arithmetic, attend(): run_sum = run_sum * shrink + jnp.sum(expo, -1)  22.7 us
    all_to_all x1, waiting for transfers between devices, shards(): lax.all_to_all(returning, ('row', 'col'), split_axis=0, concat_axis=0, ti...  21.3 us
  transfers between devices with their start and end apart: 14, of which 8 were waited for; matrix products, arithmetic and copies ran while one was open for 27% of the time, Pallas kernels for 0%

commit v1 on v0

v1 whole, which is shorter than its diff:
```python
import jax
import jax.numpy as jnp
from jax import lax
from jax.experimental import pallas as pl
from jax.experimental.pallas import tpu as pltpu
from jax.sharding import PartitionSpec as P

HEADS = 12
HD = 64
EPS = 1e-06
LOG2E = 1.4426950408889634
ROOT_HALF = 0.7071067811865476
PLANE = ("row", "col")
MIB = 1 << 20


def extended_2(cells, sides, width):
    for axis, dim in sides:
        count = lax.axis_size(axis)
        ends = count - 1
        head = lax.slice_in_dim(cells, 0, width, axis=dim)
        tail = lax.slice_in_dim(cells, cells.shape[dim] - width, cells.shape[dim], axis=dim)
        cells = jnp.concatenate(
            [
                lax.ppermute(tail, axis, [(i, (i + 1) % count) for i in range(ends)]),
                cells,
                lax.ppermute(head, axis, [((i + 1) % count, i) for i in range(ends)]),
            ],
            axis=dim,
        )
    return cells


def normalize(wide):
    mean = jnp.mean(wide, -1, keepdims=True)
    centred = wide - mean
    var = jnp.mean(centred * centred, -1, keepdims=True)
    return (centred * lax.rsqrt(var + EPS)).astype(jnp.bfloat16)


def gelu(value):
    return 0.5 * value * (1.0 + lax.erf(value * ROOT_HALF))


def dot(left, right):
    return jnp.dot(left, right, preferred_element_type=jnp.float32)


def one_hot(left, right):
    return jnp.where(left == right, 1.0, 0.0).astype(jnp.bfloat16)


def convolve(extended, taps, out_h, out_w):
    total = None
    for first in range(3):
        for second in range(3):
            term = jnp.einsum(
                "shwc,cd->shwd",
                extended[:, first : first + out_h, second : second + out_w],
                taps[first * 3 + second],
                preferred_element_type=jnp.float32,
            )
            total = term if total is None else total + term
    return total


def params(limit):
    return pltpu.CompilerParams(vmem_limit_bytes=limit * MIB)


def dispatch(my_start, cell_rank, tokens, peers):
    samples, tile, width = tokens.shape
    cap = tile // peers

    def kernel(start_ref, rank_ref, token_ref, out_ref):
        start = start_ref[pl.program_id(0)]
        slot = lax.broadcasted_iota(jnp.int32, (tile, 1), 0)
        rank = (slot % cap) * peers + ((slot // cap - start) & (peers - 1))
        chosen = one_hot(rank, rank_ref[...].reshape(1, tile))
        rows = dot(chosen, token_ref[...].reshape(tile, width)).astype(jnp.bfloat16)
        out_ref[...] = rows.reshape(peers, 1, cap, width)

    return pl.pallas_call(
        kernel,
        grid_spec=pltpu.PrefetchScalarGridSpec(
            num_scalar_prefetch=1,
            grid=(samples,),
            in_specs=[
                pl.BlockSpec((1, 1, tile), lambda s, _: (s, 0, 0)),
                pl.BlockSpec((1, tile, width), lambda s, _: (s, 0, 0)),
            ],
            out_specs=pl.BlockSpec((peers, 1, cap, width), lambda s, _: (0, s, 0, 0)),
        ),
        out_shape=jax.ShapeDtypeStruct((peers, samples, cap, width), jnp.bfloat16),
        compiler_params=params(32),
        name="dispatch",
    )(my_start, cell_rank, tokens)


def project(arrived, token_col, qkv_weight, kept):
    peers, samples, cap, width = arrived.shape
    tile = peers * cap
    lanes = 2 * HD
    groups = width // lanes
    places = peers // samples
    half = kept // 2

    def kernel(col_ref, arrived_ref, weight_ref, x_ref, out_ref):
        token = lax.broadcasted_iota(jnp.int32, (kept, 1), 0)
        chosen = one_hot(token, col_ref[...].reshape(1, tile))
        x = dot(chosen, arrived_ref[...].reshape(tile, width))
        x_ref[...] = x.astype(jnp.bfloat16).reshape(1, kept, width)
        normed = normalize(x)
        qkv = dot(normed, weight_ref[...])
        low = lax.broadcasted_iota(jnp.int32, (kept, lanes), 1) < HD
        low_half = lax.broadcasted_iota(jnp.int32, (half, lanes), 1) < HD
        for group in range(groups):
            at = group * lanes
            q = qkv[:, at : at + lanes] * (0.125 * LOG2E)
            k = qkv[:, width + at : width + at + lanes]
            v = qkv[:, 2 * width + at : 2 * width + at + lanes]
            top, bottom = v[:half], v[half:]
            first = jnp.where(low, q, pltpu.roll(k, HD, 1))
            second = jnp.where(low, pltpu.roll(q, HD, 1), k)
            first_v = jnp.where(low_half, top, pltpu.roll(bottom, HD, 1))
            second_v = jnp.where(low_half, pltpu.roll(top, HD, 1), bottom)
            out_ref[2 * group, :kept] = first.astype(jnp.bfloat16)
            out_ref[2 * group, kept:] = first_v.astype(jnp.bfloat16)
            out_ref[2 * group + 1, :kept] = second.astype(jnp.bfloat16)
            out_ref[2 * group + 1, kept:] = second_v.astype(jnp.bfloat16)
        for place in range(2 * groups, places):
            out_ref[place] = jnp.zeros((kept + half, lanes), jnp.bfloat16)

    return pl.pallas_call(
        kernel,
        grid=(samples,),
        in_specs=[
            pl.BlockSpec((1, 1, tile), lambda s: (s, 0, 0)),
            pl.BlockSpec((peers, 1, cap, width), lambda s: (0, s, 0, 0)),
            pl.BlockSpec((width, 3 * width), lambda s: (0, 0)),
        ],
        out_specs=[
            pl.BlockSpec((1, kept, width), lambda s: (s, 0, 0)),
            pl.BlockSpec((places, kept + half, lanes), lambda s: (s, 0, 0)),
        ],
        out_shape=[
            jax.ShapeDtypeStruct((samples, kept, width), jnp.bfloat16),
            jax.ShapeDtypeStruct((peers, kept + half, lanes), jnp.bfloat16),
        ],
        compiler_params=params(48),
        name="project",
    )(token_col, arrived, qkv_weight)


def attention(packed, kept):
    peers, _, lanes = packed.shape
    half = kept // 2
    keys = peers * half
    step = 2

    def kernel(packed_ref, out_ref, low_key, high_key, value):
        at = pl.program_id(0)

        @pl.when(at == 0)
        def _():
            for peer in range(peers):
                rows = pl.ds(peer * half, half)
                both = pltpu.roll(packed_ref[peer, :kept].astype(jnp.float32), HD, 1)
                both = both.astype(jnp.bfloat16)
                low_key[rows] = both[:half]
                high_key[rows] = both[half:]
                value[rows, :lanes] = packed_ref[peer, kept:]
            value[:, lanes:] = jnp.ones((keys, lanes), jnp.bfloat16)

        query = packed_ref[pl.ds(at * step, step), :kept].reshape(step * kept, lanes)
        lane = lax.broadcasted_iota(jnp.int32, query.shape, 1)
        query = jnp.where(lane < HD, query, jnp.zeros_like(query))
        contract = (((1,), (1,)), ((), ()))
        low = lax.dot_general(query, low_key[...], contract, preferred_element_type=jnp.float32)
        high = lax.dot_general(query, high_key[...], contract, preferred_element_type=jnp.float32)
        top = jnp.maximum(jnp.max(low, -1, keepdims=True), jnp.max(high, -1, keepdims=True))
        low = jnp.exp2(low - top).astype(jnp.bfloat16)
        high = jnp.exp2(high - top).astype(jnp.bfloat16)
        low = dot(low, value[...])
        high = dot(high, value[...])
        total = low[:, lanes:] + high[:, lanes:]
        mixed = (low[:, :lanes] + pltpu.roll(high[:, :lanes], HD, 1)) / total
        mixed = mixed.reshape(step, 2, half, lanes)
        lane = lax.broadcasted_iota(jnp.int32, (half, lanes), 1)
        for one in range(step):
            both = jnp.where(lane < HD, mixed[one, 0], pltpu.roll(mixed[one, 1], HD, 1))
            out_ref[one] = both.astype(jnp.bfloat16)

    return pl.pallas_call(
        kernel,
        grid=(peers // step,),
        in_specs=[pl.BlockSpec(packed.shape, lambda i: (0, 0, 0))],
        out_specs=pl.BlockSpec((step, half, lanes), lambda i: (i, 0, 0)),
        out_shape=jax.ShapeDtypeStruct((peers, half, lanes), jnp.bfloat16),
        scratch_shapes=[
            pltpu.VMEM((keys, lanes), jnp.bfloat16),
            pltpu.VMEM((keys, lanes), jnp.bfloat16),
            pltpu.VMEM((keys, 2 * lanes), jnp.bfloat16),
        ],
        compiler_params=params(48),
        name="attention",
    )(packed)


def feed_forward(mixed, x, token_col, out_weight, up, down, dec_proj, cap):
    peers, half, lanes = mixed.shape
    samples, kept, width = x.shape
    places = peers // samples
    rows = samples * kept
    blocks, _, hidden = up.shape
    narrow = dec_proj.shape[1]
    tile = peers * cap

    def kernel(mixed_ref, x_ref, col_ref, out_w, up_ref, down_ref, dec_ref, out_ref, x_one, normed, total):
        at = pl.program_id(0)

        @pl.when(at == 0)
        def _():
            low = lax.broadcasted_iota(jnp.int32, (half, lanes), 1) < HD
            for sample in range(samples):
                parts = []
                for group in range(width // lanes):
                    one = mixed_ref[sample * places + 2 * group].astype(jnp.float32)
                    two = mixed_ref[sample * places + 2 * group + 1].astype(jnp.float32)
                    top = jnp.where(low, one, pltpu.roll(two, HD, 1))
                    bottom = jnp.where(low, pltpu.roll(one, HD, 1), two)
                    parts.append(jnp.concatenate([top, bottom], 0).astype(jnp.bfloat16))
                attn = jnp.concatenate(parts, 1)
                here = pl.ds(sample * kept, kept)
                added = x_ref[sample].astype(jnp.float32) + dot(attn, out_w[...])
                added = added.astype(jnp.bfloat16)
                x_one[here] = added
                normed[here] = normalize(added.astype(jnp.float32))
            total[...] = jnp.zeros_like(total)

        inner = gelu(dot(normed[...], up_ref[0])).astype(jnp.bfloat16)
        total[...] += dot(inner, down_ref[0])

        @pl.when(at == blocks - 1)
        def _():
            encoded = (x_one[...].astype(jnp.float32) + total[...]).astype(jnp.bfloat16)
            field = dot(encoded, dec_ref[...]).astype(jnp.bfloat16)
            for sample in range(samples):
                token = lax.broadcasted_iota(jnp.int32, (1, kept), 1)
                chosen = one_hot(col_ref[sample], token)
                sent = dot(chosen, field[sample * kept : (sample + 1) * kept])
                out_ref[:, sample] = sent.astype(jnp.bfloat16).reshape(peers, cap, narrow)

    def whole(shape):
        return pl.BlockSpec(shape, lambda i: (0,) * len(shape))

    return pl.pallas_call(
        kernel,
        grid=(blocks,),
        in_specs=[
            whole(mixed.shape),
            whole(x.shape),
            whole((samples, tile, 1)),
            whole(out_weight.shape),
            pl.BlockSpec((1, width, hidden), lambda i: (i, 0, 0)),
            pl.BlockSpec((1, hidden, width), lambda i: (i, 0, 0)),
            whole(dec_proj.shape),
        ],
        out_specs=whole((peers, samples, cap, narrow)),
        out_shape=jax.ShapeDtypeStruct((peers, samples, cap, narrow), jnp.bfloat16),
        scratch_shapes=[
            pltpu.VMEM((rows, width), jnp.bfloat16),
            pltpu.VMEM((rows, width), jnp.bfloat16),
            pltpu.VMEM((rows, width), jnp.float32),
        ],
        compiler_params=params(48),
        name="feed_forward",
    )(mixed, x, token_col, out_weight, up, down, dec_proj)


def place(home, cell_slot, mask_token, dec_proj):
    peers, samples, cap, narrow = home.shape
    tile = peers * cap
    width = dec_proj.shape[0]

    def kernel(slot_ref, home_ref, token_ref, dec_ref, out_ref):
        slot = slot_ref[0]
        chosen = one_hot(slot, lax.broadcasted_iota(jnp.int32, (1, tile), 1))
        rows = dot(chosen, home_ref[...].reshape(tile, narrow))
        blank = dot(jnp.broadcast_to(token_ref[...], (8, width)), dec_ref[...])[:1]
        out_ref[0] = jnp.where(slot < 0, blank, rows).astype(jnp.bfloat16)

    return pl.pallas_call(
        kernel,
        grid=(samples,),
        in_specs=[
            pl.BlockSpec((1, tile, 1), lambda s: (s, 0, 0)),
            pl.BlockSpec((peers, 1, cap, narrow), lambda s: (0, s, 0, 0)),
            pl.BlockSpec((1, width), lambda s: (0, 0)),
            pl.BlockSpec((width, narrow), lambda s: (0, 0)),
        ],
        out_specs=pl.BlockSpec((1, tile, narrow), lambda s: (s, 0, 0)),
        out_shape=jax.ShapeDtypeStruct((samples, tile, narrow), jnp.bfloat16),
        compiler_params=params(32),
        name="place",
    )(cell_slot, home, mask_token.reshape(1, width), dec_proj)


def inside(height, width, out_h, out_w, reach):
    row = lax.axis_index("row") * height - reach + jnp.arange(out_h, dtype=jnp.int32)
    col = lax.axis_index("col") * width - reach + jnp.arange(out_w, dtype=jnp.int32)
    row_in = (row >= 0) & (row < lax.axis_size("row") * height)
    col_in = (col >= 0) & (col < lax.axis_size("col") * width)
    return row_in[:, None] & col_in[None, :]


def shards(
    patches,
    keep_mask,
    mask_token,
    qkv_weight,
    out_weight,
    up_weight,
    down_weight,
    dec_proj,
    conv_weight,
    head_weight,
):
    peers = lax.axis_size(PLANE)
    me = lax.axis_index(PLANE)
    samples, tile_h, tile_w, width = patches.shape
    tile = tile_h * tile_w
    cap = tile // peers
    kept = tile // 4
    up = lax.all_gather(up_weight, "dp", axis=0)
    down = lax.all_gather(down_weight, "dp", axis=0)

    flat_mask = keep_mask.reshape(samples, tile)
    counts = jnp.sum(flat_mask, 1)
    told = lax.all_to_all(
        jnp.broadcast_to(counts[None, None, :], (peers, 1, samples)),
        PLANE,
        split_axis=0,
        concat_axis=0,
        tiled=True,
    ).reshape(peers, samples)
    before = jnp.arange(tile)[:, None] < jnp.arange(tile)[None, :]
    running = dot(flat_mask.astype(jnp.bfloat16), before.astype(jnp.bfloat16)).astype(jnp.int32)
    cell_rank = jnp.where(flat_mask == 1, running, -1)

    ids = jnp.arange(peers, dtype=jnp.int32)
    earlier = ids[:, None] < ids[None, :]
    starts = jnp.sum(jnp.where(earlier[:, :, None], told[:, None, :], 0), 0)
    my_start = jnp.sum(jnp.where((ids < me)[:, None], told, 0), 0)

    outgoing = dispatch(
        my_start, cell_rank.reshape(samples, 1, tile), patches.reshape(samples, tile, width), peers
    )
    arrived = lax.all_to_all(outgoing, PLANE, split_axis=0, concat_axis=0, tiled=True)

    slot = jnp.arange(cap, dtype=jnp.int32)[None, None, :]
    local = slot * peers + ((me - starts.T[:, :, None]) & (peers - 1))
    token = (starts.T[:, :, None] + local - me) // peers
    token = jnp.where(local < told.T[:, :, None], token, -1)

    x, packed = project(arrived, token.reshape(samples, 1, tile), qkv_weight, kept)
    packed = lax.all_to_all(packed, PLANE, split_axis=0, concat_axis=0, tiled=True)
    mixed = attention(packed, kept)
    mixed = lax.all_to_all(mixed, PLANE, split_axis=0, concat_axis=0, tiled=True)
    returning = feed_forward(
        mixed, x, token.reshape(samples, tile, 1), out_weight, up, down, dec_proj, cap
    )
    home = lax.all_to_all(returning, PLANE, split_axis=0, concat_axis=0, tiled=True)

    cell_slot = ((my_start[:, None] + running) & (peers - 1)) * cap + running // peers
    cell_slot = jnp.where(flat_mask == 1, cell_slot, -1)
    h_zero = place(home, cell_slot.reshape(samples, tile, 1), mask_token, dec_proj)
    h_zero = h_zero.reshape(samples, tile_h, tile_w, h_zero.shape[-1])
    h_zero = extended_2(h_zero, (("row", 1), ("col", 2)), 2)
    conv_one = convolve(h_zero, conv_weight[0], tile_h + 2, tile_w + 2)
    h_one = h_zero[:, 1:-1, 1:-1].astype(jnp.float32) + gelu(conv_one)
    within = inside(tile_h, tile_w, tile_h + 2, tile_w + 2, 1)
    h_one = jnp.where(within[None, :, :, None], h_one, 0.0).astype(jnp.bfloat16)
    conv_two = convolve(h_one, conv_weight[1], tile_h, tile_w)
    h_two = (h_one[:, 1:-1, 1:-1].astype(jnp.float32) + gelu(conv_two)).astype(jnp.bfloat16)
    return dot(h_two, head_weight).astype(jnp.bfloat16)


def solution(mesh):
    return jax.shard_map(
        shards,
        mesh=mesh,
        in_specs=(
            P("dp", "row", "col", None),
            P("dp", "row", "col"),
            P(),
            P(),
            P(),
            P(None, "dp"),
            P("dp", None),
            P(),
            P(),
            P(),
        ),
        out_specs=P("dp", "row", "col", None),
        check_vma=False,
    )
```

time: 483 us -> 192 us (0.40); the launches traced: 475 us -> 190 us
  local copies, waits for them, and re-layouts: 130 us -> 5.03 us
  waiting for transfers between devices: 162 us -> 50.1 us
  matrix products: 72.5 us -> 9.38 us
  Pallas kernels: 0 us -> 49.4 us
  other arithmetic: 48 us -> 2.84 us
  blocking collectives: 16.4 us -> 26.7 us
    all_gather x4 -> x2, waiting for transfers between devices: 111 us -> 0.01 us  [the longest x1 0.01 us: shards(): up = lax.all_gather(up_weight, 'dp', axis=0)]
    gather x7 -> x0, local copies, waits for them, and re-layouts: 66.7 us -> none  [the longest x1 31.4 us: shards(): flat_tokens[sample_ids, source_pos]]
    dot_general x21 -> x2, matrix products: 66.3 us -> 2.49 us  [dot(): return jnp.dot(left, right, preferred_element_type=jnp.float32)]
    slice x21 -> x0, local copies, waits for them, and re-layouts: 52.1 us -> none  [the longest x9 25.9 us: shards(): values_piece[:, lower:upper].reshape(samples, upper - lower, HEADS, HD)]
    pallas_call x0 -> x5, Pallas kernels: none -> 49.4 us  [the longest x1 32.8 us: attention(): pl.pallas_call(kernel, grid=(peers // step,), in_specs=[pl.BlockSpec(pack...]
    all_to_all x0 -> x1, blocking collectives: none -> 26.7 us  [shards(): lax.all_to_all(packed, PLANE, split_axis=0, concat_axis=0, tiled=True)]
    reduce_sum x9 -> x2, other arithmetic: 26.3 us -> 0.21 us  [the longest x1 0.12 us: shards(): my_start = jnp.sum(jnp.where((ids < me)[:, None], told, 0), 0)]
    unnamed x1 -> x0, blocking collectives: 16.4 us -> none
  transfers between devices with their start and end apart: 14 -> 10, of which waited for: 8 -> 7; matrix products, arithmetic and copies ran while one was open for 27% -> 4% of each run, Pallas kernels for 0% -> 21%
where the time goes in v1:
time: 192 us; the launch traced here: 190 us
  waiting for transfers between devices  50.1 us (26%)
  Pallas kernels  49.4 us (26%)
  starting transfers between devices  32.9 us (17%)
  blocking collectives  26.7 us (14%)
  between operations  13.8 us (7%)
  matrix products  9.38 us (5%)
  local copies, waits for them, and re-layouts  5.03 us (3%)
  other arithmetic  2.84 us (1%)
    pallas_call x1, Pallas kernels, attention(): pl.pallas_call(kernel, grid=(peers // step,), in_specs=[pl.BlockSpec(pack...  32.8 us
    all_to_all x1, blocking collectives, shards(): lax.all_to_all(packed, PLANE, split_axis=0, concat_axis=0, tiled=True)  26.7 us
    all_to_all x1, waiting for transfers between devices, shards(): lax.all_to_all(outgoing, PLANE, split_axis=0, concat_axis=0, tiled=True)  20.8 us
    all_to_all x1, waiting for transfers between devices, shards(): lax.all_to_all(returning, PLANE, split_axis=0, concat_axis=0, tiled=True)  10.2 us
    all_to_all x1, starting transfers between devices, shards(): lax.all_to_all(jnp.broadcast_to(counts[None, None, :], (peers, 1, samples...  8.46 us
    pallas_call x1, Pallas kernels, feed_forward(): pl.pallas_call(kernel, grid=(blocks,), in_specs=[whole(mixed.shape), whol...  8.46 us
    dot_general x17, matrix products, convolve(): jnp.einsum('shwc,cd->shwd', extended[:, first:first + out_h, second:secon...  6.89 us
    ppermute x2, waiting for transfers between devices, extended_2(): lax.ppermute(head, axis, [((i + 1) % count, i) for i in range(ends)])  6 us
  transfers between devices with their start and end apart: 10, of which 7 were waited for; matrix products, arithmetic and copies ran while one was open for 4% of the time, Pallas kernels for 21%

profile of v1, /device:TPU:2, one launch (start us, length us, event | category | flops | bytes accessed | tf_op | source)
XLA Modules:
  0.0 190.2 jit_solution(16831601845942070419)
XLA Ops:
  8.8 8.5 %all-to-all-start = ((s32[32,1,2]{2,1,0:T(1,128)}), s32[32,1,2]{2,1,0:T(1,128)S(1)}, u32[]{:S(2)}, u32[]{:S(2)}) async-start(s32[32,1,2]{2,1,0:T(1,128)} %broadcast_in_dim.71), calls=%async_computation | async-start | bytes 32768 | tf_op jit(solution)/shard_map/all_to_all | solution.py:340
  17.5 5.9 %all-to-all-done = s32[32,1,2]{2,1,0:T(1,128)S(1)} async-done(((s32[32,1,2]{2,1,0:T(1,128)}), s32[32,1,2]{2,1,0:T(1,128)S(1)}, u32[]{:S(2)}, u32[]{:S(2)}) %all-to-all-start) | async-done | bytes 288 | tf_op jit(solution)/shard_map/all_to_all | solution.py:340
  23.8 2.7 %dispatch.1 = bf16[32,2,16,768]{3,2,1,0:T(8,128)(2,1)} custom-call(s32[2]{0:T(128)S(1)} %select_reduce_fusion.1.start_ref, s32[2,1,512]{2,1,0:T(1,128)S(1)} %reshape.355.rank_ref, bf16[2,512,768]{2,1,0:T(8,128)(2,1)S(1)} %bitcast.160), custom_call_target="tpu_custom_call" | custom-call | tf_op jit(solution)/shard_map/dispatch/pallas_call | solution.py:83
  26.4 5.1 %all-to-all-start.1 = ((bf16[32,2,16,768]{3,2,1,0:T(8,128)(2,1)}), bf16[32,2,16,768]{3,2,1,0:T(8,128)(2,1)S(1)}, u32[]{:S(2)}, u32[]{:S(2)}) async-start(bf16[32,2,16,768]{3,2,1,0:T(8,128)(2,1)} %dispatch.1), calls=%async_computation.1 | async-start | bytes 3145728 | tf_op jit(solution)/shard_map/all_to_all | solution.py:359
  32.3 20.8 %all-to-all-done.1.arrived_ref = bf16[32,2,16,768]{3,2,1,0:T(8,128)(2,1)S(1)} async-done(((bf16[32,2,16,768]{3,2,1,0:T(8,128)(2,1)}), bf16[32,2,16,768]{3,2,1,0:T(8,128)(2,1)S(1)}, u32[]{:S(2)}, u32[]{:S(2)}) %all-to-all-start.1) | async-done | bytes 1572896 | tf_op jit(solution)/shard_map/all_to_all | solution.py:359
  53.1 4.5 %project.1 = (bf16[2,128,768]{2,1,0:T(8,128)(2,1)S(1)}, bf16[32,192,128]{2,1,0:T(8,128)(2,1)S(1)}) custom-call(s32[2,1,512]{2,1,0:T(1,128)S(1)} %compare_select_fusion.col_ref, bf16[32,2,16,768]{3,2,1,0:T(8,128)(2,1)S(1)} %all-to-all-done.1.arrived_ref, bf16[768,2304]{1,0:T(8,128)(2,1)} %weight_ref.1), custom_call_target="tpu_custom_call" | custom-call | tf_op jit(solution)/shard_map/project/pallas_call | solution.py:134
  57.6 26.7 %all_to_all.25.packed_ref = bf16[32,192,128]{2,1,0:T(8,128)(2,1)S(1)} all-to-all(bf16[32,192,128]{2,1,0:T(8,128)(2,1)S(1)} %get-tuple-element.7), channel_id=1, replica_groups=mesh['dp'=4,'row'=8,'col'=4] {'row','col'}, dimensions={0} | all-to-all | bytes 3145728 | tf_op jit(solution)/shard_map/all_to_all | solution.py:367
  84.3 32.8 %attention.1 = bf16[32,64,128]{2,1,0:T(8,128)(2,1)} custom-call(bf16[32,192,128]{2,1,0:T(8,128)(2,1)S(1)} %all_to_all.25.packed_ref), custom_call_target="tpu_custom_call" | custom-call | tf_op jit(solution)/shard_map/attention/pallas_call | solution.py:194
  117.1 5.2 %all-to-all-start.3 = ((bf16[32,64,128]{2,1,0:T(8,128)(2,1)}), bf16[32,64,128]{2,1,0:T(8,128)(2,1)S(1)}, u32[]{:S(2)}, u32[]{:S(2)}) async-start(bf16[32,64,128]{2,1,0:T(8,128)(2,1)} %attention.1), calls=%async_computation.3 | async-start | bytes 1048576 | tf_op jit(solution)/shard_map/all_to_all | solution.py:369
  122.3 1.1 lt.102
  123.4 1.1 add.236
  125.6 1.8 fusion.9.col_ref
  127.4 5.4 %all-to-all-done.3.mixed_ref = bf16[32,64,128]{2,1,0:T(8,128)(2,1)S(1)} async-done(((bf16[32,64,128]{2,1,0:T(8,128)(2,1)}), bf16[32,64,128]{2,1,0:T(8,128)(2,1)S(1)}, u32[]{:S(2)}, u32[]{:S(2)}) %all-to-all-start.3) | async-done | bytes 524320 | tf_op jit(solution)/shard_map/all_to_all | solution.py:369
  132.8 8.5 %feed_forward.1 = bf16[32,2,16,256]{3,2,1,0:T(8,128)(2,1)} custom-call(bf16[32,64,128]{2,1,0:T(8,128)(2,1)S(1)} %all-to-all-done.3.mixed_ref, bf16[2,128,768]{2,1,0:T(8,128)(2,1)S(1)} %get-tuple-element.8.x_ref, s32[2,512,1]{2,1,0:T(8,128)S(1)} %fusion.9.col_ref, bf16[768,768]{1,0:T(8,128)(2,1)S(1)} %copy-done.3, bf16[4,768,768]{2,1,0:T(8,128)(2,1)} %bitcast.161, ...), custom_call_target="tpu_custom_call" | custom-call | tf_op jit(solution)/shard_map/feed_forward/pallas_call | solution.py:257
  141.2 5.2 %all-to-all-start.4 = ((bf16[32,2,16,256]{3,2,1,0:T(8,128)(2,1)}), bf16[32,2,16,256]{3,2,1,0:T(8,128)(2,1)S(1)}, u32[]{:S(2)}, u32[]{:S(2)}) async-start(bf16[32,2,16,256]{3,2,1,0:T(8,128)(2,1)} %feed_forward.1), calls=%async_computation.4 | async-start | bytes 1048576 | tf_op jit(solution)/shard_map/all_to_all | solution.py:373
  146.7 10.2 %all-to-all-done.4.home_ref = bf16[32,2,16,256]{3,2,1,0:T(8,128)(2,1)S(1)} async-done(((bf16[32,2,16,256]{3,2,1,0:T(8,128)(2,1)}), bf16[32,2,16,256]{3,2,1,0:T(8,128)(2,1)S(1)}, u32[]{:S(2)}, u32[]{:S(2)}) %all-to-all-start.4) | async-done | bytes 524320 | tf_op jit(solution)/shard_map/all_to_all | solution.py:373
  157.9 2.1 %collective-permute-start = (bf16[2,2,32,256]{3,2,1,0:T(8,128)(2,1)S(1)}, bf16[2,2,32,256]{3,2,1,0:T(8,128)(2,1)S(1)}, u32[]{:S(2)}, u32[]{:S(2)}) collective-permute-start(bf16[2,2,32,256]{3,2,1,0:T(8,128)(2,1)S(1)} %get-tuple-element.11), channel_id=1, source_target_pairs={{0,4},{4,8},{8,12},{12,16},{16,20},{20,24},{24,28},{1,5},{5,9},{9,... | collective-permute-start | bytes 196616 | tf_op jit(solution)/shard_map/ppermute | solution.py:25
  160.1 3.6 %collective-permute-start.1 = (bf16[2,2,32,256]{3,2,1,0:T(8,128)(2,1)S(1)}, bf16[2,2,32,256]{3,2,1,0:T(8,128)(2,1)S(1)}, u32[]{:S(2)}, u32[]{:S(2)}) collective-permute-start(bf16[2,2,32,256]{3,2,1,0:T(8,128)(2,1)S(1)} %get-tuple-element.12), channel_id=1, source_target_pairs={{4,0},{8,4},{12,8},{16,12},{20,16},{24,20},{28,24},{5,1},{9,5},{13... | collective-permute-start | bytes 196616 | tf_op jit(solution)/shard_map/ppermute | solution.py:27
  163.7 1.9 collective-permute-done.1
  165.6 1.9 collective-permute-start.2
  167.5 1.5 collective-permute-start.3
  169.4 4.1 %collective-permute-done.3 = bf16[2,20,2,256]{3,2,1,0:T(2,128)(2,1)S(1)} collective-permute-done((bf16[2,20,2,256]{3,2,1,0:T(2,128)(2,1)S(1)}, bf16[2,20,2,256]{3,2,1,0:T(2,128)(2,1)S(1)}, u32[]{:S(2)}, u32[]{:S(2)}) %collective-permute-start.3) | collective-permute-done | bytes 40992 | tf_op jit(solution)/shard_map/ppermute | solution.py:27
  177.1 1.4 select_convert_fusion
  181.0 2.3 %convolution_convert_fusion = bf16[2,16,32,128]{3,2,1,0:T(8,128)(2,1)} fusion(f32[2,16,32,256]{3,2,1,0:T(8,128)S(1)} %convolution_add_fusion.1, bf16[2,18,34,256]{3,2,1,0:T(8,128)(2,1)S(1)} %select_convert_fusion, bf16[2,9,256,256]{3,2,1,0:T(8,128)(2,1)} %param.18, bf16[256,128]{1,0:T(8,128)(2,1)S(1)} %copy-done), kind=kOutput, calls=%fused_computation.9 | convolution fusion | flops 203554816 | bytes 2555904 | tf_op jit(solution)/shard_map/dot_general | solution.py:46
  (71 shorter events, 12.4 us)
Async XLA Ops:
  6.5 174.5 %copy-start = (bf16[256,128]{1,0:T(8,128)(2,1)S(1)}, bf16[256,128]{1,0:T(8,128)(2,1)}, u32[]{:S(2)}) copy-start(bf16[256,128]{1,0:T(8,128)(2,1)} %param.19) | copy-start | bytes 196612
  6.5 1.5 copy-start.5
  6.5 17.2 %copy-start.2 = (bf16[2,16,32,768]{3,2,1,0:T(8,128)(2,1)S(1)}, bf16[2,16,32,768]{3,2,1,0:T(8,128)(2,1)}, u32[]{:S(2)}) copy-start(bf16[2,16,32,768]{3,2,1,0:T(8,128)(2,1)} %param.10) | copy-start | bytes 4718596
  6.5 126.2 %all-gather.5.cloned.1.call-start = ((), (), s32[]{:S(2)}) async-start(), calls=%async_computation.5 | async-start | bytes 5898240 | tf_op jit(solution)/shard_map/all_gather | solution.py:335
  7.3 125.5 %all-gather.7.cloned.1.call-start = ((), (), s32[]{:S(2)}) async-start(), calls=%async_computation.6 | async-start | bytes 5898240 | tf_op jit(solution)/shard_map/all_gather | solution.py:336
  8.8 14.6 %all-to-all-start = ((s32[32,1,2]{2,1,0:T(1,128)}), s32[32,1,2]{2,1,0:T(1,128)S(1)}, u32[]{:S(2)}, u32[]{:S(2)}) async-start(s32[32,1,2]{2,1,0:T(1,128)} %broadcast_in_dim.71), calls=%async_computation | async-start | bytes 32768 | tf_op jit(solution)/shard_map/all_to_all | solution.py:340
  26.4 26.6 %all-to-all-start.1 = ((bf16[32,2,16,768]{3,2,1,0:T(8,128)(2,1)}), bf16[32,2,16,768]{3,2,1,0:T(8,128)(2,1)S(1)}, u32[]{:S(2)}, u32[]{:S(2)}) async-start(bf16[32,2,16,768]{3,2,1,0:T(8,128)(2,1)} %dispatch.1), calls=%async_computation.1 | async-start | bytes 3145728 | tf_op jit(solution)/shard_map/all_to_all | solution.py:359
  117.1 15.7 %all-to-all-start.3 = ((bf16[32,64,128]{2,1,0:T(8,128)(2,1)}), bf16[32,64,128]{2,1,0:T(8,128)(2,1)S(1)}, u32[]{:S(2)}, u32[]{:S(2)}) async-start(bf16[32,64,128]{2,1,0:T(8,128)(2,1)} %attention.1), calls=%async_computation.3 | async-start | bytes 1048576 | tf_op jit(solution)/shard_map/all_to_all | solution.py:369
  123.4 9.4 %copy-start.1 = (bf16[768,256]{1,0:T(8,128)(2,1)S(1)}, bf16[768,256]{1,0:T(8,128)(2,1)}, u32[]{:S(2)}) copy-start(bf16[768,256]{1,0:T(8,128)(2,1)} %dec_ref.3) | copy-start | bytes 1179652
  123.4 9.4 %copy-start.3 = (bf16[768,768]{1,0:T(8,128)(2,1)S(1)}, bf16[768,768]{1,0:T(8,128)(2,1)}, u32[]{:S(2)}) copy-start(bf16[768,768]{1,0:T(8,128)(2,1)} %out_w.1) | copy-start | bytes 3538948
  132.8 13.7 %copy-start.6 = (bf16[768]{0:T(1024)(128)(2,1)S(1)}, bf16[768]{0:T(1024)(128)(2,1)}, u32[]{:S(2)}) copy-start(bf16[768]{0:T(1024)(128)(2,1)} %param.12) | copy-start | bytes 4612
  141.2 15.7 %all-to-all-start.4 = ((bf16[32,2,16,256]{3,2,1,0:T(8,128)(2,1)}), bf16[32,2,16,256]{3,2,1,0:T(8,128)(2,1)S(1)}, u32[]{:S(2)}, u32[]{:S(2)}) async-start(bf16[32,2,16,256]{3,2,1,0:T(8,128)(2,1)} %feed_forward.1), calls=%async_computation.4 | async-start | bytes 1048576 | tf_op jit(solution)/shard_map/all_to_all | solution.py:373
  157.9 16.1 %copy-start.4 = (bf16[2,9,256,256]{3,2,1,0:T(8,128)(2,1)S(1)}, bf16[2,9,256,256]{3,2,1,0:T(8,128)(2,1)}, u32[]{:S(2)}) copy-start(bf16[2,9,256,256]{3,2,1,0:T(8,128)(2,1)} %param.18) | copy-start | bytes 7077892
  157.9 5.7 %collective-permute-start = (bf16[2,2,32,256]{3,2,1,0:T(8,128)(2,1)S(1)}, bf16[2,2,32,256]{3,2,1,0:T(8,128)(2,1)S(1)}, u32[]{:S(2)}, u32[]{:S(2)}) collective-permute-start(bf16[2,2,32,256]{3,2,1,0:T(8,128)(2,1)S(1)} %get-tuple-element.11), channel_id=1, source_target_pairs={{0,4},{4,8},{8,12},{12,16},{16,20},{20,24},{24,28},{1,5},{5,9},{9,... | collective-permute-start | bytes 196616 | tf_op jit(solution)/shard_map/ppermute | solution.py:25
  160.1 5.4 %collective-permute-start.1 = (bf16[2,2,32,256]{3,2,1,0:T(8,128)(2,1)S(1)}, bf16[2,2,32,256]{3,2,1,0:T(8,128)(2,1)S(1)}, u32[]{:S(2)}, u32[]{:S(2)}) collective-permute-start(bf16[2,2,32,256]{3,2,1,0:T(8,128)(2,1)S(1)} %get-tuple-element.12), channel_id=1, source_target_pairs={{4,0},{8,4},{12,8},{16,12},{20,16},{24,20},{28,24},{5,1},{9,5},{13... | collective-permute-start | bytes 196616 | tf_op jit(solution)/shard_map/ppermute | solution.py:27
  165.6 3.8 %collective-permute-start.2 = (bf16[2,20,2,256]{3,2,1,0:T(2,128)(2,1)S(1)}, bf16[2,20,2,256]{3,2,1,0:T(2,128)(2,1)S(1)}, u32[]{:S(2)}, u32[]{:S(2)}) collective-permute-start(bf16[2,20,2,256]{3,2,1,0:T(2,128)(2,1)S(1)} %get-tuple-element.9), channel_id=1, source_target_pairs={{0,1},{1,2},{2,3},{4,5},{5,6},{6,7},{8,9},{9,10},{10,11},{12,13},{... | collective-permute-start | bytes 122888 | tf_op jit(solution)/shard_map/ppermute | solution.py:25
  167.5 6.1 %collective-permute-start.3 = (bf16[2,20,2,256]{3,2,1,0:T(2,128)(2,1)S(1)}, bf16[2,20,2,256]{3,2,1,0:T(2,128)(2,1)S(1)}, u32[]{:S(2)}, u32[]{:S(2)}) collective-permute-start(bf16[2,20,2,256]{3,2,1,0:T(2,128)(2,1)S(1)} %get-tuple-element.10), channel_id=1, source_target_pairs={{1,0},{2,1},{3,2},{5,4},{6,5},{7,6},{9,8},{10,9},{11,10},{13,12},{... | collective-permute-start | bytes 122888 | tf_op jit(solution)/shard_map/ppermute | solution.py:27
Sparse Core Ops, SparseCore 0:
  9.0 54.9 all-gather.4
  65.6 52.9 all-gather.6

commit v2 on v1

--- a/solution.py
+++ b/solution.py
@@ -5,13 +5,15 @@
 from jax.experimental.pallas import tpu as pltpu
 from jax.sharding import PartitionSpec as P
 
-HEADS = 12
+
 HD = 64
 EPS = 1e-06
 LOG2E = 1.4426950408889634
 ROOT_HALF = 0.7071067811865476
 PLANE = ("row", "col")
 MIB = 1 << 20
+ATTENTION_MIB = 40
+SAFE = 96.0
 
 
 def extended_2(cells, sides, width):
@@ -156,40 +158,68 @@
     peers, _, lanes = packed.shape
     half = kept // 2
     keys = peers * half
-    step = 2
-
-    def kernel(packed_ref, out_ref, low_key, high_key, value):
+    step = 8
+    contract = (((1,), (1,)), ((), ()))
+
+    def kernel(packed_ref, out_ref, low_key, high_key, value, bound):
         at = pl.program_id(0)
 
         @pl.when(at == 0)
         def _():
+            lane = lax.broadcasted_iota(jnp.int32, (kept, lanes), 1)
+            most_q = jnp.zeros((kept, 1), jnp.float32)
+            most_k = jnp.zeros((kept, 1), jnp.float32)
             for peer in range(peers):
                 rows = pl.ds(peer * half, half)
-                both = pltpu.roll(packed_ref[peer, :kept].astype(jnp.float32), HD, 1)
-                both = both.astype(jnp.bfloat16)
+                wide = packed_ref[peer, :kept].astype(jnp.float32)
+                both = pltpu.roll(wide, HD, 1).astype(jnp.bfloat16)
                 low_key[rows] = both[:half]
                 high_key[rows] = both[half:]
                 value[rows, :lanes] = packed_ref[peer, kept:]
+                square = wide * wide
+                size_q = jnp.sum(jnp.where(lane < HD, square, 0.0), -1, keepdims=True)
+                size_k = jnp.sum(jnp.where(lane < HD, 0.0, square), -1, keepdims=True)
+                most_q = jnp.maximum(most_q, size_q)
+                most_k = jnp.maximum(most_k, size_k)
             value[:, lanes:] = jnp.ones((keys, lanes), jnp.bfloat16)
-
-        query = packed_ref[pl.ds(at * step, step), :kept].reshape(step * kept, lanes)
-        lane = lax.broadcasted_iota(jnp.int32, query.shape, 1)
-        query = jnp.where(lane < HD, query, jnp.zeros_like(query))
-        contract = (((1,), (1,)), ((), ()))
-        low = lax.dot_general(query, low_key[...], contract, preferred_element_type=jnp.float32)
-        high = lax.dot_general(query, high_key[...], contract, preferred_element_type=jnp.float32)
-        top = jnp.maximum(jnp.max(low, -1, keepdims=True), jnp.max(high, -1, keepdims=True))
-        low = jnp.exp2(low - top).astype(jnp.bfloat16)
-        high = jnp.exp2(high - top).astype(jnp.bfloat16)
-        low = dot(low, value[...])
-        high = dot(high, value[...])
-        total = low[:, lanes:] + high[:, lanes:]
-        mixed = (low[:, :lanes] + pltpu.roll(high[:, :lanes], HD, 1)) / total
-        mixed = mixed.reshape(step, 2, half, lanes)
-        lane = lax.broadcasted_iota(jnp.int32, (half, lanes), 1)
-        for one in range(step):
-            both = jnp.where(lane < HD, mixed[one, 0], pltpu.roll(mixed[one, 1], HD, 1))
-            out_ref[one] = both.astype(jnp.bfloat16)
+            bound[0] = jnp.max(most_q) * jnp.max(most_k)
+
+        def finish(low, high, first, count):
+            total = low[:, lanes:] + high[:, lanes:]
+            mixed = (low[:, :lanes] + pltpu.roll(high[:, :lanes], HD, 1)) / total
+            mixed = mixed.reshape(count, 2, half, lanes)
+            lane = lax.broadcasted_iota(jnp.int32, (half, lanes), 1)
+            for one in range(count):
+                both = jnp.where(lane < HD, mixed[one, 0], pltpu.roll(mixed[one, 1], HD, 1))
+                out_ref[first + one] = both.astype(jnp.bfloat16)
+
+        def queries(first, count):
+            query = packed_ref[pl.ds(at * step + first, count), :kept].reshape(count * kept, lanes)
+            lane = lax.broadcasted_iota(jnp.int32, query.shape, 1)
+            return jnp.where(lane < HD, query, jnp.zeros_like(query))
+
+        def score(query, key):
+            return lax.dot_general(query, key[...], contract, preferred_element_type=jnp.float32)
+
+        narrow = bound[0] < SAFE * SAFE
+
+        @pl.when(narrow)
+        def _():
+            query = queries(0, step)
+            low = jnp.exp2(score(query, low_key)).astype(jnp.bfloat16)
+            high = jnp.exp2(score(query, high_key)).astype(jnp.bfloat16)
+            finish(dot(low, value[...]), dot(high, value[...]), 0, step)
+
+        @pl.when(jnp.logical_not(narrow))
+        def _():
+            @pl.loop(0, step)
+            def _(one):
+                query = queries(one, 1)
+                low, high = score(query, low_key), score(query, high_key)
+                top = jnp.maximum(jnp.max(low, -1, keepdims=True), jnp.max(high, -1, keepdims=True))
+                low = jnp.exp2(low - top).astype(jnp.bfloat16)
+                high = jnp.exp2(high - top).astype(jnp.bfloat16)
+                finish(dot(low, value[...]), dot(high, value[...]), one, 1)
 
     return pl.pallas_call(
         kernel,
@@ -201,81 +231,80 @@
             pltpu.VMEM((keys, lanes), jnp.bfloat16),
             pltpu.VMEM((keys, lanes), jnp.bfloat16),
             pltpu.VMEM((keys, 2 * lanes), jnp.bfloat16),
+            pltpu.SMEM((1,), jnp.float32),
         ],
-        compiler_params=params(48),
+        compiler_params=params(ATTENTION_MIB),
         name="attention",
     )(packed)
 
 
-def feed_forward(mixed, x, token_col, out_weight, up, down, dec_proj, cap):
+def feed_forward(mixed, x, token_col, out_weight, up, down, dec_proj, pieces, cap):
     peers, half, lanes = mixed.shape
     samples, kept, width = x.shape
     places = peers // samples
-    rows = samples * kept
-    blocks, _, hidden = up.shape
     narrow = dec_proj.shape[1]
-    tile = peers * cap
-
-    def kernel(mixed_ref, x_ref, col_ref, out_w, up_ref, down_ref, dec_ref, out_ref, x_one, normed, total):
-        at = pl.program_id(0)
-
-        @pl.when(at == 0)
-        def _():
-            low = lax.broadcasted_iota(jnp.int32, (half, lanes), 1) < HD
-            for sample in range(samples):
-                parts = []
-                for group in range(width // lanes):
-                    one = mixed_ref[sample * places + 2 * group].astype(jnp.float32)
-                    two = mixed_ref[sample * places + 2 * group + 1].astype(jnp.float32)
-                    top = jnp.where(low, one, pltpu.roll(two, HD, 1))
-                    bottom = jnp.where(low, pltpu.roll(one, HD, 1), two)
-                    parts.append(jnp.concatenate([top, bottom], 0).astype(jnp.bfloat16))
-                attn = jnp.concatenate(parts, 1)
-                here = pl.ds(sample * kept, kept)
-                added = x_ref[sample].astype(jnp.float32) + dot(attn, out_w[...])
-                added = added.astype(jnp.bfloat16)
-                x_one[here] = added
-                normed[here] = normalize(added.astype(jnp.float32))
-            total[...] = jnp.zeros_like(total)
-
-        inner = gelu(dot(normed[...], up_ref[0])).astype(jnp.bfloat16)
-        total[...] += dot(inner, down_ref[0])
-
-        @pl.when(at == blocks - 1)
-        def _():
-            encoded = (x_one[...].astype(jnp.float32) + total[...]).astype(jnp.bfloat16)
-            field = dot(encoded, dec_ref[...]).astype(jnp.bfloat16)
-            for sample in range(samples):
-                token = lax.broadcasted_iota(jnp.int32, (1, kept), 1)
-                chosen = one_hot(col_ref[sample], token)
-                sent = dot(chosen, field[sample * kept : (sample + 1) * kept])
-                out_ref[:, sample] = sent.astype(jnp.bfloat16).reshape(peers, cap, narrow)
-
-    def whole(shape):
-        return pl.BlockSpec(shape, lambda i: (0,) * len(shape))
-
+
+    def kernel(mixed_ref, x_ref, col_ref, out_w, up_ref, down_ref, dec_ref, *rest):
+        *piece_refs, out_ref = rest
+        low = lax.broadcasted_iota(jnp.int32, (half, lanes), 1) < HD
+        attn = []
+        for sample in range(samples):
+            parts = []
+            for group in range(width // lanes):
+                one = mixed_ref[sample * places + 2 * group].astype(jnp.float32)
+                two = mixed_ref[sample * places + 2 * group + 1].astype(jnp.float32)
+                top = jnp.where(low, one, pltpu.roll(two, HD, 1))
+                bottom = jnp.where(low, pltpu.roll(one, HD, 1), two)
+                parts.append(jnp.concatenate([top, bottom], 0).astype(jnp.bfloat16))
+            attn.append(jnp.concatenate(parts, 1))
+        attn = jnp.concatenate(attn, 0)
+        rows = x_ref[...].reshape(samples * kept, width)
+        x_one = (rows.astype(jnp.float32) + dot(attn, out_w[...])).astype(jnp.bfloat16)
+        normed = normalize(x_one.astype(jnp.float32))
+        total = dot(gelu(dot(normed, up_ref[...])).astype(jnp.bfloat16), down_ref[...])
+        for piece in piece_refs:
+            part = piece.shape[1]
+            inner = gelu(dot(normed, piece[:width])).astype(jnp.bfloat16)
+            added = [dot(inner, piece[pl.ds(at, part)]) for at in range(width, piece.shape[0], part)]
+            total = total + jnp.concatenate(added, 1)
+        encoded = (x_one.astype(jnp.float32) + total).astype(jnp.bfloat16)
+        field = dot(encoded, dec_ref[...]).astype(jnp.bfloat16)
+        for sample in range(samples):
+            token = lax.broadcasted_iota(jnp.int32, (1, kept), 1)
+            chosen = one_hot(col_ref[sample], token)
+            sent = dot(chosen, field[sample * kept : (sample + 1) * kept])
+            out_ref[:, sample] = sent.astype(jnp.bfloat16).reshape(peers, cap, narrow)
+
+    operands = (mixed, x, token_col, out_weight, up, down, dec_proj, *pieces)
     return pl.pallas_call(
         kernel,
-        grid=(blocks,),
-        in_specs=[
-            whole(mixed.shape),
-            whole(x.shape),
-            whole((samples, tile, 1)),
-            whole(out_weight.shape),
-            pl.BlockSpec((1, width, hidden), lambda i: (i, 0, 0)),
-            pl.BlockSpec((1, hidden, width), lambda i: (i, 0, 0)),
-            whole(dec_proj.shape),
-        ],
-        out_specs=whole((peers, samples, cap, narrow)),
+        in_specs=[pl.BlockSpec(memory_space=pltpu.VMEM)] * len(operands),
+        out_specs=pl.BlockSpec(memory_space=pltpu.VMEM),
         out_shape=jax.ShapeDtypeStruct((peers, samples, cap, narrow), jnp.bfloat16),
-        scratch_shapes=[
-            pltpu.VMEM((rows, width), jnp.bfloat16),
-            pltpu.VMEM((rows, width), jnp.bfloat16),
-            pltpu.VMEM((rows, width), jnp.float32),
-        ],
-        compiler_params=params(48),
+        compiler_params=params(40),
         name="feed_forward",
-    )(mixed, x, token_col, out_weight, up, down, dec_proj)
+    )(*operands)
+
+
+def share(up_weight, down_weight):
+    width, hidden = up_weight.shape
+    part = hidden // 2
+    at = (lax.axis_index("row") % 2) * part
+    up = lax.dynamic_slice_in_dim(up_weight, at, part, axis=1)
+    down = lax.dynamic_slice_in_dim(down_weight, at, part, axis=0)
+    return jnp.concatenate([up] + [down[:, i : i + part] for i in range(0, width, part)], 0)
+
+
+def from_dp(piece):
+    count = lax.axis_size("dp")
+    return [
+        lax.ppermute(piece, "dp", [(i, (i + hop) % count) for i in range(count)])
+        for hop in range(1, count)
+    ]
+
+
+def from_partner(piece):
+    return lax.ppermute(piece, "row", [(i, i ^ 1) for i in range(lax.axis_size("row"))])
 
 
 def place(home, cell_slot, mask_token, dec_proj):
@@ -332,8 +361,7 @@
     tile = tile_h * tile_w
     cap = tile // peers
     kept = tile // 4
-    up = lax.all_gather(up_weight, "dp", axis=0)
-    down = lax.all_gather(down_weight, "dp", axis=0)
+    piece = share(up_weight, down_weight)
 
     flat_mask = keep_mask.reshape(samples, tile)
     counts = jnp.sum(flat_mask, 1)
@@ -356,6 +384,8 @@
     outgoing = dispatch(
         my_start, cell_rank.reshape(samples, 1, tile), patches.reshape(samples, tile, width), peers
     )
+    outgoing, piece = lax.optimization_barrier((outgoing, piece))
+    pieces = from_dp(piece)
     arrived = lax.all_to_all(outgoing, PLANE, split_axis=0, concat_axis=0, tiled=True)
 
     slot = jnp.arange(cap, dtype=jnp.int32)[None, None, :]
@@ -366,9 +396,19 @@
     x, packed = project(arrived, token.reshape(samples, 1, tile), qkv_weight, kept)
     packed = lax.all_to_all(packed, PLANE, split_axis=0, concat_axis=0, tiled=True)
     mixed = attention(packed, kept)
+    mixed, *pieces = lax.optimization_barrier((mixed, *pieces))
+    pieces = pieces + [from_partner(one) for one in pieces]
     mixed = lax.all_to_all(mixed, PLANE, split_axis=0, concat_axis=0, tiled=True)
     returning = feed_forward(
-        mixed, x, token.reshape(samples, tile, 1), out_weight, up, down, dec_proj, cap
+        mixed,
+        x,
+        token.reshape(samples, tile, 1),
+        out_weight,
+        up_weight,
+        down_weight,
+        dec_proj,
+        pieces,
+        cap,
     )
     home = lax.all_to_all(returning, PLANE, split_axis=0, concat_axis=0, tiled=True)
 

time: 192 us -> 195 us (1.016)
  blocking collectives: 26.7 us -> 0 us
  between operations: 13.8 us -> 0.43 us
  waiting for transfers between devices: 50.1 us -> 62.3 us
  Pallas kernels: 49.4 us -> 60.5 us
  starting transfers between devices: 32.9 us -> 43.7 us
  local copies, waits for them, and re-layouts: 5.03 us -> 11.4 us
  other arithmetic: 2.84 us -> 5.53 us
    all_to_all x1 -> x0, blocking collectives: 26.7 us -> none  [shards(): lax.all_to_all(packed, PLANE, split_axis=0, concat_axis=0, tiled=True)]
    all_to_all x0 -> x1, waiting for transfers between devices: none -> 16.8 us  [shards(): lax.all_to_all(packed, PLANE, split_axis=0, concat_axis=0, tiled=True)]
    pallas_call x1, Pallas kernels: 32.8 us -> 43.1 us  [attention(): pl.pallas_call(kernel, grid=(peers // step,), in_specs=[pl.BlockSpec(pack...]
    ppermute x0 -> x6, starting transfers between devices: none -> 5.52 us  [the longest x3 4.67 us: from_dp(): lax.ppermute(piece, 'dp', [(i, (i + hop) % count) for i in range(count)])]
    unnamed x14 -> x24, local copies, waits for them, and re-layouts: 0.03 us -> 5.17 us
    all_to_all x0 -> x1, starting transfers between devices: none -> 5.14 us  [shards(): lax.all_to_all(packed, PLANE, split_axis=0, concat_axis=0, tiled=True)]
    all_to_all x1, waiting for transfers between devices: 5.89 us -> 2.82 us  [shards(): lax.all_to_all(jnp.broadcast_to(counts[None, None, :], (peers, 1, samples...]
  transfers between devices with their start and end apart: 10 -> 15, of which waited for: 7 -> 8; matrix products, arithmetic and copies ran while one was open for 4% -> 5% of each run, Pallas kernels for 21% -> 22%
where the time goes in v2:
time: 195 us; the launch traced here: 193 us
  waiting for transfers between devices  62.3 us (32%)
  Pallas kernels  60.5 us (31%)
  starting transfers between devices  43.7 us (22%)
  local copies, waits for them, and re-layouts  11.4 us (6%)
  matrix products  9.37 us (5%)
  other arithmetic  5.53 us (3%)
    pallas_call x1, Pallas kernels, attention(): pl.pallas_call(kernel, grid=(peers // step,), in_specs=[pl.BlockSpec(pack...  43.1 us
    all_to_all x1, waiting for transfers between devices, shards(): lax.all_to_all(outgoing, PLANE, split_axis=0, concat_axis=0, tiled=True)  20.8 us
    all_to_all x1, waiting for transfers between devices, shards(): lax.all_to_all(packed, PLANE, split_axis=0, concat_axis=0, tiled=True)  16.8 us
    all_to_all x1, waiting for transfers between devices, shards(): lax.all_to_all(returning, PLANE, split_axis=0, concat_axis=0, tiled=True)  10.2 us
    pallas_call x1, Pallas kernels, feed_forward(): pl.pallas_call(kernel, in_specs=[pl.BlockSpec(memory_space=pltpu.VMEM)] *...  9.2 us
    all_to_all x1, starting transfers between devices, shards(): lax.all_to_all(jnp.broadcast_to(counts[None, None, :], (peers, 1, samples...  8.46 us
    dot_general x17, matrix products, convolve(): jnp.einsum('shwc,cd->shwd', extended[:, first:first + out_h, second:secon...  6.89 us
    ppermute x2, waiting for transfers between devices, extended_2(): lax.ppermute(head, axis, [((i + 1) % count, i) for i in range(ends)])  6 us
  transfers between devices with their start and end apart: 15, of which 8 were waited for; matrix products, arithmetic and copies ran while one was open for 5% of the time, Pallas kernels for 22%

profile of v2, /device:TPU:2, one launch (start us, length us, event | category | flops | bytes accessed | tf_op | source)
XLA Modules:
  0.0 193.1 jit_solution(11278658010031662203)
XLA Ops:
  1.6 8.5 %all-to-all-start = ((s32[32,1,2]{2,1,0:T(1,128)}), s32[32,1,2]{2,1,0:T(1,128)S(1)}, u32[]{:S(2)}, u32[]{:S(2)}) async-start(s32[32,1,2]{2,1,0:T(1,128)} %broadcast_in_dim.71), calls=%async_computation | async-start | bytes 32768 | tf_op jit(solution)/shard_map/all_to_all | solution.py:368
  13.3 2.8 %all-to-all-done = s32[32,1,2]{2,1,0:T(1,128)S(1)} async-done(((s32[32,1,2]{2,1,0:T(1,128)}), s32[32,1,2]{2,1,0:T(1,128)S(1)}, u32[]{:S(2)}, u32[]{:S(2)}) %all-to-all-start) | async-done | bytes 288 | tf_op jit(solution)/shard_map/all_to_all | solution.py:368
  16.6 2.7 %dispatch.1 = bf16[32,2,16,768]{3,2,1,0:T(8,128)(2,1)} custom-call(s32[2]{0:T(128)S(1)} %select_reduce_fusion.1.start_ref, s32[2,1,512]{2,1,0:T(1,128)S(1)} %reshape.355.rank_ref, bf16[2,512,768]{2,1,0:T(8,128)(2,1)S(1)} %bitcast.158), custom_call_target="tpu_custom_call" | custom-call | tf_op jit(solution)/shard_map/dispatch/pallas_call | solution.py:85
  19.3 5.1 %all-to-all-start.1 = ((bf16[32,2,16,768]{3,2,1,0:T(8,128)(2,1)}), bf16[32,2,16,768]{3,2,1,0:T(8,128)(2,1)S(1)}, u32[]{:S(2)}, u32[]{:S(2)}) async-start(bf16[32,2,16,768]{3,2,1,0:T(8,128)(2,1)} %dispatch.1), calls=%async_computation.1 | async-start | bytes 3145728 | tf_op jit(solution)/shard_map/all_to_all | solution.py:389
  25.2 20.8 %all-to-all-done.1.arrived_ref = bf16[32,2,16,768]{3,2,1,0:T(8,128)(2,1)S(1)} async-done(((bf16[32,2,16,768]{3,2,1,0:T(8,128)(2,1)}), bf16[32,2,16,768]{3,2,1,0:T(8,128)(2,1)S(1)}, u32[]{:S(2)}, u32[]{:S(2)}) %all-to-all-start.1) | async-done | bytes 1572896 | tf_op jit(solution)/shard_map/all_to_all | solution.py:389
  46.0 4.5 %project.1 = (bf16[2,128,768]{2,1,0:T(8,128)(2,1)S(1)}, bf16[32,192,128]{2,1,0:T(8,128)(2,1)S(1)}) custom-call(s32[2,1,512]{2,1,0:T(1,128)S(1)} %compare_select_fusion.col_ref, bf16[32,2,16,768]{3,2,1,0:T(8,128)(2,1)S(1)} %all-to-all-done.1.arrived_ref, bf16[768,2304]{1,0:T(8,128)(2,1)} %weight_ref.1), custom_call_target="tpu_custom_call" | custom-call | tf_op jit(solution)/shard_map/project/pallas_call | solution.py:136
  52.4 5.1 %all-to-all-start.2 = ((bf16[32,192,128]{2,1,0:T(8,128)(2,1)}), bf16[32,192,128]{2,1,0:T(8,128)(2,1)S(1)}, u32[]{:S(2)}, u32[]{:S(2)}) async-start(bf16[32,192,128]{2,1,0:T(8,128)(2,1)} %copy-done.5), calls=%async_computation.2 | async-start | bytes 3145728 | tf_op jit(solution)/shard_map/all_to_all | solution.py:397
  57.5 3.1 %collective-permute-start.2 = (bf16[1536,384]{1,0:T(8,128)(2,1)}, bf16[1536,384]{1,0:T(8,128)(2,1)}, u32[]{:S(2)}, u32[]{:S(2)}) collective-permute-start(bf16[1536,384]{1,0:T(8,128)(2,1)} %pad_maximum_fusion), channel_id=1, source_target_pairs={{0,96},{32,0},{64,32},{96,64},{1,97},{33,1},{65,33},{97,65},{2,98}... | collective-permute-start | bytes 3538952 | tf_op jit(solution)/shard_map/ppermute | solution.py:301
  62.2 16.8 %all-to-all-done.2.packed_ref = bf16[32,192,128]{2,1,0:T(8,128)(2,1)S(1)} async-done(((bf16[32,192,128]{2,1,0:T(8,128)(2,1)}), bf16[32,192,128]{2,1,0:T(8,128)(2,1)S(1)}, u32[]{:S(2)}, u32[]{:S(2)}) %all-to-all-start.2) | async-done | bytes 1572896 | tf_op jit(solution)/shard_map/all_to_all | solution.py:397
  79.0 43.1 %attention.1 = bf16[32,64,128]{2,1,0:T(8,128)(2,1)} custom-call(bf16[32,192,128]{2,1,0:T(8,128)(2,1)S(1)} %all-to-all-done.2.packed_ref), custom_call_target="tpu_custom_call" | custom-call | tf_op jit(solution)/shard_map/attention/pallas_call | solution.py:224
  122.9 5.1 %all-to-all-start.3 = ((bf16[32,64,128]{2,1,0:T(8,128)(2,1)}), bf16[32,64,128]{2,1,0:T(8,128)(2,1)S(1)}, u32[]{:S(2)}, u32[]{:S(2)}) async-start(bf16[32,64,128]{2,1,0:T(8,128)(2,1)} %attention.1), calls=%async_computation.3 | async-start | bytes 1048576 | tf_op jit(solution)/shard_map/all_to_all | solution.py:401
  131.4 1.8 fusion.9.col_ref
  133.2 5.3 %all-to-all-done.3.mixed_ref = bf16[32,64,128]{2,1,0:T(8,128)(2,1)S(1)} async-done(((bf16[32,64,128]{2,1,0:T(8,128)(2,1)}), bf16[32,64,128]{2,1,0:T(8,128)(2,1)S(1)}, u32[]{:S(2)}, u32[]{:S(2)}) %all-to-all-start.3) | async-done | bytes 524320 | tf_op jit(solution)/shard_map/all_to_all | solution.py:401
  141.8 9.2 %feed_forward.1 = bf16[32,2,16,256]{3,2,1,0:T(8,128)(2,1)} custom-call(bf16[32,64,128]{2,1,0:T(8,128)(2,1)S(1)} %all-to-all-done.3.mixed_ref, bf16[2,128,768]{2,1,0:T(8,128)(2,1)S(1)} %copy-done.9, s32[2,512,1]{2,1,0:T(8,128)S(1)} %fusion.9.col_ref, bf16[768,768]{1,0:T(8,128)(2,1)S(1)} %copy-done.7, bf16[768,768]{1,0:T(8,128)(2,1)S(1)} %copy-done.1, ...), custom_call_target="tpu_custom_call" | custom-call | tf_op jit(solution)/shard_map/feed_forward/pallas_call | solution.py:279
  151.0 5.3 %all-to-all-start.4 = ((bf16[32,2,16,256]{3,2,1,0:T(8,128)(2,1)}), bf16[32,2,16,256]{3,2,1,0:T(8,128)(2,1)S(1)}, u32[]{:S(2)}, u32[]{:S(2)}) async-start(bf16[32,2,16,256]{3,2,1,0:T(8,128)(2,1)} %feed_forward.1), calls=%async_computation.4 | async-start | bytes 1048576 | tf_op jit(solution)/shard_map/all_to_all | solution.py:413
  156.5 10.2 %all-to-all-done.4.home_ref = bf16[32,2,16,256]{3,2,1,0:T(8,128)(2,1)S(1)} async-done(((bf16[32,2,16,256]{3,2,1,0:T(8,128)(2,1)}), bf16[32,2,16,256]{3,2,1,0:T(8,128)(2,1)S(1)}, u32[]{:S(2)}, u32[]{:S(2)}) %all-to-all-start.4) | async-done | bytes 524320 | tf_op jit(solution)/shard_map/all_to_all | solution.py:413
  167.8 2.1 %collective-permute-start.6 = (bf16[2,2,32,256]{3,2,1,0:T(8,128)(2,1)S(1)}, bf16[2,2,32,256]{3,2,1,0:T(8,128)(2,1)S(1)}, u32[]{:S(2)}, u32[]{:S(2)}) collective-permute-start(bf16[2,2,32,256]{3,2,1,0:T(8,128)(2,1)S(1)} %get-tuple-element.25), channel_id=1, source_target_pairs={{0,4},{4,8},{8,12},{12,16},{16,20},{20,24},{24,28},{1,5},{5,9},{9,... | collective-permute-start | bytes 196616 | tf_op jit(solution)/shard_map/ppermute | solution.py:27
  169.9 3.6 %collective-permute-start.7 = (bf16[2,2,32,256]{3,2,1,0:T(8,128)(2,1)S(1)}, bf16[2,2,32,256]{3,2,1,0:T(8,128)(2,1)S(1)}, u32[]{:S(2)}, u32[]{:S(2)}) collective-permute-start(bf16[2,2,32,256]{3,2,1,0:T(8,128)(2,1)S(1)} %get-tuple-element.26), channel_id=1, source_target_pairs={{4,0},{8,4},{12,8},{16,12},{20,16},{24,20},{28,24},{5,1},{9,5},{13... | collective-permute-start | bytes 196616 | tf_op jit(solution)/shard_map/ppermute | solution.py:29
  173.5 1.9 collective-permute-done.7
  175.4 1.9 collective-permute-start.8
  177.3 1.5 collective-permute-start.9
  179.2 4.1 %collective-permute-done.9 = bf16[2,20,2,256]{3,2,1,0:T(2,128)(2,1)S(1)} collective-permute-done((bf16[2,20,2,256]{3,2,1,0:T(2,128)(2,1)S(1)}, bf16[2,20,2,256]{3,2,1,0:T(2,128)(2,1)S(1)}, u32[]{:S(2)}, u32[]{:S(2)}) %collective-permute-start.9) | collective-permute-done | bytes 40992 | tf_op jit(solution)/shard_map/ppermute | solution.py:29
  187.0 1.4 select_convert_fusion
  190.9 2.3 %convolution_convert_fusion = bf16[2,16,32,128]{3,2,1,0:T(8,128)(2,1)} fusion(f32[2,16,32,256]{3,2,1,0:T(8,128)S(1)} %convolution_add_fusion.1, bf16[2,18,34,256]{3,2,1,0:T(8,128)(2,1)S(1)} %select_convert_fusion, bf16[2,9,256,256]{3,2,1,0:T(8,128)(2,1)} %param.18, bf16[256,128]{1,0:T(8,128)(2,1)S(1)} %copy-done), kind=kOutput, calls=%fused_computation.9 | convolution fusion | flops 203554816 | bytes 2555904 | tf_op jit(solution)/shard_map/dot_general | solution.py:48
  (91 shorter events, 24.7 us)
Async XLA Ops:
  0.0 190.9 %copy-start = (bf16[256,128]{1,0:T(8,128)(2,1)S(1)}, bf16[256,128]{1,0:T(8,128)(2,1)}, u32[]{:S(2)}) copy-start(bf16[256,128]{1,0:T(8,128)(2,1)} %param.19) | copy-start | bytes 196612
  0.0 11.9 %copy-start.2 = (bf16[768,768]{1,0:T(8,128)(2,1)S(1)}, bf16[768,768]{1,0:T(8,128)(2,1)}, u32[]{:S(2)}) copy-start(bf16[768,768]{1,0:T(8,128)(2,1)} %down_ref.1) | copy-start | bytes 3538948
  1.6 14.6 %all-to-all-start = ((s32[32,1,2]{2,1,0:T(1,128)}), s32[32,1,2]{2,1,0:T(1,128)S(1)}, u32[]{:S(2)}, u32[]{:S(2)}) async-start(s32[32,1,2]{2,1,0:T(1,128)} %broadcast_in_dim.71), calls=%async_computation | async-start | bytes 32768 | tf_op jit(solution)/shard_map/all_to_all | solution.py:368
  12.0 4.6 %copy-start.6 = (bf16[2,16,32,768]{3,2,1,0:T(8,128)(2,1)S(1)}, bf16[2,16,32,768]{3,2,1,0:T(8,128)(2,1)}, u32[]{:S(2)}) copy-start(bf16[2,16,32,768]{3,2,1,0:T(8,128)(2,1)} %param.10) | copy-start | bytes 4718596
  19.3 26.6 %all-to-all-start.1 = ((bf16[32,2,16,768]{3,2,1,0:T(8,128)(2,1)}), bf16[32,2,16,768]{3,2,1,0:T(8,128)(2,1)S(1)}, u32[]{:S(2)}, u32[]{:S(2)}) async-start(bf16[32,2,16,768]{3,2,1,0:T(8,128)(2,1)} %dispatch.1), calls=%async_computation.1 | async-start | bytes 3145728 | tf_op jit(solution)/shard_map/all_to_all | solution.py:389
  50.5 1.2 copy-start.5
  52.4 26.6 %all-to-all-start.2 = ((bf16[32,192,128]{2,1,0:T(8,128)(2,1)}), bf16[32,192,128]{2,1,0:T(8,128)(2,1)S(1)}, u32[]{:S(2)}, u32[]{:S(2)}) async-start(bf16[32,192,128]{2,1,0:T(8,128)(2,1)} %copy-done.5), calls=%async_computation.2 | async-start | bytes 3145728 | tf_op jit(solution)/shard_map/all_to_all | solution.py:397
  57.5 64.5 %collective-permute-start.2 = (bf16[1536,384]{1,0:T(8,128)(2,1)}, bf16[1536,384]{1,0:T(8,128)(2,1)}, u32[]{:S(2)}, u32[]{:S(2)}) collective-permute-start(bf16[1536,384]{1,0:T(8,128)(2,1)} %pad_maximum_fusion), channel_id=1, source_target_pairs={{0,96},{32,0},{64,32},{96,64},{1,97},{33,1},{65,33},{97,65},{2,98}... | collective-permute-start | bytes 3538952 | tf_op jit(solution)/shard_map/ppermute | solution.py:301
  60.6 61.5 %collective-permute-start.1 = (bf16[1536,384]{1,0:T(8,128)(2,1)}, bf16[1536,384]{1,0:T(8,128)(2,1)}, u32[]{:S(2)}, u32[]{:S(2)}) collective-permute-start(bf16[1536,384]{1,0:T(8,128)(2,1)} %pad_maximum_fusion), channel_id=1, source_target_pairs={{0,64},{32,96},{64,0},{96,32},{1,65},{33,97},{65,1},{97,33},{2,66}... | collective-permute-start | bytes 3538952 | tf_op jit(solution)/shard_map/ppermute | solution.py:301
  61.2 60.8 %collective-permute-start = (bf16[1536,384]{1,0:T(8,128)(2,1)}, bf16[1536,384]{1,0:T(8,128)(2,1)}, u32[]{:S(2)}, u32[]{:S(2)}) collective-permute-start(bf16[1536,384]{1,0:T(8,128)(2,1)} %pad_maximum_fusion), channel_id=1, source_target_pairs={{0,32},{32,64},{64,96},{96,0},{1,33},{33,65},{65,97},{97,1},{2,34}... | collective-permute-start | bytes 3538952 | tf_op jit(solution)/shard_map/ppermute | solution.py:301
  122.1 16.4 %collective-permute-start.3 = (bf16[1536,384]{1,0:T(8,128)(2,1)}, bf16[1536,384]{1,0:T(8,128)(2,1)}, u32[]{:S(2)}, u32[]{:S(2)}) collective-permute-start(bf16[1536,384]{1,0:T(8,128)(2,1)} %collective-permute-done.rest_0_), channel_id=1, source_target_pairs={{0,4},{4,0},{8,12},{12,8},{16,20},{20,16},{24,28},{28,24},{1,5},{5... | collective-permute-start | bytes 3538952 | tf_op jit(solution)/shard_map/ppermute | solution.py:307
  122.2 16.3 %collective-permute-start.4 = (bf16[1536,384]{1,0:T(8,128)(2,1)}, bf16[1536,384]{1,0:T(8,128)(2,1)}, u32[]{:S(2)}, u32[]{:S(2)}) collective-permute-start(bf16[1536,384]{1,0:T(8,128)(2,1)} %collective-permute-done.1.rest_1_), channel_id=1, source_target_pairs={{0,4},{4,0},{8,12},{12,8},{16,20},{20,16},{24,28},{28,24},{1,5},{5... | collective-permute-start | bytes 3538952 | tf_op jit(solution)/shard_map/ppermute | solution.py:307
  122.7 15.8 %collective-permute-start.5 = (bf16[1536,384]{1,0:T(8,128)(2,1)}, bf16[1536,384]{1,0:T(8,128)(2,1)}, u32[]{:S(2)}, u32[]{:S(2)}) collective-permute-start(bf16[1536,384]{1,0:T(8,128)(2,1)} %collective-permute-done.2.rest_2_), channel_id=1, source_target_pairs={{0,4},{4,0},{8,12},{12,8},{16,20},{20,16},{24,28},{28,24},{1,5},{5... | collective-permute-start | bytes 3538952 | tf_op jit(solution)/shard_map/ppermute | solution.py:307
  122.9 15.5 %all-to-all-start.3 = ((bf16[32,64,128]{2,1,0:T(8,128)(2,1)}), bf16[32,64,128]{2,1,0:T(8,128)(2,1)S(1)}, u32[]{:S(2)}, u32[]{:S(2)}) async-start(bf16[32,64,128]{2,1,0:T(8,128)(2,1)} %attention.1), calls=%async_computation.3 | async-start | bytes 1048576 | tf_op jit(solution)/shard_map/all_to_all | solution.py:401
  129.2 9.3 %copy-start.1 = (bf16[768,768]{1,0:T(8,128)(2,1)S(1)}, bf16[768,768]{1,0:T(8,128)(2,1)}, u32[]{:S(2)}) copy-start(bf16[768,768]{1,0:T(8,128)(2,1)} %up_ref.1) | copy-start | bytes 3538948
  139.5 1.3 copy-start.7
  141.8 14.5 %copy-start.11 = (bf16[768]{0:T(1024)(128)(2,1)S(1)}, bf16[768]{0:T(1024)(128)(2,1)}, u32[]{:S(2)}) copy-start(bf16[768]{0:T(1024)(128)(2,1)} %param.12) | copy-start | bytes 4612
  151.0 15.8 %copy-start.4 = (bf16[768,256]{1,0:T(8,128)(2,1)S(1)}, bf16[768,256]{1,0:T(8,128)(2,1)}, u32[]{:S(2)}) copy-start(bf16[768,256]{1,0:T(8,128)(2,1)} %dec_ref.3) | copy-start | bytes 1179652
  151.0 15.8 %all-to-all-start.4 = ((bf16[32,2,16,256]{3,2,1,0:T(8,128)(2,1)}), bf16[32,2,16,256]{3,2,1,0:T(8,128)(2,1)S(1)}, u32[]{:S(2)}, u32[]{:S(2)}) async-start(bf16[32,2,16,256]{3,2,1,0:T(8,128)(2,1)} %feed_forward.1), calls=%async_computation.4 | async-start | bytes 1048576 | tf_op jit(solution)/shard_map/all_to_all | solution.py:413
  167.8 16.1 %copy-start.10 = (bf16[2,9,256,256]{3,2,1,0:T(8,128)(2,1)S(1)}, bf16[2,9,256,256]{3,2,1,0:T(8,128)(2,1)}, u32[]{:S(2)}) copy-start(bf16[2,9,256,256]{3,2,1,0:T(8,128)(2,1)} %param.18) | copy-start | bytes 7077892
  167.8 5.7 %collective-permute-start.6 = (bf16[2,2,32,256]{3,2,1,0:T(8,128)(2,1)S(1)}, bf16[2,2,32,256]{3,2,1,0:T(8,128)(2,1)S(1)}, u32[]{:S(2)}, u32[]{:S(2)}) collective-permute-start(bf16[2,2,32,256]{3,2,1,0:T(8,128)(2,1)S(1)} %get-tuple-element.25), channel_id=1, source_target_pairs={{0,4},{4,8},{8,12},{12,16},{16,20},{20,24},{24,28},{1,5},{5,9},{9,... | collective-permute-start | bytes 196616 | tf_op jit(solution)/shard_map/ppermute | solution.py:27
  169.9 5.4 %collective-permute-start.7 = (bf16[2,2,32,256]{3,2,1,0:T(8,128)(2,1)S(1)}, bf16[2,2,32,256]{3,2,1,0:T(8,128)(2,1)S(1)}, u32[]{:S(2)}, u32[]{:S(2)}) collective-permute-start(bf16[2,2,32,256]{3,2,1,0:T(8,128)(2,1)S(1)} %get-tuple-element.26), channel_id=1, source_target_pairs={{4,0},{8,4},{12,8},{16,12},{20,16},{24,20},{28,24},{5,1},{9,5},{13... | collective-permute-start | bytes 196616 | tf_op jit(solution)/shard_map/ppermute | solution.py:29
  175.4 3.8 %collective-permute-start.8 = (bf16[2,20,2,256]{3,2,1,0:T(2,128)(2,1)S(1)}, bf16[2,20,2,256]{3,2,1,0:T(2,128)(2,1)S(1)}, u32[]{:S(2)}, u32[]{:S(2)}) collective-permute-start(bf16[2,20,2,256]{3,2,1,0:T(2,128)(2,1)S(1)} %get-tuple-element.23), channel_id=1, source_target_pairs={{0,1},{1,2},{2,3},{4,5},{5,6},{6,7},{8,9},{9,10},{10,11},{12,13},{... | collective-permute-start | bytes 122888 | tf_op jit(solution)/shard_map/ppermute | solution.py:27
  177.3 6.1 %collective-permute-start.9 = (bf16[2,20,2,256]{3,2,1,0:T(2,128)(2,1)S(1)}, bf16[2,20,2,256]{3,2,1,0:T(2,128)(2,1)S(1)}, u32[]{:S(2)}, u32[]{:S(2)}) collective-permute-start(bf16[2,20,2,256]{3,2,1,0:T(2,128)(2,1)S(1)} %get-tuple-element.24), channel_id=1, source_target_pairs={{1,0},{2,1},{3,2},{5,4},{6,5},{7,6},{9,8},{10,9},{11,10},{13,12},{... | collective-permute-start | bytes 122888 | tf_op jit(solution)/shard_map/ppermute | solution.py:29
  (3 other events, 2.7 us)

commit v3 on v2

--- a/solution.py
+++ b/solution.py
@@ -1,5 +1,6 @@
 import jax
 import jax.numpy as jnp
+import numpy as np
 from jax import lax
 from jax.experimental import pallas as pl
 from jax.experimental.pallas import tpu as pltpu
@@ -12,7 +13,7 @@
 ROOT_HALF = 0.7071067811865476
 PLANE = ("row", "col")
 MIB = 1 << 20
-ATTENTION_MIB = 40
+ATTENTION_MIB = 34
 SAFE = 96.0
 
 
@@ -33,6 +34,44 @@
     return cells
 
 
+def ring(height, width):
+    low, high = slice(0, REACH), slice(-REACH, None)
+    mid = slice(REACH, -REACH)
+    order = np.zeros((height, width), np.int32)
+    ends = [0]
+    for rows, cols in (
+        (low, low),
+        (low, mid),
+        (low, high),
+        (mid, high),
+        (high, high),
+        (high, mid),
+        (high, low),
+        (mid, low),
+        (mid, mid),
+    ):
+        block = order[rows, cols]
+        block[...] = ends[-1] + np.arange(block.size, dtype=np.int32).reshape(block.shape)
+        ends.append(ends[-1] + block.size)
+    return order, np.array(ends, np.int32)
+
+
+PIECES = (
+    (0, 0, 0, 9, 16),
+    (-1, 0, 4, 7, 2),
+    (1, 0, 0, 3, 2),
+    (0, -1, 2, 5, 1),
+    (0, 1, 6, 8, 1),
+    (0, 1, 0, 1, 1),
+    (-1, -1, 4, 5, 1),
+    (-1, 1, 6, 7, 1),
+    (1, -1, 2, 3, 1),
+    (1, 1, 0, 1, 1),
+)
+REACH = 2
+SLOTS = 32
+
+
 def normalize(wide):
     mean = jnp.mean(wide, -1, keepdims=True)
     centred = wide - mean
@@ -64,6 +103,10 @@
             )
             total = term if total is None else total + term
     return total
+
+
+def in_hbm(array):
+    return pltpu.with_memory_space_constraint(array, pltpu.HBM)
 
 
 def params(limit):
@@ -107,51 +150,62 @@
     places = peers // samples
     half = kept // 2
 
-    def kernel(col_ref, arrived_ref, weight_ref, x_ref, out_ref):
+    def kernel(col_ref, arrived_ref, weight_hbm, x_ref, out_ref, weight, sems):
+        copies = []
+        for third in range(3):
+            cols = pl.ds(third * width, width)
+            copies.append(
+                pltpu.make_async_copy(weight_hbm.at[:, cols], weight.at[third], sems.at[third])
+            )
+            copies[-1].start()
         token = lax.broadcasted_iota(jnp.int32, (kept, 1), 0)
-        chosen = one_hot(token, col_ref[...].reshape(1, tile))
-        x = dot(chosen, arrived_ref[...].reshape(tile, width))
-        x_ref[...] = x.astype(jnp.bfloat16).reshape(1, kept, width)
-        normed = normalize(x)
-        qkv = dot(normed, weight_ref[...])
+        rows = []
+        for sample in range(samples):
+            chosen = one_hot(token, col_ref[sample])
+            rows.append(dot(chosen, arrived_ref[:, sample].reshape(tile, width)))
+            x_ref[sample] = rows[-1].astype(jnp.bfloat16)
+        normed = normalize(jnp.concatenate(rows, 0))
+        qkv = []
+        for third in range(3):
+            copies[third].wait()
+            qkv.append(dot(normed, weight[third]))
         low = lax.broadcasted_iota(jnp.int32, (kept, lanes), 1) < HD
         low_half = lax.broadcasted_iota(jnp.int32, (half, lanes), 1) < HD
-        for group in range(groups):
-            at = group * lanes
-            q = qkv[:, at : at + lanes] * (0.125 * LOG2E)
-            k = qkv[:, width + at : width + at + lanes]
-            v = qkv[:, 2 * width + at : 2 * width + at + lanes]
-            top, bottom = v[:half], v[half:]
-            first = jnp.where(low, q, pltpu.roll(k, HD, 1))
-            second = jnp.where(low, pltpu.roll(q, HD, 1), k)
-            first_v = jnp.where(low_half, top, pltpu.roll(bottom, HD, 1))
-            second_v = jnp.where(low_half, pltpu.roll(top, HD, 1), bottom)
-            out_ref[2 * group, :kept] = first.astype(jnp.bfloat16)
-            out_ref[2 * group, kept:] = first_v.astype(jnp.bfloat16)
-            out_ref[2 * group + 1, :kept] = second.astype(jnp.bfloat16)
-            out_ref[2 * group + 1, kept:] = second_v.astype(jnp.bfloat16)
-        for place in range(2 * groups, places):
-            out_ref[place] = jnp.zeros((kept + half, lanes), jnp.bfloat16)
+        for sample in range(samples):
+            q_all, k_all, v_all = (one[sample * kept : (sample + 1) * kept] for one in qkv)
+            for group in range(groups):
+                at = group * lanes
+                to = sample * places + 2 * group
+                q = q_all[:, at : at + lanes] * (0.125 * LOG2E)
+                k = k_all[:, at : at + lanes]
+                v = v_all[:, at : at + lanes]
+                top, bottom = v[:half], v[half:]
+                first = jnp.where(low, q, pltpu.roll(k, HD, 1))
+                second = jnp.where(low, pltpu.roll(q, HD, 1), k)
+                first_v = jnp.where(low_half, top, pltpu.roll(bottom, HD, 1))
+                second_v = jnp.where(low_half, pltpu.roll(top, HD, 1), bottom)
+                out_ref[to, :kept] = first.astype(jnp.bfloat16)
+                out_ref[to, kept:] = first_v.astype(jnp.bfloat16)
+                out_ref[to + 1, :kept] = second.astype(jnp.bfloat16)
+                out_ref[to + 1, kept:] = second_v.astype(jnp.bfloat16)
+            for place in range(2 * groups, places):
+                out_ref[sample * places + place] = jnp.zeros((kept + half, lanes), jnp.bfloat16)
 
     return pl.pallas_call(
         kernel,
-        grid=(samples,),
-        in_specs=[
-            pl.BlockSpec((1, 1, tile), lambda s: (s, 0, 0)),
-            pl.BlockSpec((peers, 1, cap, width), lambda s: (0, s, 0, 0)),
-            pl.BlockSpec((width, 3 * width), lambda s: (0, 0)),
-        ],
-        out_specs=[
-            pl.BlockSpec((1, kept, width), lambda s: (s, 0, 0)),
-            pl.BlockSpec((places, kept + half, lanes), lambda s: (s, 0, 0)),
-        ],
+        in_specs=[pl.BlockSpec(memory_space=pltpu.VMEM)] * 2 + [pl.BlockSpec(memory_space=pltpu.HBM)],
+        out_specs=[pl.BlockSpec(memory_space=pltpu.VMEM)] * 2,
         out_shape=[
             jax.ShapeDtypeStruct((samples, kept, width), jnp.bfloat16),
             jax.ShapeDtypeStruct((peers, kept + half, lanes), jnp.bfloat16),
         ],
-        compiler_params=params(48),
+        scratch_shapes=[
+            pltpu.VMEM((3, width, width), jnp.bfloat16),
+            pltpu.SemaphoreType.DMA((3,)),
+        ],
+        compiler_params=params(20),
         name="project",
-    )(token_col, arrived, qkv_weight)
+    )(token_col, arrived, in_hbm(qkv_weight))
 
 
 def attention(packed, kept):
@@ -238,14 +292,28 @@
     )(packed)
 
 
-def feed_forward(mixed, x, token_col, out_weight, up, down, dec_proj, pieces, cap):
+def feed_forward(mixed, x, token_col, out_weight, up, down, dec_proj, pieces, slots):
     peers, half, lanes = mixed.shape
     samples, kept, width = x.shape
     places = peers // samples
     narrow = dec_proj.shape[1]
 
-    def kernel(mixed_ref, x_ref, col_ref, out_w, up_ref, down_ref, dec_ref, *rest):
-        *piece_refs, out_ref = rest
+    weights = [in_hbm(one) for one in (out_weight, up, down, *pieces, dec_proj)]
+    count = len(weights)
+
+    def kernel(mixed_ref, x_ref, col_ref, *rest):
+        sources, out_ref, held, sems = rest[:count], rest[count], rest[count + 1 : -1], rest[-1]
+        copies = [
+            pltpu.make_async_copy(source, held[at], sems.at[at])
+            for at, source in enumerate(sources)
+        ]
+        for copy in copies:
+            copy.start()
+
+        def ready(at):
+            copies[at].wait()
+            return held[at]
+
         low = lax.broadcasted_iota(jnp.int32, (half, lanes), 1) < HD
         attn = []
         for sample in range(samples):
@@ -259,31 +327,35 @@
             attn.append(jnp.concatenate(parts, 1))
         attn = jnp.concatenate(attn, 0)
         rows = x_ref[...].reshape(samples * kept, width)
-        x_one = (rows.astype(jnp.float32) + dot(attn, out_w[...])).astype(jnp.bfloat16)
+        x_one = (rows.astype(jnp.float32) + dot(attn, ready(0)[...])).astype(jnp.bfloat16)
         normed = normalize(x_one.astype(jnp.float32))
-        total = dot(gelu(dot(normed, up_ref[...])).astype(jnp.bfloat16), down_ref[...])
-        for piece in piece_refs:
+        inner = gelu(dot(normed, ready(1)[...])).astype(jnp.bfloat16)
+        total = dot(inner, ready(2)[...])
+        for at in range(3, count - 1):
+            piece = ready(at)
             part = piece.shape[1]
             inner = gelu(dot(normed, piece[:width])).astype(jnp.bfloat16)
             added = [dot(inner, piece[pl.ds(at, part)]) for at in range(width, piece.shape[0], part)]
             total = total + jnp.concatenate(added, 1)
         encoded = (x_one.astype(jnp.float32) + total).astype(jnp.bfloat16)
-        field = dot(encoded, dec_ref[...]).astype(jnp.bfloat16)
+        field = dot(encoded, ready(count - 1)[...]).astype(jnp.bfloat16)
         for sample in range(samples):
             token = lax.broadcasted_iota(jnp.int32, (1, kept), 1)
             chosen = one_hot(col_ref[sample], token)
             sent = dot(chosen, field[sample * kept : (sample + 1) * kept])
-            out_ref[:, sample] = sent.astype(jnp.bfloat16).reshape(peers, cap, narrow)
-
-    operands = (mixed, x, token_col, out_weight, up, down, dec_proj, *pieces)
+            out_ref[:, sample] = sent.astype(jnp.bfloat16).reshape(peers, slots, narrow)
+
     return pl.pallas_call(
         kernel,
-        in_specs=[pl.BlockSpec(memory_space=pltpu.VMEM)] * len(operands),
+        in_specs=[pl.BlockSpec(memory_space=pltpu.VMEM)] * 3
+        + [pl.BlockSpec(memory_space=pltpu.HBM)] * count,
         out_specs=pl.BlockSpec(memory_space=pltpu.VMEM),
-        out_shape=jax.ShapeDtypeStruct((peers, samples, cap, narrow), jnp.bfloat16),
-        compiler_params=params(40),
+        out_shape=jax.ShapeDtypeStruct((peers, samples, slots, narrow), jnp.bfloat16),
+        scratch_shapes=[pltpu.VMEM(one.shape, one.dtype) for one in weights]
+        + [pltpu.SemaphoreType.DMA((count,))],
+        compiler_params=params(32),
         name="feed_forward",
-    )(*operands)
+    )(mixed, x, token_col, *weights)
 
 
 def share(up_weight, down_weight):
@@ -307,32 +379,132 @@
     return lax.ppermute(piece, "row", [(i, i ^ 1) for i in range(lax.axis_size("row"))])
 
 
-def place(home, cell_slot, mask_token, dec_proj):
-    peers, samples, cap, narrow = home.shape
-    tile = peers * cap
+def place(home, cell_slot, mask_token, dec_proj, cells):
+    peers, samples, slots, narrow = home.shape
     width = dec_proj.shape[0]
 
     def kernel(slot_ref, home_ref, token_ref, dec_ref, out_ref):
         slot = slot_ref[0]
-        chosen = one_hot(slot, lax.broadcasted_iota(jnp.int32, (1, tile), 1))
-        rows = dot(chosen, home_ref[...].reshape(tile, narrow))
+        chosen = one_hot(slot, lax.broadcasted_iota(jnp.int32, (1, peers * slots), 1))
+        rows = dot(chosen, home_ref[...].reshape(peers * slots, narrow))
         blank = dot(jnp.broadcast_to(token_ref[...], (8, width)), dec_ref[...])[:1]
-        out_ref[0] = jnp.where(slot < 0, blank, rows).astype(jnp.bfloat16)
+        out_ref[0] = jnp.where(slot == -1, blank, rows).astype(jnp.bfloat16)
 
     return pl.pallas_call(
         kernel,
         grid=(samples,),
         in_specs=[
-            pl.BlockSpec((1, tile, 1), lambda s: (s, 0, 0)),
-            pl.BlockSpec((peers, 1, cap, narrow), lambda s: (0, s, 0, 0)),
+            pl.BlockSpec((1, cells, 1), lambda s: (s, 0, 0)),
+            pl.BlockSpec((peers, 1, slots, narrow), lambda s: (0, s, 0, 0)),
             pl.BlockSpec((1, width), lambda s: (0, 0)),
             pl.BlockSpec((width, narrow), lambda s: (0, 0)),
         ],
-        out_specs=pl.BlockSpec((1, tile, narrow), lambda s: (s, 0, 0)),
-        out_shape=jax.ShapeDtypeStruct((samples, tile, narrow), jnp.bfloat16),
-        compiler_params=params(32),
+        out_specs=pl.BlockSpec((1, cells, narrow), lambda s: (s, 0, 0)),
+        out_shape=jax.ShapeDtypeStruct((samples, cells, narrow), jnp.bfloat16),
+        compiler_params=params(16),
         name="place",
     )(cell_slot, home, mask_token.reshape(1, width), dec_proj)
+
+
+def pick(which, table):
+    lane = lax.broadcasted_iota(jnp.int32, (1, table.shape[1]), 1)
+    found = jnp.sum(jnp.where(which == lane, table, 0.0), -1, keepdims=True)
+    return found.astype(jnp.int32)
+
+
+def index(me, told, rank, tiles, tile_h, tile_w, wide):
+    samples, peers, marks = told.shape
+    tiles_h, tiles_w = tiles
+    cells = rank.shape[1]
+    bases = [sum(piece[4] for piece in PIECES[:number]) for number in range(len(PIECES))]
+
+    def kernel(me_ref, told_ref, rank_ref, back_ref, slot_ref):
+        me = me_ref[0]
+        ahead = told_ref[0].astype(jnp.float32)
+        tile = lax.broadcasted_iota(jnp.int32, (peers, 1), 0)
+        other = lax.broadcasted_iota(jnp.int32, (1, peers), 1)
+        earlier = jnp.where(other < tile, 1.0, 0.0)
+        totals = jnp.broadcast_to(ahead[:, marks - 1 :], (peers, 128))
+        starts = jnp.dot(
+            earlier, totals, precision=lax.Precision.HIGHEST, preferred_element_type=jnp.float32
+        )
+        lane = lax.broadcasted_iota(jnp.int32, (1, 128), 1)
+        begins = jnp.zeros((peers, 128), jnp.float32)
+        ends = jnp.zeros((peers, 128), jnp.float32)
+        for number, (down, right, first, last, _) in enumerate(PIECES):
+            row, col = tile // tiles_w + down, tile % tiles_w + right
+            there = (row >= 0) & (row < tiles_h) & (col >= 0) & (col < tiles_w) & (lane == number)
+            for side, mark in enumerate((first, last)):
+                value = ahead[:, mark : mark + 1] + starts
+                hop = (-(down * tiles_w + right)) % peers
+                if hop:
+                    value = pltpu.roll(value, hop, 0)
+                if side:
+                    ends = jnp.where(there, value, ends)
+                else:
+                    begins = jnp.where(there, value, begins)
+
+        at = lax.broadcasted_iota(jnp.int32, (peers * SLOTS, 1), 0)
+        expand = jnp.where(at // SLOTS == other, 1.0, 0.0)
+        at = at % SLOTS
+        which = jnp.full(at.shape, len(PIECES), jnp.int32)
+        nth = jnp.zeros(at.shape, jnp.int32)
+        for number, base in enumerate(bases):
+            here = (at >= base) & (at < base + PIECES[number][4])
+            which = jnp.where(here, number, which)
+            nth = jnp.where(here, at - base, nth)
+
+        def spread(table):
+            rows = jnp.dot(
+                expand, table, precision=lax.Precision.HIGHEST, preferred_element_type=jnp.float32
+            )
+            return pick(which, rows)
+
+        position = (spread(begins) - me + peers - 1) // peers + nth
+        back_ref[0] = jnp.where(position * peers + me < spread(ends), position, -1)
+
+        cell = lax.broadcasted_iota(jnp.int32, (cells, 1), 0)
+        row, col = cell // wide, cell % wide
+        side = [(col < REACH), (col >= REACH + tile_w)]
+        which = jnp.where(row < REACH, 1, jnp.where(row >= REACH + tile_h, 2, 0))
+        right = jnp.where(row < 2 * REACH, 5, 4)
+        left = jnp.where(which == 0, 3, jnp.where(which == 1, 6, 8))
+        right = jnp.where(which == 0, right, jnp.where(which == 1, 7, 9))
+        which = jnp.where(side[0], left, jnp.where(side[1], right, which))
+        base = jnp.zeros(cell.shape, jnp.int32)
+        for number in range(1, len(bases)):
+            base = jnp.where(which == number, bases[number], base)
+        mine = jnp.sum(jnp.where(tile == me, begins, 0.0), 0, keepdims=True)
+        rank = rank_ref[0] - 1
+        peer = rank & (peers - 1)
+        nth = rank // peers - (pick(which, mine) - peer + peers - 1) // peers
+        row = row + (me // tiles_w) * tile_h - REACH
+        col = col + (me % tiles_w) * tile_w - REACH
+        within = (row >= 0) & (row < tiles_h * tile_h) & (col >= 0) & (col < tiles_w * tile_w)
+        slot = jnp.where(rank >= 0, peer * SLOTS + base + nth, -1)
+        slot_ref[0] = jnp.where(within, slot, -2)
+
+    return pl.pallas_call(
+        kernel,
+        grid_spec=pltpu.PrefetchScalarGridSpec(
+            num_scalar_prefetch=1,
+            grid=(samples,),
+            in_specs=[
+                pl.BlockSpec((1, peers, marks), lambda s, _: (s, 0, 0)),
+                pl.BlockSpec((1, cells, 1), lambda s, _: (s, 0, 0)),
+            ],
+            out_specs=[
+                pl.BlockSpec((1, peers * SLOTS, 1), lambda s, _: (s, 0, 0)),
+                pl.BlockSpec((1, cells, 1), lambda s, _: (s, 0, 0)),
+            ],
+        ),
+        out_shape=[
+            jax.ShapeDtypeStruct((samples, peers * SLOTS, 1), jnp.int32),
+            jax.ShapeDtypeStruct((samples, cells, 1), jnp.int32),
+        ],
+        compiler_params=params(16),
+        name="index",
+    )(me.reshape(1), told, rank)
 
 
 def inside(height, width, out_h, out_w, reach):
@@ -364,15 +536,21 @@
     piece = share(up_weight, down_weight)
 
     flat_mask = keep_mask.reshape(samples, tile)
-    counts = jnp.sum(flat_mask, 1)
+    order, ends = ring(tile_h, tile_w)
+    order = jnp.asarray(order.reshape(-1))
+    marks = len(ends)
+    earlier = order[:, None] < jnp.asarray(ends)[None, :]
+    counts = dot(flat_mask.astype(jnp.bfloat16), earlier.astype(jnp.bfloat16)).astype(jnp.int32)
     told = lax.all_to_all(
-        jnp.broadcast_to(counts[None, None, :], (peers, 1, samples)),
+        jnp.broadcast_to(counts.reshape(1, 1, samples * marks), (peers, 1, samples * marks)),
         PLANE,
         split_axis=0,
         concat_axis=0,
         tiled=True,
-    ).reshape(peers, samples)
-    before = jnp.arange(tile)[:, None] < jnp.arange(tile)[None, :]
+    ).reshape(peers, samples, marks)
+    segments = told
+    told = told[:, :, -1]
+    before = order[:, None] < order[None, :]
     running = dot(flat_mask.astype(jnp.bfloat16), before.astype(jnp.bfloat16)).astype(jnp.int32)
     cell_rank = jnp.where(flat_mask == 1, running, -1)
 
@@ -392,6 +570,22 @@
     local = slot * peers + ((me - starts.T[:, :, None]) & (peers - 1))
     token = (starts.T[:, :, None] + local - me) // peers
     token = jnp.where(local < told.T[:, :, None], token, -1)
+
+    rank = jnp.where(flat_mask == 1, my_start[:, None] + running + 1, 0)
+    rank = rank.reshape(samples, tile_h, tile_w)
+    rank = extended_2(rank, (("row", 1), ("col", 2)), REACH)
+    tiles = lax.axis_size("row"), lax.axis_size("col")
+    high, wide = tile_h + 2 * REACH, -(-(tile_w + 2 * REACH) // 8) * 8
+    rank = jnp.pad(rank, ((0, 0), (0, 0), (0, wide - rank.shape[2])))
+    back, cell_slot = index(
+        me,
+        segments.transpose(1, 0, 2),
+        rank.reshape(samples, high * wide, 1),
+        tiles,
+        tile_h,
+        tile_w,
+        wide,
+    )
 
     x, packed = project(arrived, token.reshape(samples, 1, tile), qkv_weight, kept)
     packed = lax.all_to_all(packed, PLANE, split_axis=0, concat_axis=0, tiled=True)
@@ -402,21 +596,18 @@
     returning = feed_forward(
         mixed,
         x,
-        token.reshape(samples, tile, 1),
+        back,
         out_weight,
         up_weight,
         down_weight,
         dec_proj,
         pieces,
-        cap,
+        SLOTS,
     )
     home = lax.all_to_all(returning, PLANE, split_axis=0, concat_axis=0, tiled=True)
 
-    cell_slot = ((my_start[:, None] + running) & (peers - 1)) * cap + running // peers
-    cell_slot = jnp.where(flat_mask == 1, cell_slot, -1)
-    h_zero = place(home, cell_slot.reshape(samples, tile, 1), mask_token, dec_proj)
-    h_zero = h_zero.reshape(samples, tile_h, tile_w, h_zero.shape[-1])
-    h_zero = extended_2(h_zero, (("row", 1), ("col", 2)), 2)
+    h_zero = place(home, cell_slot, mask_token, dec_proj, high * wide)
+    h_zero = h_zero.reshape(samples, high, wide, h_zero.shape[-1])[:, :, : tile_w + 2 * REACH]
     conv_one = convolve(h_zero, conv_weight[0], tile_h + 2, tile_w + 2)
     h_one = h_zero[:, 1:-1, 1:-1].astype(jnp.float32) + gelu(conv_one)
     within = inside(tile_h, tile_w, tile_h + 2, tile_w + 2, 1)

time: 195 us -> 197 us (1.010)
  Pallas kernels: 60.5 us -> 67.4 us
  local copies, waits for them, and re-layouts: 11.4 us -> 5.1 us
  other arithmetic: 5.53 us -> 2.12 us
  starting transfers between devices: 43.7 us -> 46.8 us
    pallas_call x2 -> x3, Pallas kernels: 5.46 us -> 12.2 us  [the longest x1 5.89 us: index(): pl.pallas_call(kernel, grid_spec=pltpu.PrefetchScalarGridSpec(num_scalar_...]
    all_to_all x1, waiting for transfers between devices: 10.2 us -> 15.5 us  [shards(): lax.all_to_all(returning, PLANE, split_axis=0, concat_axis=0, tiled=True)]
    all_to_all x1, waiting for transfers between devices: 5.27 us -> 0.01 us  [shards(): lax.all_to_all(mixed, PLANE, split_axis=0, concat_axis=0, tiled=True)]
    unnamed x24 -> x18, local copies, waits for them, and re-layouts: 5.17 us -> 1.82 us
  transfers between devices with their start and end apart: 15 -> 15, of which waited for: 8 -> 7; matrix products, arithmetic and copies ran while one was open for 5% -> 2% of each run, Pallas kernels for 22% -> 25%
where the time goes in v3:
time: 197 us; the launch traced here: 195 us
  Pallas kernels  67.4 us (34%)
  waiting for transfers between devices  62.5 us (32%)
  starting transfers between devices  46.8 us (24%)
  matrix products  10.3 us (5%)
  local copies, waits for them, and re-layouts  5.1 us (3%)
  other arithmetic  2.12 us (1%)
    pallas_call x1, Pallas kernels, attention(): pl.pallas_call(kernel, grid=(peers // step,), in_specs=[pl.BlockSpec(pack...  43.1 us
    all_to_all x1, waiting for transfers between devices, shards(): lax.all_to_all(outgoing, PLANE, split_axis=0, concat_axis=0, tiled=True)  20.8 us
    all_to_all x1, waiting for transfers between devices, shards(): lax.all_to_all(packed, PLANE, split_axis=0, concat_axis=0, tiled=True)  16.8 us
    all_to_all x1, waiting for transfers between devices, shards(): lax.all_to_all(returning, PLANE, split_axis=0, concat_axis=0, tiled=True)  15.5 us
    pallas_call x1, Pallas kernels, feed_forward(): pl.pallas_call(kernel, in_specs=[pl.BlockSpec(memory_space=pltpu.VMEM)] *...  9.36 us
    all_to_all x1, starting transfers between devices, shards(): lax.all_to_all(jnp.broadcast_to(counts.reshape(1, 1, samples * marks), (p...  8.47 us
    all_to_all x1, starting transfers between devices, shards(): lax.all_to_all(returning, PLANE, split_axis=0, concat_axis=0, tiled=True)  7.23 us
    dot_general x17, matrix products, convolve(): jnp.einsum('shwc,cd->shwd', extended[:, first:first + out_h, second:secon...  6.72 us
  transfers between devices with their start and end apart: 15, of which 7 were waited for; matrix products, arithmetic and copies ran while one was open for 2% of the time, Pallas kernels for 25%

profile of v3, /device:TPU:2, one launch (start us, length us, event | category | flops | bytes accessed | tf_op | source)
XLA Modules:
  0.0 194.6 jit_solution(3420311562458766333)
XLA Ops:
  2.6 8.5 %all-to-all-start = ((s32[32,1,20]{2,1,0:T(1,128)}), s32[32,1,20]{2,1,0:T(1,128)S(1)}, u32[]{:S(2)}, u32[]{:S(2)}) async-start(s32[32,1,20]{2,1,0:T(1,128)} %broadcast_in_dim.78), calls=%async_computation | async-start | bytes 32768 | tf_op jit(solution)/shard_map/all_to_all | solution.py:544
  13.3 3.9 %all-to-all-done = s32[32,1,20]{2,1,0:T(1,128)S(1)} async-done(((s32[32,1,20]{2,1,0:T(1,128)}), s32[32,1,20]{2,1,0:T(1,128)S(1)}, u32[]{:S(2)}, u32[]{:S(2)}) %all-to-all-start) | async-done | bytes 2592 | tf_op jit(solution)/shard_map/all_to_all | solution.py:544
  17.7 2.7 %dispatch.1 = bf16[32,2,16,768]{3,2,1,0:T(8,128)(2,1)} custom-call(s32[2]{0:T(128)S(1)} %select_reduce_fusion.1.start_ref, s32[2,1,512]{2,1,0:T(1,128)S(1)} %reshape.258.rank_ref, bf16[2,512,768]{2,1,0:T(8,128)(2,1)S(1)} %bitcast.158), custom_call_target="tpu_custom_call" | custom-call | tf_op jit(solution)/shard_map/dispatch/pallas_call | solution.py:128
  20.5 5.1 %all-to-all-start.1 = ((bf16[32,2,16,768]{3,2,1,0:T(8,128)(2,1)}), bf16[32,2,16,768]{3,2,1,0:T(8,128)(2,1)S(1)}, u32[]{:S(2)}, u32[]{:S(2)}) async-start(bf16[32,2,16,768]{3,2,1,0:T(8,128)(2,1)} %dispatch.1), calls=%async_computation.1 | async-start | bytes 3145728 | tf_op jit(solution)/shard_map/all_to_all | solution.py:567
  26.3 20.8 %all-to-all-done.1.arrived_ref = bf16[32,2,16,768]{3,2,1,0:T(8,128)(2,1)S(1)} async-done(((bf16[32,2,16,768]{3,2,1,0:T(8,128)(2,1)}), bf16[32,2,16,768]{3,2,1,0:T(8,128)(2,1)S(1)}, u32[]{:S(2)}, u32[]{:S(2)}) %all-to-all-start.1) | async-done | bytes 1572896 | tf_op jit(solution)/shard_map/all_to_all | solution.py:567
  47.1 4.6 %project.1 = (bf16[2,128,768]{2,1,0:T(8,128)(2,1)S(1)}, bf16[32,192,128]{2,1,0:T(8,128)(2,1)}) custom-call(s32[2,1,512]{2,1,0:T(1,128)S(1)} %compare_select_fusion.col_ref, bf16[32,2,16,768]{3,2,1,0:T(8,128)(2,1)S(1)} %all-to-all-done.1.arrived_ref, bf16[768,2304]{1,0:T(8,128)(2,1)} %weight_hbm.1), custom_call_target="tpu_custom_call" | custom-call | tf_op jit(solution)/shard_map/project/pallas_call | solution.py:194
  52.6 5.1 %all-to-all-start.2 = ((bf16[32,192,128]{2,1,0:T(8,128)(2,1)}), bf16[32,192,128]{2,1,0:T(8,128)(2,1)S(1)}, u32[]{:S(2)}, u32[]{:S(2)}) async-start(bf16[32,192,128]{2,1,0:T(8,128)(2,1)} %get-tuple-element.17), calls=%async_computation.2 | async-start | bytes 3145728 | tf_op jit(solution)/shard_map/all_to_all | solution.py:591
  57.7 3.1 %collective-permute-start.6 = (bf16[1536,384]{1,0:T(8,128)(2,1)S(1)}, bf16[1536,384]{1,0:T(8,128)(2,1)}, u32[]{:S(2)}, u32[]{:S(2)}) collective-permute-start(bf16[1536,384]{1,0:T(8,128)(2,1)S(1)} %pad_maximum_fusion), channel_id=1, source_target_pairs={{0,96},{32,0},{64,32},{96,64},{1,97},{33,1},{65,33},{97,65},{2,98}... | collective-permute-start | bytes 3538952 | tf_op jit(solution)/shard_map/ppermute | solution.py:373
  62.4 16.8 %all-to-all-done.2.packed_ref = bf16[32,192,128]{2,1,0:T(8,128)(2,1)S(1)} async-done(((bf16[32,192,128]{2,1,0:T(8,128)(2,1)}), bf16[32,192,128]{2,1,0:T(8,128)(2,1)S(1)}, u32[]{:S(2)}, u32[]{:S(2)}) %all-to-all-start.2) | async-done | bytes 1572896 | tf_op jit(solution)/shard_map/all_to_all | solution.py:591
  79.2 43.1 %attention.1 = bf16[32,64,128]{2,1,0:T(8,128)(2,1)} custom-call(bf16[32,192,128]{2,1,0:T(8,128)(2,1)S(1)} %all-to-all-done.2.packed_ref), custom_call_target="tpu_custom_call" | custom-call | tf_op jit(solution)/shard_map/attention/pallas_call | solution.py:278
  123.1 5.1 %all-to-all-start.3 = ((bf16[32,64,128]{2,1,0:T(8,128)(2,1)}), bf16[32,64,128]{2,1,0:T(8,128)(2,1)S(1)}, u32[]{:S(2)}, u32[]{:S(2)}) async-start(bf16[32,64,128]{2,1,0:T(8,128)(2,1)} %attention.1), calls=%async_computation.3 | async-start | bytes 1048576 | tf_op jit(solution)/shard_map/all_to_all | solution.py:595
  128.2 2.0 %collective-permute-start = (s32[2,2,32]{2,1,0:T(2,128)S(1)}, s32[2,2,32]{2,1,0:T(2,128)S(1)}, u32[]{:S(2)}, u32[]{:S(2)}) collective-permute-start(s32[2,2,32]{2,1,0:T(2,128)S(1)} %get-tuple-element.29), channel_id=1, source_target_pairs={{0,4},{4,8},{8,12},{12,16},{16,20},{20,24},{24,28},{1,5},{5,9},{9,... | collective-permute-start | bytes 1544 | tf_op jit(solution)/shard_map/ppermute | solution.py:28
  130.2 3.5 %collective-permute-start.1 = (s32[2,2,32]{2,1,0:T(2,128)S(1)}, s32[2,2,32]{2,1,0:T(2,128)S(1)}, u32[]{:S(2)}, u32[]{:S(2)}) collective-permute-start(s32[2,2,32]{2,1,0:T(2,128)S(1)} %get-tuple-element.30), channel_id=1, source_target_pairs={{4,0},{8,4},{12,8},{16,12},{20,16},{24,20},{28,24},{5,1},{9,5},{13... | collective-permute-start | bytes 1544 | tf_op jit(solution)/shard_map/ppermute | solution.py:30
  133.7 1.2 collective-permute-done
  135.1 3.4 %collective-permute-start.2 = (s32[2,20,2]{2,1,0:T(8,128)S(1)}, s32[2,20,2]{2,1,0:T(8,128)S(1)}, u32[]{:S(2)}, u32[]{:S(2)}) collective-permute-start(s32[2,20,2]{2,1,0:T(8,128)S(1)} %get-tuple-element.27), channel_id=1, source_target_pairs={{0,1},{1,2},{2,3},{4,5},{5,6},{6,7},{8,9},{9,10},{10,11},{12,13},{... | collective-permute-start | bytes 968 | tf_op jit(solution)/shard_map/ppermute | solution.py:28
  138.5 1.5 collective-permute-start.3
  140.1 4.1 %collective-permute-done.3 = s32[2,20,2]{2,1,0:T(8,128)S(1)} collective-permute-done((s32[2,20,2]{2,1,0:T(8,128)S(1)}, s32[2,20,2]{2,1,0:T(8,128)S(1)}, u32[]{:S(2)}, u32[]{:S(2)}) %collective-permute-start.3) | collective-permute-done | bytes 352 | tf_op jit(solution)/shard_map/ppermute | solution.py:30
  144.6 5.9 %index.1 = (s32[2,1024,1]{2,1,0:T(8,128)S(1)}, s32[2,800,1]{2,1,0:T(8,128)S(1)}) custom-call(s32[1]{0:T(128)} %bitcast.me_ref, s32[2,32,10]{2,1,0:T(8,128)S(1)} %bitcast.159, s32[2,800,1]{2,1,0:T(8,128)S(1)} %reshape.281.rank_ref), custom_call_target="tpu_custom_call" | custom-call | tf_op jit(solution)/shard_map/index/pallas_call | solution.py:487
  151.5 9.4 %feed_forward.1 = bf16[32,2,32,256]{3,2,1,0:T(8,128)(2,1)} custom-call(bf16[32,64,128]{2,1,0:T(8,128)(2,1)S(1)} %all-to-all-done.3.mixed_ref, bf16[2,128,768]{2,1,0:T(8,128)(2,1)S(1)} %copy-done.4, s32[2,1024,1]{2,1,0:T(8,128)S(1)} %get-tuple-element.21.col_ref, bf16[768,768]{1,0:T(8,128)(2,1)} %rest_0_.1, bf16[768,768]{1,0:T(8,128)(2,1)} %rest_1_.1, ...), custom_call_target="tpu_custom_call" | custom-call | tf_op jit(solution)/shard_map/feed_forward/pallas_call | solution.py:348
  160.9 7.2 %all-to-all-start.4 = ((bf16[32,2,32,256]{3,2,1,0:T(8,128)(2,1)}), bf16[32,2,32,256]{3,2,1,0:T(8,128)(2,1)S(1)}, u32[]{:S(2)}, u32[]{:S(2)}) async-start(bf16[32,2,32,256]{3,2,1,0:T(8,128)(2,1)} %feed_forward.1), calls=%async_computation.4 | async-start | bytes 2097152 | tf_op jit(solution)/shard_map/all_to_all | solution.py:607
  168.3 15.5 %all-to-all-done.4.home_ref = bf16[32,2,32,256]{3,2,1,0:T(8,128)(2,1)S(1)} async-done(((bf16[32,2,32,256]{3,2,1,0:T(8,128)(2,1)}), bf16[32,2,32,256]{3,2,1,0:T(8,128)(2,1)S(1)}, u32[]{:S(2)}, u32[]{:S(2)}) %all-to-all-start.4) | async-done | bytes 1048608 | tf_op jit(solution)/shard_map/all_to_all | solution.py:607
  183.8 1.7 place.1
  188.5 1.3 select_convert_fusion
  192.3 2.3 %convolution_convert_fusion = bf16[2,16,32,128]{3,2,1,0:T(8,128)(2,1)} fusion(f32[2,16,32,256]{3,2,1,0:T(8,128)S(1)} %convolution_add_fusion.1, bf16[2,18,34,256]{3,2,1,0:T(8,128)(2,1)S(1)} %select_convert_fusion, bf16[2,9,256,256]{3,2,1,0:T(8,128)(2,1)} %param.20, bf16[256,128]{1,0:T(8,128)(2,1)S(1)} %copy-done), kind=kOutput, calls=%fused_computation.9 | convolution fusion | flops 203554816 | bytes 2555904 | tf_op jit(solution)/shard_map/dot_general | solution.py:87
  (90 shorter events, 16.3 us)
Async XLA Ops:
  0.0 192.3 %copy-start = (bf16[256,128]{1,0:T(8,128)(2,1)S(1)}, bf16[256,128]{1,0:T(8,128)(2,1)}, u32[]{:S(2)}) copy-start(bf16[256,128]{1,0:T(8,128)(2,1)} %param.21) | copy-start | bytes 196612
  0.0 12.9 %copy-start.5 = (bf16[768,768]{1,0:T(8,128)(2,1)S(1)}, bf16[768,768]{1,0:T(8,128)(2,1)}, u32[]{:S(2)}) copy-start(bf16[768,768]{1,0:T(8,128)(2,1)} %rest_2_.1) | copy-start | bytes 3538948
  2.6 14.6 %all-to-all-start = ((s32[32,1,20]{2,1,0:T(1,128)}), s32[32,1,20]{2,1,0:T(1,128)S(1)}, u32[]{:S(2)}, u32[]{:S(2)}) async-start(s32[32,1,20]{2,1,0:T(1,128)} %broadcast_in_dim.78), calls=%async_computation | async-start | bytes 32768 | tf_op jit(solution)/shard_map/all_to_all | solution.py:544
  13.0 4.4 %copy-start.8 = (s32[512]{0:T(512)S(1)}, s32[512]{0:T(512)}, u32[]{:S(2)}) copy-start(s32[512]{0:T(512)} %constant.73.clone) | copy-start | bytes 6148
  13.0 4.7 %copy-start.2 = (bf16[2,16,32,768]{3,2,1,0:T(8,128)(2,1)S(1)}, bf16[2,16,32,768]{3,2,1,0:T(8,128)(2,1)}, u32[]{:S(2)}) copy-start(bf16[2,16,32,768]{3,2,1,0:T(8,128)(2,1)} %param.12) | copy-start | bytes 4718596
  20.5 26.6 %all-to-all-start.1 = ((bf16[32,2,16,768]{3,2,1,0:T(8,128)(2,1)}), bf16[32,2,16,768]{3,2,1,0:T(8,128)(2,1)S(1)}, u32[]{:S(2)}, u32[]{:S(2)}) async-start(bf16[32,2,16,768]{3,2,1,0:T(8,128)(2,1)} %dispatch.1), calls=%async_computation.1 | async-start | bytes 3145728 | tf_op jit(solution)/shard_map/all_to_all | solution.py:567
  51.8 0.8 copy-start.3
  52.6 26.6 %all-to-all-start.2 = ((bf16[32,192,128]{2,1,0:T(8,128)(2,1)}), bf16[32,192,128]{2,1,0:T(8,128)(2,1)S(1)}, u32[]{:S(2)}, u32[]{:S(2)}) async-start(bf16[32,192,128]{2,1,0:T(8,128)(2,1)} %get-tuple-element.17), calls=%async_computation.2 | async-start | bytes 3145728 | tf_op jit(solution)/shard_map/all_to_all | solution.py:591
  57.7 64.6 %collective-permute-start.6 = (bf16[1536,384]{1,0:T(8,128)(2,1)S(1)}, bf16[1536,384]{1,0:T(8,128)(2,1)}, u32[]{:S(2)}, u32[]{:S(2)}) collective-permute-start(bf16[1536,384]{1,0:T(8,128)(2,1)S(1)} %pad_maximum_fusion), channel_id=1, source_target_pairs={{0,96},{32,0},{64,32},{96,64},{1,97},{33,1},{65,33},{97,65},{2,98}... | collective-permute-start | bytes 3538952 | tf_op jit(solution)/shard_map/ppermute | solution.py:373
  60.8 61.5 %collective-permute-start.5 = (bf16[1536,384]{1,0:T(8,128)(2,1)S(1)}, bf16[1536,384]{1,0:T(8,128)(2,1)}, u32[]{:S(2)}, u32[]{:S(2)}) collective-permute-start(bf16[1536,384]{1,0:T(8,128)(2,1)S(1)} %pad_maximum_fusion), channel_id=1, source_target_pairs={{0,64},{32,96},{64,0},{96,32},{1,65},{33,97},{65,1},{97,33},{2,66}... | collective-permute-start | bytes 3538952 | tf_op jit(solution)/shard_map/ppermute | solution.py:373
  61.4 60.9 %collective-permute-start.4 = (bf16[1536,384]{1,0:T(8,128)(2,1)S(1)}, bf16[1536,384]{1,0:T(8,128)(2,1)}, u32[]{:S(2)}, u32[]{:S(2)}) collective-permute-start(bf16[1536,384]{1,0:T(8,128)(2,1)S(1)} %pad_maximum_fusion), channel_id=1, source_target_pairs={{0,32},{32,64},{64,96},{96,0},{1,33},{33,65},{65,97},{97,1},{2,34}... | collective-permute-start | bytes 3538952 | tf_op jit(solution)/shard_map/ppermute | solution.py:373
  122.3 28.2 %collective-permute-start.7 = (bf16[1536,384]{1,0:T(8,128)(2,1)}, bf16[1536,384]{1,0:T(8,128)(2,1)}, u32[]{:S(2)}, u32[]{:S(2)}) collective-permute-start(bf16[1536,384]{1,0:T(8,128)(2,1)} %collective-permute-done.4.rest_3_), channel_id=1, source_target_pairs={{0,4},{4,0},{8,12},{12,8},{16,20},{20,16},{24,28},{28,24},{1,5},{5... | collective-permute-start | bytes 3538952 | tf_op jit(solution)/shard_map/ppermute | solution.py:379
  122.4 28.1 %collective-permute-start.8 = (bf16[1536,384]{1,0:T(8,128)(2,1)}, bf16[1536,384]{1,0:T(8,128)(2,1)}, u32[]{:S(2)}, u32[]{:S(2)}) collective-permute-start(bf16[1536,384]{1,0:T(8,128)(2,1)} %collective-permute-done.5.rest_4_), channel_id=1, source_target_pairs={{0,4},{4,0},{8,12},{12,8},{16,20},{20,16},{24,28},{28,24},{1,5},{5... | collective-permute-start | bytes 3538952 | tf_op jit(solution)/shard_map/ppermute | solution.py:379
  122.9 27.6 %collective-permute-start.9 = (bf16[1536,384]{1,0:T(8,128)(2,1)}, bf16[1536,384]{1,0:T(8,128)(2,1)}, u32[]{:S(2)}, u32[]{:S(2)}) collective-permute-start(bf16[1536,384]{1,0:T(8,128)(2,1)} %collective-permute-done.6.rest_5_), channel_id=1, source_target_pairs={{0,4},{4,0},{8,12},{12,8},{16,20},{20,16},{24,28},{28,24},{1,5},{5... | collective-permute-start | bytes 3538952 | tf_op jit(solution)/shard_map/ppermute | solution.py:379
  123.1 27.4 %all-to-all-start.3 = ((bf16[32,64,128]{2,1,0:T(8,128)(2,1)}), bf16[32,64,128]{2,1,0:T(8,128)(2,1)S(1)}, u32[]{:S(2)}, u32[]{:S(2)}) async-start(bf16[32,64,128]{2,1,0:T(8,128)(2,1)} %attention.1), calls=%async_computation.3 | async-start | bytes 1048576 | tf_op jit(solution)/shard_map/all_to_all | solution.py:595
  128.2 6.8 %collective-permute-start = (s32[2,2,32]{2,1,0:T(2,128)S(1)}, s32[2,2,32]{2,1,0:T(2,128)S(1)}, u32[]{:S(2)}, u32[]{:S(2)}) collective-permute-start(s32[2,2,32]{2,1,0:T(2,128)S(1)} %get-tuple-element.29), channel_id=1, source_target_pairs={{0,4},{4,8},{8,12},{12,16},{16,20},{20,24},{24,28},{1,5},{5,9},{9,... | collective-permute-start | bytes 1544 | tf_op jit(solution)/shard_map/ppermute | solution.py:28
  130.2 4.8 %collective-permute-start.1 = (s32[2,2,32]{2,1,0:T(2,128)S(1)}, s32[2,2,32]{2,1,0:T(2,128)S(1)}, u32[]{:S(2)}, u32[]{:S(2)}) collective-permute-start(s32[2,2,32]{2,1,0:T(2,128)S(1)} %get-tuple-element.30), channel_id=1, source_target_pairs={{4,0},{8,4},{12,8},{16,12},{20,16},{24,20},{28,24},{5,1},{9,5},{13... | collective-permute-start | bytes 1544 | tf_op jit(solution)/shard_map/ppermute | solution.py:30
  135.1 5.0 %collective-permute-start.2 = (s32[2,20,2]{2,1,0:T(8,128)S(1)}, s32[2,20,2]{2,1,0:T(8,128)S(1)}, u32[]{:S(2)}, u32[]{:S(2)}) collective-permute-start(s32[2,20,2]{2,1,0:T(8,128)S(1)} %get-tuple-element.27), channel_id=1, source_target_pairs={{0,1},{1,2},{2,3},{4,5},{5,6},{6,7},{8,9},{9,10},{10,11},{12,13},{... | collective-permute-start | bytes 968 | tf_op jit(solution)/shard_map/ppermute | solution.py:28
  138.5 5.7 %collective-permute-start.3 = (s32[2,20,2]{2,1,0:T(8,128)S(1)}, s32[2,20,2]{2,1,0:T(8,128)S(1)}, u32[]{:S(2)}, u32[]{:S(2)}) collective-permute-start(s32[2,20,2]{2,1,0:T(8,128)S(1)} %get-tuple-element.28), channel_id=1, source_target_pairs={{1,0},{2,1},{3,2},{5,4},{6,5},{7,6},{9,8},{10,9},{11,10},{13,12},{... | collective-permute-start | bytes 968 | tf_op jit(solution)/shard_map/ppermute | solution.py:30
  150.5 1.0 copy-start.4
  160.9 7.3 %copy-start.7 = (bf16[768]{0:T(1024)(128)(2,1)S(1)}, bf16[768]{0:T(1024)(128)(2,1)}, u32[]{:S(2)}) copy-start(bf16[768]{0:T(1024)(128)(2,1)} %param.14) | copy-start | bytes 4612
  160.9 22.9 %copy-start.1 = (bf16[768,256]{1,0:T(8,128)(2,1)S(1)}, bf16[768,256]{1,0:T(8,128)(2,1)}, u32[]{:S(2)}) copy-start(bf16[768,256]{1,0:T(8,128)(2,1)} %dec_ref.1) | copy-start | bytes 1179652
  160.9 22.9 %all-to-all-start.4 = ((bf16[32,2,32,256]{3,2,1,0:T(8,128)(2,1)}), bf16[32,2,32,256]{3,2,1,0:T(8,128)(2,1)S(1)}, u32[]{:S(2)}, u32[]{:S(2)}) async-start(bf16[32,2,32,256]{3,2,1,0:T(8,128)(2,1)} %feed_forward.1), calls=%async_computation.4 | async-start | bytes 2097152 | tf_op jit(solution)/shard_map/all_to_all | solution.py:607
  183.8 1.7 copy-start.6

commit v4 on v3

--- a/solution.py
+++ b/solution.py
@@ -17,40 +17,12 @@
 SAFE = 96.0
 
 
-def extended_2(cells, sides, width):
-    for axis, dim in sides:
-        count = lax.axis_size(axis)
-        ends = count - 1
-        head = lax.slice_in_dim(cells, 0, width, axis=dim)
-        tail = lax.slice_in_dim(cells, cells.shape[dim] - width, cells.shape[dim], axis=dim)
-        cells = jnp.concatenate(
-            [
-                lax.ppermute(tail, axis, [(i, (i + 1) % count) for i in range(ends)]),
-                cells,
-                lax.ppermute(head, axis, [((i + 1) % count, i) for i in range(ends)]),
-            ],
-            axis=dim,
-        )
-    return cells
-
-
 def ring(height, width):
-    low, high = slice(0, REACH), slice(-REACH, None)
-    mid = slice(REACH, -REACH)
+    bands = (slice(0, REACH), slice(REACH, -REACH), slice(-REACH, None))
     order = np.zeros((height, width), np.int32)
     ends = [0]
-    for rows, cols in (
-        (low, low),
-        (low, mid),
-        (low, high),
-        (mid, high),
-        (high, high),
-        (high, mid),
-        (high, low),
-        (mid, low),
-        (mid, mid),
-    ):
-        block = order[rows, cols]
+    for row, col in CORNERS + ((1, 1),):
+        block = order[bands[row], bands[col]]
         block[...] = ends[-1] + np.arange(block.size, dtype=np.int32).reshape(block.shape)
         ends.append(ends[-1] + block.size)
     return order, np.array(ends, np.int32)
@@ -70,6 +42,8 @@
 )
 REACH = 2
 SLOTS = 32
+SIDES = ((-1, 0), (1, 0), (0, -1), (0, 1), (-1, -1), (-1, 1), (1, -1), (1, 1))
+CORNERS = ((0, 0), (0, 1), (0, 2), (1, 2), (2, 2), (2, 1), (2, 0), (1, 0))
 
 
 def normalize(wide):
@@ -412,15 +386,18 @@
     return found.astype(jnp.int32)
 
 
-def index(me, told, rank, tiles, tile_h, tile_w, wide):
-    samples, peers, marks = told.shape
+def index(me, told, rank, cuts, tiles, tile_h, tile_w, wide):
+    samples, peers, width = told.shape
+    marks = len(cuts)
+    edge = width - marks
     tiles_h, tiles_w = tiles
     cells = rank.shape[1]
     bases = [sum(piece[4] for piece in PIECES[:number]) for number in range(len(PIECES))]
 
     def kernel(me_ref, told_ref, rank_ref, back_ref, slot_ref):
         me = me_ref[0]
-        ahead = told_ref[0].astype(jnp.float32)
+        ahead = told_ref[0][:, :marks].astype(jnp.float32)
+        bits = told_ref[0][:, marks:].astype(jnp.float32)
         tile = lax.broadcasted_iota(jnp.int32, (peers, 1), 0)
         other = lax.broadcasted_iota(jnp.int32, (1, peers), 1)
         earlier = jnp.where(other < tile, 1.0, 0.0)
@@ -475,7 +452,45 @@
         for number in range(1, len(bases)):
             base = jnp.where(which == number, bases[number], base)
         mine = jnp.sum(jnp.where(tile == me, begins, 0.0), 0, keepdims=True)
-        rank = rank_ref[0] - 1
+
+        one = lax.broadcasted_iota(jnp.int32, (edge, 1), 0)
+        two = lax.broadcasted_iota(jnp.int32, (1, edge), 1)
+        ranks = dot(bits.astype(jnp.bfloat16), jnp.where(one < two, 1.0, 0.0).astype(jnp.bfloat16))
+        ranks = jnp.where(bits > 0.5, ranks + starts[:, :1] + 1.0, 0.0)
+        number = lax.broadcasted_iota(jnp.int32, (128, 1), 0)
+        there = jnp.full((128, 1), -1, jnp.int32)
+        for at, (down, right) in enumerate(SIDES):
+            there = jnp.where(number == at, me + down * tiles_w + right, there)
+        chosen = jnp.where(there == other, 1.0, 0.0)
+        table = jnp.dot(
+            chosen, ranks, precision=lax.Precision.HIGHEST, preferred_element_type=jnp.float32
+        )
+        i, j = (row - REACH) % tile_h, (col - REACH) % tile_w
+        down = jnp.where(row < REACH, -1, jnp.where(row >= REACH + tile_h, 1, 0))
+        right = jnp.where(side[0], -1, jnp.where(side[1], 1, 0))
+        place = jnp.zeros(cell.shape, jnp.int32)
+        for at, (top, left) in enumerate(CORNERS):
+            rows = ((i < REACH), (i >= REACH) & (i < tile_h - REACH), (i >= tile_h - REACH))[top]
+            cols = ((j < REACH), (j >= REACH) & (j < tile_w - REACH), (j >= tile_w - REACH))[left]
+            first_i = (0, REACH, tile_h - REACH)[top]
+            first_j = (0, REACH, tile_w - REACH)[left]
+            span = tile_w - 2 * REACH if left == 1 else REACH
+            found = int(cuts[at]) + (i - first_i) * span + (j - first_j)
+            place = jnp.where(rows & cols, found, place)
+        spot = jnp.where(place == two, 1.0, 0.0)
+        border = lax.dot_general(
+            spot,
+            table,
+            (((1,), (1,)), ((), ())),
+            precision=lax.Precision.HIGHEST,
+            preferred_element_type=jnp.float32,
+        )
+        which_side = jnp.full(cell.shape, -1, jnp.int32)
+        for at, (one_down, one_right) in enumerate(SIDES):
+            which_side = jnp.where((down == one_down) & (right == one_right), at, which_side)
+        own = jnp.sum(jnp.where(tile == me, starts[:, :1], 0.0), 0, keepdims=True).astype(jnp.int32)
+        rank = jnp.where(rank_ref[0] > 0, rank_ref[0] + own, 0)
+        rank = jnp.where(which_side >= 0, pick(which_side, border), rank) - 1
         peer = rank & (peers - 1)
         nth = rank // peers - (pick(which, mine) - peer + peers - 1) // peers
         row = row + (me // tiles_w) * tile_h - REACH
@@ -490,7 +505,7 @@
             num_scalar_prefetch=1,
             grid=(samples,),
             in_specs=[
-                pl.BlockSpec((1, peers, marks), lambda s, _: (s, 0, 0)),
+                pl.BlockSpec((1, peers, width), lambda s, _: (s, 0, 0)),
                 pl.BlockSpec((1, cells, 1), lambda s, _: (s, 0, 0)),
             ],
             out_specs=[
@@ -538,18 +553,19 @@
     flat_mask = keep_mask.reshape(samples, tile)
     order, ends = ring(tile_h, tile_w)
     order = jnp.asarray(order.reshape(-1))
-    marks = len(ends)
-    earlier = order[:, None] < jnp.asarray(ends)[None, :]
-    counts = dot(flat_mask.astype(jnp.bfloat16), earlier.astype(jnp.bfloat16)).astype(jnp.int32)
-    told = lax.all_to_all(
-        jnp.broadcast_to(counts.reshape(1, 1, samples * marks), (peers, 1, samples * marks)),
+    marks, edge = len(ends), int(ends[-2])
+    sums = order[:, None] < jnp.asarray(ends)[None, :]
+    bits = order[:, None] == jnp.arange(edge, dtype=jnp.int32)[None, :]
+    sums = jnp.concatenate([sums, bits], 1).astype(jnp.bfloat16)
+    counts = dot(flat_mask.astype(jnp.bfloat16), sums).astype(jnp.int32)
+    told_all = lax.all_to_all(
+        jnp.broadcast_to(counts.reshape(1, 1, counts.size), (peers, 1, counts.size)),
         PLANE,
         split_axis=0,
         concat_axis=0,
         tiled=True,
-    ).reshape(peers, samples, marks)
-    segments = told
-    told = told[:, :, -1]
+    ).reshape(peers, samples, marks + edge)
+    told = told_all[:, :, marks - 1]
     before = order[:, None] < order[None, :]
     running = dot(flat_mask.astype(jnp.bfloat16), before.astype(jnp.bfloat16)).astype(jnp.int32)
     cell_rank = jnp.where(flat_mask == 1, running, -1)
@@ -571,16 +587,15 @@
     token = (starts.T[:, :, None] + local - me) // peers
     token = jnp.where(local < told.T[:, :, None], token, -1)
 
-    rank = jnp.where(flat_mask == 1, my_start[:, None] + running + 1, 0)
-    rank = rank.reshape(samples, tile_h, tile_w)
-    rank = extended_2(rank, (("row", 1), ("col", 2)), REACH)
     tiles = lax.axis_size("row"), lax.axis_size("col")
     high, wide = tile_h + 2 * REACH, -(-(tile_w + 2 * REACH) // 8) * 8
-    rank = jnp.pad(rank, ((0, 0), (0, 0), (0, wide - rank.shape[2])))
+    rank = (cell_rank + 1).reshape(samples, tile_h, tile_w)
+    rank = jnp.pad(rank, ((0, 0), (REACH, REACH), (REACH, wide - tile_w - REACH)))
     back, cell_slot = index(
         me,
-        segments.transpose(1, 0, 2),
+        told_all.transpose(1, 0, 2),
         rank.reshape(samples, high * wide, 1),
+        ends,
         tiles,
         tile_h,
         tile_w,

time: 197 us -> 188 us (0.954)
  starting transfers between devices: 46.8 us -> 36.7 us
  waiting for transfers between devices: 62.5 us -> 56 us
  Pallas kernels: 67.4 us -> 72.6 us
    ppermute x4 -> x0, starting transfers between devices: 10.4 us -> none  [the longest x2 5.39 us: extended_2(): lax.ppermute(tail, axis, [(i, (i + 1) % count) for i in range(ends)])]
    pallas_call x1, Pallas kernels: 5.89 us -> 11.3 us  [index(): pl.pallas_call(kernel, grid_spec=pltpu.PrefetchScalarGridSpec(num_scalar_...]
    ppermute x4 -> x0, waiting for transfers between devices: 5.39 us -> none  [the longest x2 4.16 us: extended_2(): lax.ppermute(head, axis, [((i + 1) % count, i) for i in range(ends)])]
  transfers between devices with their start and end apart: 15 -> 11, of which waited for: 7 -> 4; matrix products, arithmetic and copies ran while one was open for 2% -> 2% of each run, Pallas kernels for 25% -> 29%
where the time goes in v4:
time: 188 us; the launch traced here: 185 us
  Pallas kernels  72.6 us (39%)
  waiting for transfers between devices  56 us (30%)
  starting transfers between devices  36.7 us (20%)
  matrix products  10.4 us (6%)
  local copies, waits for them, and re-layouts  5.22 us (3%)
  other arithmetic  3.8 us (2%)
    pallas_call x1, Pallas kernels, attention(): pl.pallas_call(kernel, grid=(peers // step,), in_specs=[pl.BlockSpec(pack...  43 us
    all_to_all x1, waiting for transfers between devices, shards(): lax.all_to_all(outgoing, PLANE, split_axis=0, concat_axis=0, tiled=True)  20.8 us
    all_to_all x1, waiting for transfers between devices, shards(): lax.all_to_all(packed, PLANE, split_axis=0, concat_axis=0, tiled=True)  16.8 us
    all_to_all x1, waiting for transfers between devices, shards(): lax.all_to_all(returning, PLANE, split_axis=0, concat_axis=0, tiled=True)  15.5 us
    pallas_call x1, Pallas kernels, index(): pl.pallas_call(kernel, grid_spec=pltpu.PrefetchScalarGridSpec(num_scalar_...  11.3 us
    pallas_call x1, Pallas kernels, feed_forward(): pl.pallas_call(kernel, in_specs=[pl.BlockSpec(memory_space=pltpu.VMEM)] *...  9.35 us
    all_to_all x1, starting transfers between devices, shards(): lax.all_to_all(jnp.broadcast_to(counts.reshape(1, 1, counts.size), (peers...  8.46 us
    all_to_all x1, starting transfers between devices, shards(): lax.all_to_all(returning, PLANE, split_axis=0, concat_axis=0, tiled=True)  7.55 us
  transfers between devices with their start and end apart: 11, of which 4 were waited for; matrix products, arithmetic and copies ran while one was open for 2% of the time, Pallas kernels for 29%

profile of v4, /device:TPU:2, one launch (start us, length us, event | category | flops | bytes accessed | tf_op | source)
XLA Modules:
  0.0 185.3 jit_solution(1668787372608986195)
XLA Ops:
  0.0 0.8 convert_element_type.36
  1.7 0.8 broadcast_compare_fusion
  3.6 8.5 %all-to-all-start = ((s32[32,1,372]{2,1,0:T(1,128)}), s32[32,1,372]{2,1,0:T(1,128)S(1)}, u32[]{:S(2)}, u32[]{:S(2)}) async-start(s32[32,1,372]{2,1,0:T(1,128)} %broadcast_in_dim.78), calls=%async_computation | async-start | bytes 98304 | tf_op jit(solution)/shard_map/all_to_all | solution.py:561
  12.9 1.1 broadcast_add_fusion
  14.0 1.1 constant_dynamic-slice_fusion
  15.4 2.9 %all-to-all-done = s32[32,1,372]{2,1,0:T(1,128)S(1)} async-done(((s32[32,1,372]{2,1,0:T(1,128)}), s32[32,1,372]{2,1,0:T(1,128)S(1)}, u32[]{:S(2)}, u32[]{:S(2)}) %all-to-all-start) | async-done | bytes 47648 | tf_op jit(solution)/shard_map/all_to_all | solution.py:561
  18.9 2.7 %dispatch.1 = bf16[32,2,16,768]{3,2,1,0:T(8,128)(2,1)} custom-call(s32[2]{0:T(128)S(1)} %select_reduce_fusion.1.start_ref, s32[2,1,512]{2,1,0:T(1,128)S(1)} %reshape.257.rank_ref, bf16[2,512,768]{2,1,0:T(8,128)(2,1)S(1)} %bitcast.161), custom_call_target="tpu_custom_call" | custom-call | tf_op jit(solution)/shard_map/dispatch/pallas_call | solution.py:102
  21.6 5.1 %all-to-all-start.1 = ((bf16[32,2,16,768]{3,2,1,0:T(8,128)(2,1)}), bf16[32,2,16,768]{3,2,1,0:T(8,128)(2,1)S(1)}, u32[]{:S(2)}, u32[]{:S(2)}) async-start(bf16[32,2,16,768]{3,2,1,0:T(8,128)(2,1)} %dispatch.1), calls=%async_computation.1 | async-start | bytes 3145728 | tf_op jit(solution)/shard_map/all_to_all | solution.py:583
  27.5 20.8 %all-to-all-done.1.arrived_ref = bf16[32,2,16,768]{3,2,1,0:T(8,128)(2,1)S(1)} async-done(((bf16[32,2,16,768]{3,2,1,0:T(8,128)(2,1)}), bf16[32,2,16,768]{3,2,1,0:T(8,128)(2,1)S(1)}, u32[]{:S(2)}, u32[]{:S(2)}) %all-to-all-start.1) | async-done | bytes 1572896 | tf_op jit(solution)/shard_map/all_to_all | solution.py:583
  48.2 4.6 %project.1 = (bf16[2,128,768]{2,1,0:T(8,128)(2,1)S(1)}, bf16[32,192,128]{2,1,0:T(8,128)(2,1)}) custom-call(s32[2,1,512]{2,1,0:T(1,128)S(1)} %compare_select_fusion.col_ref, bf16[32,2,16,768]{3,2,1,0:T(8,128)(2,1)S(1)} %all-to-all-done.1.arrived_ref, bf16[768,2304]{1,0:T(8,128)(2,1)} %weight_hbm.1), custom_call_target="tpu_custom_call" | custom-call | tf_op jit(solution)/shard_map/project/pallas_call | solution.py:168
  53.6 5.1 %all-to-all-start.2 = ((bf16[32,192,128]{2,1,0:T(8,128)(2,1)}), bf16[32,192,128]{2,1,0:T(8,128)(2,1)S(1)}, u32[]{:S(2)}, u32[]{:S(2)}) async-start(bf16[32,192,128]{2,1,0:T(8,128)(2,1)} %get-tuple-element.17), calls=%async_computation.2 | async-start | bytes 3145728 | tf_op jit(solution)/shard_map/all_to_all | solution.py:606
  58.7 3.1 %collective-permute-start.2 = (bf16[1536,384]{1,0:T(8,128)(2,1)S(1)}, bf16[1536,384]{1,0:T(8,128)(2,1)}, u32[]{:S(2)}, u32[]{:S(2)}) collective-permute-start(bf16[1536,384]{1,0:T(8,128)(2,1)S(1)} %pad_maximum_fusion), channel_id=1, source_target_pairs={{0,96},{32,0},{64,32},{96,64},{1,97},{33,1},{65,33},{97,65},{2,98}... | collective-permute-start | bytes 3538952 | tf_op jit(solution)/shard_map/ppermute | solution.py:347
  62.4 1.0 collective-permute-start
  63.4 16.8 %all-to-all-done.2.packed_ref = bf16[32,192,128]{2,1,0:T(8,128)(2,1)S(1)} async-done(((bf16[32,192,128]{2,1,0:T(8,128)(2,1)}), bf16[32,192,128]{2,1,0:T(8,128)(2,1)S(1)}, u32[]{:S(2)}, u32[]{:S(2)}) %all-to-all-start.2) | async-done | bytes 1572896 | tf_op jit(solution)/shard_map/all_to_all | solution.py:606
  80.2 43.0 %attention.1 = bf16[32,64,128]{2,1,0:T(8,128)(2,1)} custom-call(bf16[32,192,128]{2,1,0:T(8,128)(2,1)S(1)} %all-to-all-done.2.packed_ref), custom_call_target="tpu_custom_call" | custom-call | tf_op jit(solution)/shard_map/attention/pallas_call | solution.py:252
  123.9 5.1 %all-to-all-start.3 = ((bf16[32,64,128]{2,1,0:T(8,128)(2,1)}), bf16[32,64,128]{2,1,0:T(8,128)(2,1)S(1)}, u32[]{:S(2)}, u32[]{:S(2)}) async-start(bf16[32,64,128]{2,1,0:T(8,128)(2,1)} %attention.1), calls=%async_computation.3 | async-start | bytes 1048576 | tf_op jit(solution)/shard_map/all_to_all | solution.py:610
  129.5 11.3 %index.1 = (s32[2,1024,1]{2,1,0:T(8,128)S(1)}, s32[2,800,1]{2,1,0:T(8,128)S(1)}) custom-call(s32[1]{0:T(128)} %bitcast.me_ref, s32[2,32,186]{2,1,0:T(8,128)S(1)} %bitcast.162, s32[2,800,1]{2,1,0:T(8,128)S(1)} %reshape.280.rank_ref), custom_call_target="tpu_custom_call" | custom-call | tf_op jit(solution)/shard_map/index/pallas_call | solution.py:502
  140.9 1.0 copy-done.4
  141.9 9.3 %feed_forward.1 = bf16[32,2,32,256]{3,2,1,0:T(8,128)(2,1)} custom-call(bf16[32,64,128]{2,1,0:T(8,128)(2,1)S(1)} %all-to-all-done.3.mixed_ref, bf16[2,128,768]{2,1,0:T(8,128)(2,1)S(1)} %copy-done.4, s32[2,1024,1]{2,1,0:T(8,128)S(1)} %get-tuple-element.21.col_ref, bf16[768,768]{1,0:T(8,128)(2,1)} %rest_0_.1, bf16[768,768]{1,0:T(8,128)(2,1)} %rest_1_.1, ...), custom_call_target="tpu_custom_call" | custom-call | tf_op jit(solution)/shard_map/feed_forward/pallas_call | solution.py:322
  151.3 7.6 %all-to-all-start.4 = ((bf16[32,2,32,256]{3,2,1,0:T(8,128)(2,1)}), bf16[32,2,32,256]{3,2,1,0:T(8,128)(2,1)S(1)}, u32[]{:S(2)}, u32[]{:S(2)}) async-start(bf16[32,2,32,256]{3,2,1,0:T(8,128)(2,1)} %feed_forward.1), calls=%async_computation.4 | async-start | bytes 2097152 | tf_op jit(solution)/shard_map/all_to_all | solution.py:622
  159.0 15.5 %all-to-all-done.4.home_ref = bf16[32,2,32,256]{3,2,1,0:T(8,128)(2,1)S(1)} async-done(((bf16[32,2,32,256]{3,2,1,0:T(8,128)(2,1)}), bf16[32,2,32,256]{3,2,1,0:T(8,128)(2,1)S(1)}, u32[]{:S(2)}, u32[]{:S(2)}) %all-to-all-start.4) | async-done | bytes 1048608 | tf_op jit(solution)/shard_map/all_to_all | solution.py:622
  174.5 1.7 place.1
  179.2 1.3 select_convert_fusion
  183.0 2.3 %convolution_convert_fusion = bf16[2,16,32,128]{3,2,1,0:T(8,128)(2,1)} fusion(f32[2,16,32,256]{3,2,1,0:T(8,128)S(1)} %convolution_add_fusion.1, bf16[2,18,34,256]{3,2,1,0:T(8,128)(2,1)S(1)} %select_convert_fusion, bf16[2,9,256,256]{3,2,1,0:T(8,128)(2,1)} %param.20, bf16[256,128]{1,0:T(8,128)(2,1)S(1)} %copy-done), kind=kOutput, calls=%fused_computation.9 | convolution fusion | flops 203554816 | bytes 2555904 | tf_op jit(solution)/shard_map/dot_general | solution.py:61
  (79 shorter events, 12.3 us)
Async XLA Ops:
  0.0 183.0 %copy-start = (bf16[256,128]{1,0:T(8,128)(2,1)S(1)}, bf16[256,128]{1,0:T(8,128)(2,1)}, u32[]{:S(2)}) copy-start(bf16[256,128]{1,0:T(8,128)(2,1)} %param.21) | copy-start | bytes 196612
  0.0 15.2 %copy-start.5 = (bf16[768,768]{1,0:T(8,128)(2,1)S(1)}, bf16[768,768]{1,0:T(8,128)(2,1)}, u32[]{:S(2)}) copy-start(bf16[768,768]{1,0:T(8,128)(2,1)} %rest_2_.1) | copy-start | bytes 3538948
  3.6 14.7 %all-to-all-start = ((s32[32,1,372]{2,1,0:T(1,128)}), s32[32,1,372]{2,1,0:T(1,128)S(1)}, u32[]{:S(2)}, u32[]{:S(2)}) async-start(s32[32,1,372]{2,1,0:T(1,128)} %broadcast_in_dim.78), calls=%async_computation | async-start | bytes 98304 | tf_op jit(solution)/shard_map/all_to_all | solution.py:561
  15.3 3.6 %copy-start.2 = (bf16[2,16,32,768]{3,2,1,0:T(8,128)(2,1)S(1)}, bf16[2,16,32,768]{3,2,1,0:T(8,128)(2,1)}, u32[]{:S(2)}) copy-start(bf16[2,16,32,768]{3,2,1,0:T(8,128)(2,1)} %param.12) | copy-start | bytes 4718596
  21.6 26.6 %all-to-all-start.1 = ((bf16[32,2,16,768]{3,2,1,0:T(8,128)(2,1)}), bf16[32,2,16,768]{3,2,1,0:T(8,128)(2,1)S(1)}, u32[]{:S(2)}, u32[]{:S(2)}) async-start(bf16[32,2,16,768]{3,2,1,0:T(8,128)(2,1)} %dispatch.1), calls=%async_computation.1 | async-start | bytes 3145728 | tf_op jit(solution)/shard_map/all_to_all | solution.py:583
  52.9 0.8 copy-start.3
  53.6 26.6 %all-to-all-start.2 = ((bf16[32,192,128]{2,1,0:T(8,128)(2,1)}), bf16[32,192,128]{2,1,0:T(8,128)(2,1)S(1)}, u32[]{:S(2)}, u32[]{:S(2)}) async-start(bf16[32,192,128]{2,1,0:T(8,128)(2,1)} %get-tuple-element.17), calls=%async_computation.2 | async-start | bytes 3145728 | tf_op jit(solution)/shard_map/all_to_all | solution.py:606
  58.7 64.5 %collective-permute-start.2 = (bf16[1536,384]{1,0:T(8,128)(2,1)S(1)}, bf16[1536,384]{1,0:T(8,128)(2,1)}, u32[]{:S(2)}, u32[]{:S(2)}) collective-permute-start(bf16[1536,384]{1,0:T(8,128)(2,1)S(1)} %pad_maximum_fusion), channel_id=1, source_target_pairs={{0,96},{32,0},{64,32},{96,64},{1,97},{33,1},{65,33},{97,65},{2,98}... | collective-permute-start | bytes 3538952 | tf_op jit(solution)/shard_map/ppermute | solution.py:347
  61.8 61.4 %collective-permute-start.1 = (bf16[1536,384]{1,0:T(8,128)(2,1)S(1)}, bf16[1536,384]{1,0:T(8,128)(2,1)}, u32[]{:S(2)}, u32[]{:S(2)}) collective-permute-start(bf16[1536,384]{1,0:T(8,128)(2,1)S(1)} %pad_maximum_fusion), channel_id=1, source_target_pairs={{0,64},{32,96},{64,0},{96,32},{1,65},{33,97},{65,1},{97,33},{2,66}... | collective-permute-start | bytes 3538952 | tf_op jit(solution)/shard_map/ppermute | solution.py:347
  62.4 60.8 %collective-permute-start = (bf16[1536,384]{1,0:T(8,128)(2,1)S(1)}, bf16[1536,384]{1,0:T(8,128)(2,1)}, u32[]{:S(2)}, u32[]{:S(2)}) collective-permute-start(bf16[1536,384]{1,0:T(8,128)(2,1)S(1)} %pad_maximum_fusion), channel_id=1, source_target_pairs={{0,32},{32,64},{64,96},{96,0},{1,33},{33,65},{65,97},{97,1},{2,34}... | collective-permute-start | bytes 3538952 | tf_op jit(solution)/shard_map/ppermute | solution.py:347
  123.2 17.6 %collective-permute-start.3 = (bf16[1536,384]{1,0:T(8,128)(2,1)}, bf16[1536,384]{1,0:T(8,128)(2,1)}, u32[]{:S(2)}, u32[]{:S(2)}) collective-permute-start(bf16[1536,384]{1,0:T(8,128)(2,1)} %collective-permute-done.rest_3_), channel_id=1, source_target_pairs={{0,4},{4,0},{8,12},{12,8},{16,20},{20,16},{24,28},{28,24},{1,5},{5... | collective-permute-start | bytes 3538952 | tf_op jit(solution)/shard_map/ppermute | solution.py:353
  123.3 17.5 %collective-permute-start.4 = (bf16[1536,384]{1,0:T(8,128)(2,1)}, bf16[1536,384]{1,0:T(8,128)(2,1)}, u32[]{:S(2)}, u32[]{:S(2)}) collective-permute-start(bf16[1536,384]{1,0:T(8,128)(2,1)} %collective-permute-done.1.rest_4_), channel_id=1, source_target_pairs={{0,4},{4,0},{8,12},{12,8},{16,20},{20,16},{24,28},{28,24},{1,5},{5... | collective-permute-start | bytes 3538952 | tf_op jit(solution)/shard_map/ppermute | solution.py:353
  123.8 17.0 %collective-permute-start.5 = (bf16[1536,384]{1,0:T(8,128)(2,1)}, bf16[1536,384]{1,0:T(8,128)(2,1)}, u32[]{:S(2)}, u32[]{:S(2)}) collective-permute-start(bf16[1536,384]{1,0:T(8,128)(2,1)} %collective-permute-done.2.rest_5_), channel_id=1, source_target_pairs={{0,4},{4,0},{8,12},{12,8},{16,20},{20,16},{24,28},{28,24},{1,5},{5... | collective-permute-start | bytes 3538952 | tf_op jit(solution)/shard_map/ppermute | solution.py:353
  123.9 16.9 %all-to-all-start.3 = ((bf16[32,64,128]{2,1,0:T(8,128)(2,1)}), bf16[32,64,128]{2,1,0:T(8,128)(2,1)S(1)}, u32[]{:S(2)}, u32[]{:S(2)}) async-start(bf16[32,64,128]{2,1,0:T(8,128)(2,1)} %attention.1), calls=%async_computation.3 | async-start | bytes 1048576 | tf_op jit(solution)/shard_map/all_to_all | solution.py:610
  140.9 1.0 copy-start.4
  151.2 7.6 %copy-start.7 = (bf16[768]{0:T(1024)(128)(2,1)S(1)}, bf16[768]{0:T(1024)(128)(2,1)}, u32[]{:S(2)}) copy-start(bf16[768]{0:T(1024)(128)(2,1)} %param.14) | copy-start | bytes 4612
  151.3 23.3 %copy-start.1 = (bf16[768,256]{1,0:T(8,128)(2,1)S(1)}, bf16[768,256]{1,0:T(8,128)(2,1)}, u32[]{:S(2)}) copy-start(bf16[768,256]{1,0:T(8,128)(2,1)} %dec_ref.1) | copy-start | bytes 1179652
  151.3 23.2 %all-to-all-start.4 = ((bf16[32,2,32,256]{3,2,1,0:T(8,128)(2,1)}), bf16[32,2,32,256]{3,2,1,0:T(8,128)(2,1)S(1)}, u32[]{:S(2)}, u32[]{:S(2)}) async-start(bf16[32,2,32,256]{3,2,1,0:T(8,128)(2,1)} %feed_forward.1), calls=%async_computation.4 | async-start | bytes 2097152 | tf_op jit(solution)/shard_map/all_to_all | solution.py:622
  174.5 1.7 copy-start.6

commit v5 on v4

--- a/solution.py
+++ b/solution.py
@@ -66,16 +66,17 @@
 
 
 def convolve(extended, taps, out_h, out_w):
+    beside = jnp.concatenate([extended[:, :, second : second + out_w] for second in range(3)], -1)
+    taps = taps.reshape(3, beside.shape[-1], taps.shape[-1])
     total = None
     for first in range(3):
-        for second in range(3):
-            term = jnp.einsum(
-                "shwc,cd->shwd",
-                extended[:, first : first + out_h, second : second + out_w],
-                taps[first * 3 + second],
-                preferred_element_type=jnp.float32,
-            )
-            total = term if total is None else total + term
+        term = jnp.einsum(
+            "shwc,cd->shwd",
+            beside[:, first : first + out_h],
+            taps[first],
+            preferred_element_type=jnp.float32,
+        )
+        total = term if total is None else total + term
     return total
 
 
@@ -124,7 +125,7 @@
     places = peers // samples
     half = kept // 2
 
-    def kernel(col_ref, arrived_ref, weight_hbm, x_ref, out_ref, weight, sems):
+    def kernel(col_ref, arrived_ref, weight_hbm, x_hbm, out_ref, weight, x_ref, sems):
         copies = []
         for third in range(3):
             cols = pl.ds(third * width, width)
@@ -138,6 +139,8 @@
             chosen = one_hot(token, col_ref[sample])
             rows.append(dot(chosen, arrived_ref[:, sample].reshape(tile, width)))
             x_ref[sample] = rows[-1].astype(jnp.bfloat16)
+        keep = pltpu.make_async_copy(x_ref, x_hbm, sems.at[3])
+        keep.start()
         normed = normalize(jnp.concatenate(rows, 0))
         qkv = []
         for third in range(3):
@@ -164,18 +167,20 @@
                 out_ref[to + 1, kept:] = second_v.astype(jnp.bfloat16)
             for place in range(2 * groups, places):
                 out_ref[sample * places + place] = jnp.zeros((kept + half, lanes), jnp.bfloat16)
+        keep.wait()
 
     return pl.pallas_call(
         kernel,
         in_specs=[pl.BlockSpec(memory_space=pltpu.VMEM)] * 2 + [pl.BlockSpec(memory_space=pltpu.HBM)],
-        out_specs=[pl.BlockSpec(memory_space=pltpu.VMEM)] * 2,
+        out_specs=[pl.BlockSpec(memory_space=pltpu.HBM), pl.BlockSpec(memory_space=pltpu.VMEM)],
         out_shape=[
-            jax.ShapeDtypeStruct((samples, kept, width), jnp.bfloat16),
+            pltpu.HBM((samples, kept, width), jnp.bfloat16),
             jax.ShapeDtypeStruct((peers, kept + half, lanes), jnp.bfloat16),
         ],
         scratch_shapes=[
             pltpu.VMEM((3, width, width), jnp.bfloat16),
-            pltpu.SemaphoreType.DMA((3,)),
+            pltpu.VMEM((samples, kept, width), jnp.bfloat16),
+            pltpu.SemaphoreType.DMA((4,)),
         ],
         compiler_params=params(20),
         name="project",
@@ -281,11 +286,14 @@
             pltpu.make_async_copy(source, held[at], sems.at[at])
             for at, source in enumerate(sources)
         ]
-        for copy in copies:
+        ahead = 3
+        for copy in copies[:ahead]:
             copy.start()
 
         def ready(at):
             copies[at].wait()
+            if at + ahead < count:
+                copies[at + ahead].start()
             return held[at]
 
         low = lax.broadcasted_iota(jnp.int32, (half, lanes), 1) < HD
@@ -554,9 +562,11 @@
     order, ends = ring(tile_h, tile_w)
     order = jnp.asarray(order.reshape(-1))
     marks, edge = len(ends), int(ends[-2])
-    sums = order[:, None] < jnp.asarray(ends)[None, :]
-    bits = order[:, None] == jnp.arange(edge, dtype=jnp.int32)[None, :]
-    sums = jnp.concatenate([sums, bits], 1).astype(jnp.bfloat16)
+    spots = np.arange(edge, dtype=np.int32)
+    low = jnp.asarray(np.concatenate([np.zeros_like(ends), spots]))
+    high = jnp.asarray(np.concatenate([ends, spots + 1]))
+    sums = (order[:, None] >= low[None, :]) & (order[:, None] < high[None, :])
+    sums = sums.astype(jnp.bfloat16)
     counts = dot(flat_mask.astype(jnp.bfloat16), sums).astype(jnp.int32)
     told_all = lax.all_to_all(
         jnp.broadcast_to(counts.reshape(1, 1, counts.size), (peers, 1, counts.size)),

time: 188 us -> 190 us (1.011)
  waiting for transfers between devices: 56 us -> 49 us
  local copies, waits for them, and re-layouts: 5.22 us -> 10.5 us
  starting transfers between devices: 36.7 us -> 40.1 us
    slice x0 -> x3, local copies, waits for them, and re-layouts: none -> 3.87 us  [the longest x1 2.88 us: convolve(): taps[first]]
    all_to_all x1, waiting for transfers between devices: 2.92 us -> 0.01 us  [shards(): lax.all_to_all(jnp.broadcast_to(counts.reshape(1, 1, counts.size), (peers...]
    all_to_all x1, waiting for transfers between devices: 15.5 us -> 12.7 us  [shards(): lax.all_to_all(returning, PLANE, split_axis=0, concat_axis=0, tiled=True)]
    all_to_all x1, starting transfers between devices: 5.14 us -> 7.37 us  [shards(): lax.all_to_all(outgoing, PLANE, split_axis=0, concat_axis=0, tiled=True)]
    concatenate x1, other arithmetic: 0.12 us -> 2.22 us  [share(): jnp.concatenate([up] + [down[:, i:i + part] for i in range(0, width, part...]
    dot_general x17 -> x5, matrix products: 6.73 us -> 5.74 us  [convolve(): jnp.einsum('shwc,cd->shwd', beside[:, first:first + out_h], taps[first],...]
  transfers between devices with their start and end apart: 11 -> 11, of which waited for: 4 -> 3; matrix products, arithmetic and copies ran while one was open for 2% -> 5% of each run, Pallas kernels for 29% -> 29%
where the time goes in v5:
time: 190 us; the launch traced here: 188 us
  Pallas kernels  72.8 us (38%)
  waiting for transfers between devices  49 us (26%)
  starting transfers between devices  40.1 us (21%)
  matrix products  10.7 us (6%)
  local copies, waits for them, and re-layouts  10.5 us (6%)
  other arithmetic  4.25 us (2%)
    pallas_call x1, Pallas kernels, attention(): pl.pallas_call(kernel, grid=(peers // step,), in_specs=[pl.BlockSpec(pack...  43.1 us
    all_to_all x1, waiting for transfers between devices, shards(): lax.all_to_all(outgoing, PLANE, split_axis=0, concat_axis=0, tiled=True)  20.7 us
    all_to_all x1, waiting for transfers between devices, shards(): lax.all_to_all(packed, PLANE, split_axis=0, concat_axis=0, tiled=True)  15.6 us
    all_to_all x1, waiting for transfers between devices, shards(): lax.all_to_all(returning, PLANE, split_axis=0, concat_axis=0, tiled=True)  12.7 us
    pallas_call x1, Pallas kernels, index(): pl.pallas_call(kernel, grid_spec=pltpu.PrefetchScalarGridSpec(num_scalar_...  11.3 us
    pallas_call x1, Pallas kernels, feed_forward(): pl.pallas_call(kernel, in_specs=[pl.BlockSpec(memory_space=pltpu.VMEM)] *...  9.31 us
    all_to_all x1, starting transfers between devices, shards(): lax.all_to_all(jnp.broadcast_to(counts.reshape(1, 1, counts.size), (peers...  8.47 us
    all_to_all x1, starting transfers between devices, shards(): lax.all_to_all(outgoing, PLANE, split_axis=0, concat_axis=0, tiled=True)  7.37 us
  transfers between devices with their start and end apart: 11, of which 3 were waited for; matrix products, arithmetic and copies ran while one was open for 5% of the time, Pallas kernels for 29%

profile of v5, /device:TPU:2, one launch (start us, length us, event | category | flops | bytes accessed | tf_op | source)
XLA Modules:
  0.0 187.7 jit_solution(6269390598268336727)
XLA Ops:
  2.7 8.5 %all-to-all-start = ((s32[32,1,372]{2,1,0:T(1,128)}), s32[32,1,372]{2,1,0:T(1,128)S(1)}, u32[]{:S(2)}, u32[]{:S(2)}) async-start(s32[32,1,372]{2,1,0:T(1,128)} %broadcast_in_dim.78), calls=%async_computation | async-start | bytes 98304 | tf_op jit(solution)/shard_map/all_to_all | solution.py:571
  12.0 1.1 broadcast_add_fusion
  13.1 1.1 constant_dynamic-slice_fusion
  15.1 2.2 %pad_maximum_fusion.2 = bf16[1536,384]{1,0:T(8,128)(2,1)} fusion(bf16[384,384]{1,0:T(8,128)(2,1)} %get-tuple-element.32, bf16[384,384]{1,0:T(8,128)(2,1)} %get-tuple-element.31, bf16[768,384]{1,0:T(8,128)(2,1)S(1)} %constant_dynamic-slice_fusion), kind=kLoop, calls=%fused_computation.6 | loop fusion | flops 3538944 | bytes 2359296 | tf_op jit(solution)/shard_map/concatenate | solution.py:349
  17.9 2.7 %dispatch.1 = bf16[32,2,16,768]{3,2,1,0:T(8,128)(2,1)} custom-call(s32[2]{0:T(128)S(1)} %select_reduce_fusion.1.start_ref, s32[2,1,512]{2,1,0:T(1,128)S(1)} %reshape.234.rank_ref, bf16[2,512,768]{2,1,0:T(8,128)(2,1)S(1)} %bitcast.63), custom_call_target="tpu_custom_call" | custom-call | tf_op jit(solution)/shard_map/dispatch/pallas_call | solution.py:103
  20.6 7.4 %all-to-all-start.1 = ((bf16[32,2,16,768]{3,2,1,0:T(8,128)(2,1)}), bf16[32,2,16,768]{3,2,1,0:T(8,128)(2,1)S(1)}, u32[]{:S(2)}, u32[]{:S(2)}) async-start(bf16[32,2,16,768]{3,2,1,0:T(8,128)(2,1)} %dispatch.1), calls=%async_computation.1 | async-start | bytes 3145728 | tf_op jit(solution)/shard_map/all_to_all | solution.py:593
  28.8 20.7 %all-to-all-done.1.arrived_ref = bf16[32,2,16,768]{3,2,1,0:T(8,128)(2,1)S(1)} async-done(((bf16[32,2,16,768]{3,2,1,0:T(8,128)(2,1)}), bf16[32,2,16,768]{3,2,1,0:T(8,128)(2,1)S(1)}, u32[]{:S(2)}, u32[]{:S(2)}) %all-to-all-start.1) | async-done | bytes 1572896 | tf_op jit(solution)/shard_map/all_to_all | solution.py:593
  49.5 4.7 %project.1 = (bf16[2,128,768]{2,1,0:T(8,128)(2,1)}, bf16[32,192,128]{2,1,0:T(8,128)(2,1)}) custom-call(s32[2,1,512]{2,1,0:T(1,128)S(1)} %compare_select_fusion.col_ref, bf16[32,2,16,768]{3,2,1,0:T(8,128)(2,1)S(1)} %all-to-all-done.1.arrived_ref, bf16[768,2304]{1,0:T(8,128)(2,1)} %weight_hbm.1), custom_call_target="tpu_custom_call" | custom-call | tf_op jit(solution)/shard_map/project/pallas_call | solution.py:172
  54.2 5.2 %all-to-all-start.2 = ((bf16[32,192,128]{2,1,0:T(8,128)(2,1)}), bf16[32,192,128]{2,1,0:T(8,128)(2,1)S(1)}, u32[]{:S(2)}, u32[]{:S(2)}) async-start(bf16[32,192,128]{2,1,0:T(8,128)(2,1)} %get-tuple-element.17), calls=%async_computation.2 | async-start | bytes 3145728 | tf_op jit(solution)/shard_map/all_to_all | solution.py:616
  59.4 1.6 collective-permute-start
  61.1 2.9 %collective-permute-start.1 = (bf16[1536,384]{1,0:T(8,128)(2,1)S(1)}, bf16[1536,384]{1,0:T(8,128)(2,1)}, u32[]{:S(2)}, u32[]{:S(2)}) collective-permute-start(bf16[1536,384]{1,0:T(8,128)(2,1)S(1)} %copy-done.5), channel_id=1, source_target_pairs={{0,64},{32,96},{64,0},{96,32},{1,65},{33,97},{65,1},{97,33},{2,66}... | collective-permute-start | bytes 3538952 | tf_op jit(solution)/shard_map/ppermute | solution.py:355
  64.0 1.3 collective-permute-start.2
  65.3 15.6 %all-to-all-done.2.packed_ref = bf16[32,192,128]{2,1,0:T(8,128)(2,1)S(1)} async-done(((bf16[32,192,128]{2,1,0:T(8,128)(2,1)}), bf16[32,192,128]{2,1,0:T(8,128)(2,1)S(1)}, u32[]{:S(2)}, u32[]{:S(2)}) %all-to-all-start.2) | async-done | bytes 1572896 | tf_op jit(solution)/shard_map/all_to_all | solution.py:616
  80.9 43.1 %attention.1 = bf16[32,64,128]{2,1,0:T(8,128)(2,1)} custom-call(bf16[32,192,128]{2,1,0:T(8,128)(2,1)S(1)} %all-to-all-done.2.packed_ref), custom_call_target="tpu_custom_call" | custom-call | tf_op jit(solution)/shard_map/attention/pallas_call | solution.py:257
  124.7 5.1 %all-to-all-start.3 = ((bf16[32,64,128]{2,1,0:T(8,128)(2,1)}), bf16[32,64,128]{2,1,0:T(8,128)(2,1)S(1)}, u32[]{:S(2)}, u32[]{:S(2)}) async-start(bf16[32,64,128]{2,1,0:T(8,128)(2,1)} %attention.1), calls=%async_computation.3 | async-start | bytes 1048576 | tf_op jit(solution)/shard_map/all_to_all | solution.py:620
  130.3 11.3 %index.1 = (s32[2,1024,1]{2,1,0:T(8,128)S(1)}, s32[2,800,1]{2,1,0:T(8,128)S(1)}) custom-call(s32[1]{0:T(128)} %bitcast.me_ref, s32[2,32,186]{2,1,0:T(8,128)S(1)} %bitcast.64, s32[2,800,1]{2,1,0:T(8,128)S(1)} %reshape.245.rank_ref), custom_call_target="tpu_custom_call" | custom-call | tf_op jit(solution)/shard_map/index/pallas_call | solution.py:510
  142.7 9.3 %feed_forward.1 = bf16[32,2,32,256]{3,2,1,0:T(8,128)(2,1)} custom-call(bf16[32,64,128]{2,1,0:T(8,128)(2,1)S(1)} %all-to-all-done.3.mixed_ref, bf16[2,128,768]{2,1,0:T(8,128)(2,1)S(1)} %copy-done.3, s32[2,1024,1]{2,1,0:T(8,128)S(1)} %get-tuple-element.21.col_ref, bf16[768,768]{1,0:T(8,128)(2,1)} %rest_0_.1, bf16[768,768]{1,0:T(8,128)(2,1)} %rest_1_.1, ...), custom_call_target="tpu_custom_call" | custom-call | tf_op jit(solution)/shard_map/feed_forward/pallas_call | solution.py:330
  152.0 7.4 %all-to-all-start.4 = ((bf16[32,2,32,256]{3,2,1,0:T(8,128)(2,1)}), bf16[32,2,32,256]{3,2,1,0:T(8,128)(2,1)S(1)}, u32[]{:S(2)}, u32[]{:S(2)}) async-start(bf16[32,2,32,256]{3,2,1,0:T(8,128)(2,1)} %feed_forward.1), calls=%async_computation.4 | async-start | bytes 2097152 | tf_op jit(solution)/shard_map/all_to_all | solution.py:632
  159.5 2.9 %fusion.23 = (bf16[1,3,256,256]{3,2,1,0:T(8,128)(2,1)S(1)}, bf16[1,3,256,256]{3,2,1,0:T(8,128)(2,1)}, bf16[1,3,256,256]{3,2,1,0:T(8,128)(2,1)}, bf16[1,3,256,256...) fusion(bf16[2,9,256,256]{3,2,1,0:T(8,128)(2,1)} %param.21), kind=kLoop, calls=%fused_computation.53 | loop fusion | bytes 4718592 | tf_op jit(solution)/shard_map/slice | solution.py:76
  162.4 12.7 %all-to-all-done.4.home_ref = bf16[32,2,32,256]{3,2,1,0:T(8,128)(2,1)S(1)} async-done(((bf16[32,2,32,256]{3,2,1,0:T(8,128)(2,1)}), bf16[32,2,32,256]{3,2,1,0:T(8,128)(2,1)S(1)}, u32[]{:S(2)}, u32[]{:S(2)}) %all-to-all-start.4) | async-done | bytes 1048608 | tf_op jit(solution)/shard_map/all_to_all | solution.py:632
  175.1 1.7 place.1
  179.7 2.0 %select_convert_fusion = bf16[2,18,34,256]{3,2,1,0:T(8,128)(2,1)S(1)} fusion(f32[2,18,34,256]{3,2,1,0:T(8,128)S(1)} %fusion.20, f32[2,18,34,256]{3,2,1,0:T(8,128)S(1)} %fusion.21, bf16[2,20,40,256]{3,2,1,0:T(8,128)(2,1)S(1)} %bitcast.62, pred[18,34]{1,0:T(8,128)(4,1)S(1)} %broadcast_and_fusion, bf16[768,256,1,1]{1,0,3,2:T(8,128)(2,1)S(1)} %bitcast.68, ...), kind=kOutput, calls=%fused_computation.2 | convolution fusion | flops 490696704 | bytes 6242916 | tf_op jit(solution)/shard_map/shwc,cd->shwd/dot_general | solution.py:73
  183.3 1.6 convolution_add_fusion.1
  184.9 2.9 %convolution_convert_fusion = bf16[2,16,32,128]{3,2,1,0:T(8,128)(2,1)} fusion(f32[2,16,32,256]{3,2,1,0:T(8,128)} %convolution_add_fusion.1, bf16[768,256,1,1]{1,0,3,2:T(8,128)(2,1)S(1)} %bitcast.65, bf16[2,18,34,256]{3,2,1,0:T(8,128)(2,1)S(1)} %select_convert_fusion, bf16[256,128]{1,0:T(8,128)(2,1)S(1)} %copy-done, ...), kind=kOutput, calls=%fused_computation.5 | convolution fusion | flops 477298688 | bytes 4063232 | tf_op jit(solution)/shard_map/dot_general | solution.py:61
  (74 shorter events, 12.4 us)
Async XLA Ops:
  0.0 184.9 %copy-start = (bf16[256,128]{1,0:T(8,128)(2,1)S(1)}, bf16[256,128]{1,0:T(8,128)(2,1)}, u32[]{:S(2)}) copy-start(bf16[256,128]{1,0:T(8,128)(2,1)} %param.22) | copy-start | bytes 196612
  0.0 14.2 %copy-start.4 = (bf16[768,768]{1,0:T(8,128)(2,1)S(1)}, bf16[768,768]{1,0:T(8,128)(2,1)}, u32[]{:S(2)}) copy-start(bf16[768,768]{1,0:T(8,128)(2,1)} %rest_2_.1) | copy-start | bytes 3538948
  2.7 14.7 %all-to-all-start = ((s32[32,1,372]{2,1,0:T(1,128)}), s32[32,1,372]{2,1,0:T(1,128)S(1)}, u32[]{:S(2)}, u32[]{:S(2)}) async-start(s32[32,1,372]{2,1,0:T(1,128)} %broadcast_in_dim.78), calls=%async_computation | async-start | bytes 98304 | tf_op jit(solution)/shard_map/all_to_all | solution.py:571
  14.2 3.7 %copy-start.2 = (bf16[2,16,32,768]{3,2,1,0:T(8,128)(2,1)S(1)}, bf16[2,16,32,768]{3,2,1,0:T(8,128)(2,1)}, u32[]{:S(2)}) copy-start(bf16[2,16,32,768]{3,2,1,0:T(8,128)(2,1)} %param.13) | copy-start | bytes 4718596
  20.6 28.9 %all-to-all-start.1 = ((bf16[32,2,16,768]{3,2,1,0:T(8,128)(2,1)}), bf16[32,2,16,768]{3,2,1,0:T(8,128)(2,1)S(1)}, u32[]{:S(2)}, u32[]{:S(2)}) async-start(bf16[32,2,16,768]{3,2,1,0:T(8,128)(2,1)} %dispatch.1), calls=%async_computation.1 | async-start | bytes 3145728 | tf_op jit(solution)/shard_map/all_to_all | solution.py:593
  54.2 5.3 %copy-start.5 = (bf16[1536,384]{1,0:T(8,128)(2,1)S(1)}, bf16[1536,384]{1,0:T(8,128)(2,1)}, u32[]{:S(2)}) copy-start(bf16[1536,384]{1,0:T(8,128)(2,1)} %pad_maximum_fusion.2) | copy-start | bytes 3538948
  54.2 26.7 %all-to-all-start.2 = ((bf16[32,192,128]{2,1,0:T(8,128)(2,1)}), bf16[32,192,128]{2,1,0:T(8,128)(2,1)S(1)}, u32[]{:S(2)}, u32[]{:S(2)}) async-start(bf16[32,192,128]{2,1,0:T(8,128)(2,1)} %get-tuple-element.17), calls=%async_computation.2 | async-start | bytes 3145728 | tf_op jit(solution)/shard_map/all_to_all | solution.py:616
  59.4 64.6 %collective-permute-start = (bf16[1536,384]{1,0:T(8,128)(2,1)S(1)}, bf16[1536,384]{1,0:T(8,128)(2,1)}, u32[]{:S(2)}, u32[]{:S(2)}) collective-permute-start(bf16[1536,384]{1,0:T(8,128)(2,1)S(1)} %copy-done.5), channel_id=1, source_target_pairs={{0,32},{32,64},{64,96},{96,0},{1,33},{33,65},{65,97},{97,1},{2,34}... | collective-permute-start | bytes 3538952 | tf_op jit(solution)/shard_map/ppermute | solution.py:355
  61.1 63.0 %collective-permute-start.1 = (bf16[1536,384]{1,0:T(8,128)(2,1)S(1)}, bf16[1536,384]{1,0:T(8,128)(2,1)}, u32[]{:S(2)}, u32[]{:S(2)}) collective-permute-start(bf16[1536,384]{1,0:T(8,128)(2,1)S(1)} %copy-done.5), channel_id=1, source_target_pairs={{0,64},{32,96},{64,0},{96,32},{1,65},{33,97},{65,1},{97,33},{2,66}... | collective-permute-start | bytes 3538952 | tf_op jit(solution)/shard_map/ppermute | solution.py:355
  64.0 60.1 %collective-permute-start.2 = (bf16[1536,384]{1,0:T(8,128)(2,1)S(1)}, bf16[1536,384]{1,0:T(8,128)(2,1)}, u32[]{:S(2)}, u32[]{:S(2)}) collective-permute-start(bf16[1536,384]{1,0:T(8,128)(2,1)S(1)} %copy-done.5), channel_id=1, source_target_pairs={{0,96},{32,0},{64,32},{96,64},{1,97},{33,1},{65,33},{97,65},{2,98}... | collective-permute-start | bytes 3538952 | tf_op jit(solution)/shard_map/ppermute | solution.py:355
  124.1 17.6 %collective-permute-start.3 = (bf16[1536,384]{1,0:T(8,128)(2,1)}, bf16[1536,384]{1,0:T(8,128)(2,1)}, u32[]{:S(2)}, u32[]{:S(2)}) collective-permute-start(bf16[1536,384]{1,0:T(8,128)(2,1)} %collective-permute-done.rest_3_), channel_id=1, source_target_pairs={{0,4},{4,0},{8,12},{12,8},{16,20},{20,16},{24,28},{28,24},{1,5},{5... | collective-permute-start | bytes 3538952 | tf_op jit(solution)/shard_map/ppermute | solution.py:361
  124.1 17.5 %collective-permute-start.4 = (bf16[1536,384]{1,0:T(8,128)(2,1)}, bf16[1536,384]{1,0:T(8,128)(2,1)}, u32[]{:S(2)}, u32[]{:S(2)}) collective-permute-start(bf16[1536,384]{1,0:T(8,128)(2,1)} %collective-permute-done.1.rest_4_), channel_id=1, source_target_pairs={{0,4},{4,0},{8,12},{12,8},{16,20},{20,16},{24,28},{28,24},{1,5},{5... | collective-permute-start | bytes 3538952 | tf_op jit(solution)/shard_map/ppermute | solution.py:361
  124.6 17.0 %collective-permute-start.5 = (bf16[1536,384]{1,0:T(8,128)(2,1)}, bf16[1536,384]{1,0:T(8,128)(2,1)}, u32[]{:S(2)}, u32[]{:S(2)}) collective-permute-start(bf16[1536,384]{1,0:T(8,128)(2,1)} %collective-permute-done.2.rest_5_), channel_id=1, source_target_pairs={{0,4},{4,0},{8,12},{12,8},{16,20},{20,16},{24,28},{28,24},{1,5},{5... | collective-permute-start | bytes 3538952 | tf_op jit(solution)/shard_map/ppermute | solution.py:361
  124.7 16.9 %all-to-all-start.3 = ((bf16[32,64,128]{2,1,0:T(8,128)(2,1)}), bf16[32,64,128]{2,1,0:T(8,128)(2,1)S(1)}, u32[]{:S(2)}, u32[]{:S(2)}) async-start(bf16[32,64,128]{2,1,0:T(8,128)(2,1)} %attention.1), calls=%async_computation.3 | async-start | bytes 1048576 | tf_op jit(solution)/shard_map/all_to_all | solution.py:620
  141.7 1.0 copy-start.3
  152.0 7.4 %copy-start.10 = (bf16[768]{0:T(1024)(128)(2,1)S(1)}, bf16[768]{0:T(1024)(128)(2,1)}, u32[]{:S(2)}) copy-start(bf16[768]{0:T(1024)(128)(2,1)} %param.15) | copy-start | bytes 4612
  152.0 23.1 %all-to-all-start.4 = ((bf16[32,2,32,256]{3,2,1,0:T(8,128)(2,1)}), bf16[32,2,32,256]{3,2,1,0:T(8,128)(2,1)S(1)}, u32[]{:S(2)}, u32[]{:S(2)}) async-start(bf16[32,2,32,256]{3,2,1,0:T(8,128)(2,1)} %feed_forward.1), calls=%async_computation.4 | async-start | bytes 2097152 | tf_op jit(solution)/shard_map/all_to_all | solution.py:632
  159.5 15.5 %copy-start.1 = (bf16[768,256]{1,0:T(8,128)(2,1)S(1)}, bf16[768,256]{1,0:T(8,128)(2,1)}, u32[]{:S(2)}) copy-start(bf16[768,256]{1,0:T(8,128)(2,1)} %dec_ref.1) | copy-start | bytes 1179652
  176.7 1.0 copy-start.9
  177.7 1.0 copy-start.8
  178.7 1.0 copy-start.7
  181.7 1.0 copy-start.6

commit v6 on v5

--- a/solution.py
+++ b/solution.py
@@ -15,6 +15,7 @@
 MIB = 1 << 20
 ATTENTION_MIB = 34
 SAFE = 96.0
+EXTRA = 16
 
 
 def ring(height, width):
@@ -66,17 +67,16 @@
 
 
 def convolve(extended, taps, out_h, out_w):
-    beside = jnp.concatenate([extended[:, :, second : second + out_w] for second in range(3)], -1)
-    taps = taps.reshape(3, beside.shape[-1], taps.shape[-1])
     total = None
     for first in range(3):
-        term = jnp.einsum(
-            "shwc,cd->shwd",
-            beside[:, first : first + out_h],
-            taps[first],
-            preferred_element_type=jnp.float32,
-        )
-        total = term if total is None else total + term
+        for second in range(3):
+            term = jnp.einsum(
+                "shwc,cd->shwd",
+                extended[:, first : first + out_h, second : second + out_w],
+                taps[first * 3 + second],
+                preferred_element_type=jnp.float32,
+            )
+            total = term if total is None else total + term
     return total
 
 
@@ -114,7 +114,7 @@
         out_shape=jax.ShapeDtypeStruct((peers, samples, cap, width), jnp.bfloat16),
         compiler_params=params(32),
         name="dispatch",
-    )(my_start, cell_rank, tokens)
+    )(my_start, cell_rank, in_hbm(tokens))
 
 
 def project(arrived, token_col, qkv_weight, kept):
@@ -194,7 +194,7 @@
     step = 8
     contract = (((1,), (1,)), ((), ()))
 
-    def kernel(packed_ref, out_ref, low_key, high_key, value, bound):
+    def kernel(packed_ref, out_ref, low_key, high_key, low_value, high_value, bound):
         at = pl.program_id(0)
 
         @pl.when(at == 0)
@@ -208,23 +208,28 @@
                 both = pltpu.roll(wide, HD, 1).astype(jnp.bfloat16)
                 low_key[rows] = both[:half]
                 high_key[rows] = both[half:]
-                value[rows, :lanes] = packed_ref[peer, kept:]
                 square = wide * wide
                 size_q = jnp.sum(jnp.where(lane < HD, square, 0.0), -1, keepdims=True)
                 size_k = jnp.sum(jnp.where(lane < HD, 0.0, square), -1, keepdims=True)
                 most_q = jnp.maximum(most_q, size_q)
                 most_k = jnp.maximum(most_k, size_k)
-            value[:, lanes:] = jnp.ones((keys, lanes), jnp.bfloat16)
+            for pair in range(peers // 2):
+                cols = pl.ds(pair * 2 * half, 2 * half)
+                turned = packed_ref[2 * pair : 2 * pair + 2, kept:].reshape(2 * half, lanes)
+                turned = turned.astype(jnp.float32).T.astype(jnp.bfloat16)
+                low_value[:HD, cols] = turned[:HD]
+                high_value[:HD, cols] = turned[HD:]
+            low_value[HD:] = jnp.ones((EXTRA, keys), jnp.bfloat16)
+            high_value[HD:] = jnp.ones((EXTRA, keys), jnp.bfloat16)
             bound[0] = jnp.max(most_q) * jnp.max(most_k)
 
         def finish(low, high, first, count):
-            total = low[:, lanes:] + high[:, lanes:]
-            mixed = (low[:, :lanes] + pltpu.roll(high[:, :lanes], HD, 1)) / total
-            mixed = mixed.reshape(count, 2, half, lanes)
-            lane = lax.broadcasted_iota(jnp.int32, (half, lanes), 1)
+            mixed = dot(low_value[...], low) + dot(high_value[...], high)
+            mixed = mixed[:HD] / mixed[HD : HD + 1]
             for one in range(count):
-                both = jnp.where(lane < HD, mixed[one, 0], pltpu.roll(mixed[one, 1], HD, 1))
-                out_ref[first + one] = both.astype(jnp.bfloat16)
+                here = mixed[:, one * kept : (one + 1) * kept]
+                both = jnp.concatenate([here, pltpu.roll(here, half, 1)], 0).T
+                out_ref[first + one] = both[:half].astype(jnp.bfloat16)
 
         def queries(first, count):
             query = packed_ref[pl.ds(at * step + first, count), :kept].reshape(count * kept, lanes)
@@ -232,7 +237,7 @@
             return jnp.where(lane < HD, query, jnp.zeros_like(query))
 
         def score(query, key):
-            return lax.dot_general(query, key[...], contract, preferred_element_type=jnp.float32)
+            return lax.dot_general(key[...], query, contract, preferred_element_type=jnp.float32)
 
         narrow = bound[0] < SAFE * SAFE
 
@@ -241,7 +246,7 @@
             query = queries(0, step)
             low = jnp.exp2(score(query, low_key)).astype(jnp.bfloat16)
             high = jnp.exp2(score(query, high_key)).astype(jnp.bfloat16)
-            finish(dot(low, value[...]), dot(high, value[...]), 0, step)
+            finish(low, high, 0, step)
 
         @pl.when(jnp.logical_not(narrow))
         def _():
@@ -249,10 +254,10 @@
             def _(one):
                 query = queries(one, 1)
                 low, high = score(query, low_key), score(query, high_key)
-                top = jnp.maximum(jnp.max(low, -1, keepdims=True), jnp.max(high, -1, keepdims=True))
+                top = jnp.maximum(jnp.max(low, 0, keepdims=True), jnp.max(high, 0, keepdims=True))
                 low = jnp.exp2(low - top).astype(jnp.bfloat16)
                 high = jnp.exp2(high - top).astype(jnp.bfloat16)
-                finish(dot(low, value[...]), dot(high, value[...]), one, 1)
+                finish(low, high, one, 1)
 
     return pl.pallas_call(
         kernel,
@@ -263,7 +268,8 @@
         scratch_shapes=[
             pltpu.VMEM((keys, lanes), jnp.bfloat16),
             pltpu.VMEM((keys, lanes), jnp.bfloat16),
-            pltpu.VMEM((keys, 2 * lanes), jnp.bfloat16),
+            pltpu.VMEM((HD + EXTRA, keys), jnp.bfloat16),
+            pltpu.VMEM((HD + EXTRA, keys), jnp.bfloat16),
             pltpu.SMEM((1,), jnp.float32),
         ],
         compiler_params=params(ATTENTION_MIB),
@@ -311,16 +317,23 @@
         rows = x_ref[...].reshape(samples * kept, width)
         x_one = (rows.astype(jnp.float32) + dot(attn, ready(0)[...])).astype(jnp.bfloat16)
         normed = normalize(x_one.astype(jnp.float32))
-        inner = gelu(dot(normed, ready(1)[...])).astype(jnp.bfloat16)
-        total = dot(inner, ready(2)[...])
-        for at in range(3, count - 1):
+        raised = dot(normed, ready(1)[...])
+        total = jnp.zeros((samples * kept, width), jnp.float32)
+        lower = ready(2)
+        for at in range(3, count):
             piece = ready(at)
-            part = piece.shape[1]
-            inner = gelu(dot(normed, piece[:width])).astype(jnp.bfloat16)
-            added = [dot(inner, piece[pl.ds(at, part)]) for at in range(width, piece.shape[0], part)]
-            total = total + jnp.concatenate(added, 1)
+            later = dot(normed, piece[:width]) if at < count - 1 else None
+            inner = gelu(raised).astype(jnp.bfloat16)
+            if at == 3:
+                total = total + dot(inner, lower[...])
+            else:
+                part = lower.shape[1]
+                ends = range(width, lower.shape[0], part)
+                added = [dot(inner, lower[pl.ds(end, part)]) for end in ends]
+                total = total + jnp.concatenate(added, 1)
+            raised, lower = later, piece
         encoded = (x_one.astype(jnp.float32) + total).astype(jnp.bfloat16)
-        field = dot(encoded, ready(count - 1)[...]).astype(jnp.bfloat16)
+        field = dot(encoded, held[count - 1][...]).astype(jnp.bfloat16)
         for sample in range(samples):
             token = lax.broadcasted_iota(jnp.int32, (1, kept), 1)
             chosen = one_hot(col_ref[sample], token)
@@ -556,8 +569,6 @@
     tile = tile_h * tile_w
     cap = tile // peers
     kept = tile // 4
-    piece = share(up_weight, down_weight)
-
     flat_mask = keep_mask.reshape(samples, tile)
     order, ends = ring(tile_h, tile_w)
     order = jnp.asarray(order.reshape(-1))
@@ -588,7 +599,8 @@
     outgoing = dispatch(
         my_start, cell_rank.reshape(samples, 1, tile), patches.reshape(samples, tile, width), peers
     )
-    outgoing, piece = lax.optimization_barrier((outgoing, piece))
+    outgoing, *halves = lax.optimization_barrier((outgoing, up_weight, down_weight))
+    piece = share(*halves)
     pieces = from_dp(piece)
     arrived = lax.all_to_all(outgoing, PLANE, split_axis=0, concat_axis=0, tiled=True)
 

time: 190 us -> 183 us (0.963)
  waiting for transfers between devices: 49 us -> 57.1 us
  local copies, waits for them, and re-layouts: 10.5 us -> 3.39 us
  starting transfers between devices: 40.1 us -> 37 us
  Pallas kernels: 72.8 us -> 70 us
  other arithmetic: 4.25 us -> 2.07 us
    all_to_all x1, waiting for transfers between devices: 0.01 us -> 4.28 us  [shards(): lax.all_to_all(jnp.broadcast_to(counts.reshape(1, 1, counts.size), (peers...]
    slice x3 -> x0, local copies, waits for them, and re-layouts: 3.87 us -> none  [the longest x1 2.88 us: convolve(): taps[first]]
    pallas_call x1, Pallas kernels: 43.1 us -> 39.4 us  [attention(): pl.pallas_call(kernel, grid=(peers // step,), in_specs=[pl.BlockSpec(pack...]
    all_to_all x1, waiting for transfers between devices: 12.7 us -> 15.5 us  [shards(): lax.all_to_all(returning, PLANE, split_axis=0, concat_axis=0, tiled=True)]
    all_to_all x1, starting transfers between devices: 7.37 us -> 5.21 us  [shards(): lax.all_to_all(outgoing, PLANE, split_axis=0, concat_axis=0, tiled=True)]
    concatenate x1, other arithmetic: 2.22 us -> 0.12 us  [share(): jnp.concatenate([up] + [down[:, i:i + part] for i in range(0, width, part...]
    dot_general x5 -> x17, matrix products: 5.74 us -> 6.75 us  [convolve(): jnp.einsum('shwc,cd->shwd', extended[:, first:first + out_h, second:secon...]
  transfers between devices with their start and end apart: 11 -> 11, of which waited for: 3 -> 4; matrix products, arithmetic and copies ran while one was open for 5% -> 2% of each run, Pallas kernels for 29% -> 28%
where the time goes in v6:
time: 183 us; the launch traced here: 181 us
  Pallas kernels  70 us (38%)
  waiting for transfers between devices  57.1 us (31%)
  starting transfers between devices  37 us (20%)
  matrix products  11.1 us (6%)
  local copies, waits for them, and re-layouts  3.39 us (2%)
  other arithmetic  2.07 us (1%)
    pallas_call x1, Pallas kernels, attention(): pl.pallas_call(kernel, grid=(peers // step,), in_specs=[pl.BlockSpec(pack...  39.4 us
    all_to_all x1, waiting for transfers between devices, shards(): lax.all_to_all(outgoing, PLANE, split_axis=0, concat_axis=0, tiled=True)  20.7 us
    all_to_all x1, waiting for transfers between devices, shards(): lax.all_to_all(packed, PLANE, split_axis=0, concat_axis=0, tiled=True)  16.6 us
    all_to_all x1, waiting for transfers between devices, shards(): lax.all_to_all(returning, PLANE, split_axis=0, concat_axis=0, tiled=True)  15.5 us
    pallas_call x1, Pallas kernels, index(): pl.pallas_call(kernel, grid_spec=pltpu.PrefetchScalarGridSpec(num_scalar_...  11.3 us
    pallas_call x1, Pallas kernels, feed_forward(): pl.pallas_call(kernel, in_specs=[pl.BlockSpec(memory_space=pltpu.VMEM)] *...  9.15 us
    all_to_all x1, starting transfers between devices, shards(): lax.all_to_all(jnp.broadcast_to(counts.reshape(1, 1, counts.size), (peers...  8.46 us
    all_to_all x1, starting transfers between devices, shards(): lax.all_to_all(returning, PLANE, split_axis=0, concat_axis=0, tiled=True)  7.53 us
  transfers between devices with their start and end apart: 11, of which 4 were waited for; matrix products, arithmetic and copies ran while one was open for 2% of the time, Pallas kernels for 28%

profile of v6, /device:TPU:2, one launch (start us, length us, event | category | flops | bytes accessed | tf_op | source)
XLA Modules:
  0.0 181.1 jit_solution(3050201699977580191)
XLA Ops:
  0.0 0.8 convert_element_type.36
  0.8 1.0 fusion.2
  2.6 8.5 %all-to-all-start = ((s32[32,1,372]{2,1,0:T(1,128)}), s32[32,1,372]{2,1,0:T(1,128)S(1)}, u32[]{:S(2)}, u32[]{:S(2)}) async-start(s32[32,1,372]{2,1,0:T(1,128)} %broadcast_in_dim.78), calls=%async_computation | async-start | bytes 98304 | tf_op jit(solution)/shard_map/all_to_all | solution.py:582
  11.1 0.7 broadcast_compare_fusion
  11.9 1.1 broadcast_add_fusion
  13.0 4.3 %all-to-all-done = s32[32,1,372]{2,1,0:T(1,128)S(1)} async-done(((s32[32,1,372]{2,1,0:T(1,128)}), s32[32,1,372]{2,1,0:T(1,128)S(1)}, u32[]{:S(2)}, u32[]{:S(2)}) %all-to-all-start) | async-done | bytes 47648 | tf_op jit(solution)/shard_map/all_to_all | solution.py:582
  17.8 3.8 %dispatch.1 = bf16[32,2,16,768]{3,2,1,0:T(8,128)(2,1)} custom-call(s32[2]{0:T(128)S(1)} %select_reduce_fusion.1.start_ref, s32[2,1,512]{2,1,0:T(1,128)S(1)} %reshape.258.rank_ref, bf16[2,512,768]{2,1,0:T(8,128)(2,1)} %bitcast.162), custom_call_target="tpu_custom_call" | custom-call | tf_op jit(solution)/shard_map/dispatch/pallas_call | solution.py:103
  21.6 5.2 %all-to-all-start.1 = ((bf16[32,2,16,768]{3,2,1,0:T(8,128)(2,1)}), bf16[32,2,16,768]{3,2,1,0:T(8,128)(2,1)S(1)}, u32[]{:S(2)}, u32[]{:S(2)}) async-start(bf16[32,2,16,768]{3,2,1,0:T(8,128)(2,1)} %dispatch.1), calls=%async_computation.1 | async-start | bytes 3145728 | tf_op jit(solution)/shard_map/all_to_all | solution.py:605
  27.7 20.7 %all-to-all-done.1.arrived_ref = bf16[32,2,16,768]{3,2,1,0:T(8,128)(2,1)S(1)} async-done(((bf16[32,2,16,768]{3,2,1,0:T(8,128)(2,1)}), bf16[32,2,16,768]{3,2,1,0:T(8,128)(2,1)S(1)}, u32[]{:S(2)}, u32[]{:S(2)}) %all-to-all-start.1) | async-done | bytes 1572896 | tf_op jit(solution)/shard_map/all_to_all | solution.py:605
  48.4 4.7 %project.1 = (bf16[2,128,768]{2,1,0:T(8,128)(2,1)}, bf16[32,192,128]{2,1,0:T(8,128)(2,1)}) custom-call(s32[2,1,512]{2,1,0:T(1,128)S(1)} %compare_select_fusion.col_ref, bf16[32,2,16,768]{3,2,1,0:T(8,128)(2,1)S(1)} %all-to-all-done.1.arrived_ref, bf16[768,2304]{1,0:T(8,128)(2,1)} %weight_hbm.1), custom_call_target="tpu_custom_call" | custom-call | tf_op jit(solution)/shard_map/project/pallas_call | solution.py:172
  53.1 5.3 %all-to-all-start.2 = ((bf16[32,192,128]{2,1,0:T(8,128)(2,1)}), bf16[32,192,128]{2,1,0:T(8,128)(2,1)S(1)}, u32[]{:S(2)}, u32[]{:S(2)}) async-start(bf16[32,192,128]{2,1,0:T(8,128)(2,1)} %get-tuple-element.18), calls=%async_computation.2 | async-start | bytes 3145728 | tf_op jit(solution)/shard_map/all_to_all | solution.py:628
  58.6 3.1 %collective-permute-start.2 = (bf16[1536,384]{1,0:T(8,128)(2,1)S(1)}, bf16[1536,384]{1,0:T(8,128)(2,1)}, u32[]{:S(2)}, u32[]{:S(2)}) collective-permute-start(bf16[1536,384]{1,0:T(8,128)(2,1)S(1)} %pad_maximum_fusion), channel_id=1, source_target_pairs={{0,96},{32,0},{64,32},{96,64},{1,97},{33,1},{65,33},{97,65},{2,98}... | collective-permute-start | bytes 3538952 | tf_op jit(solution)/shard_map/ppermute | solution.py:368
  62.3 1.0 collective-permute-start
  63.3 16.6 %all-to-all-done.2.packed_ref = bf16[32,192,128]{2,1,0:T(8,128)(2,1)S(1)} async-done(((bf16[32,192,128]{2,1,0:T(8,128)(2,1)}), bf16[32,192,128]{2,1,0:T(8,128)(2,1)S(1)}, u32[]{:S(2)}, u32[]{:S(2)}) %all-to-all-start.2) | async-done | bytes 1572896 | tf_op jit(solution)/shard_map/all_to_all | solution.py:628
  79.9 39.4 %attention.1 = bf16[32,64,128]{2,1,0:T(8,128)(2,1)} custom-call(bf16[32,192,128]{2,1,0:T(8,128)(2,1)S(1)} %all-to-all-done.2.packed_ref), custom_call_target="tpu_custom_call" | custom-call | tf_op jit(solution)/shard_map/attention/pallas_call | solution.py:262
  120.0 5.1 %all-to-all-start.3 = ((bf16[32,64,128]{2,1,0:T(8,128)(2,1)}), bf16[32,64,128]{2,1,0:T(8,128)(2,1)S(1)}, u32[]{:S(2)}, u32[]{:S(2)}) async-start(bf16[32,64,128]{2,1,0:T(8,128)(2,1)} %attention.1), calls=%async_computation.3 | async-start | bytes 1048576 | tf_op jit(solution)/shard_map/all_to_all | solution.py:632
  125.6 11.3 %index.1 = (s32[2,1024,1]{2,1,0:T(8,128)S(1)}, s32[2,800,1]{2,1,0:T(8,128)S(1)}) custom-call(s32[1]{0:T(128)} %bitcast.me_ref, s32[2,32,186]{2,1,0:T(8,128)S(1)} %bitcast.161, s32[2,800,1]{2,1,0:T(8,128)S(1)} %reshape.281.rank_ref), custom_call_target="tpu_custom_call" | custom-call | tf_op jit(solution)/shard_map/index/pallas_call | solution.py:523
  136.9 1.0 copy-done.2
  137.9 9.2 %feed_forward.1 = bf16[32,2,32,256]{3,2,1,0:T(8,128)(2,1)} custom-call(bf16[32,64,128]{2,1,0:T(8,128)(2,1)S(1)} %all-to-all-done.3.mixed_ref, bf16[2,128,768]{2,1,0:T(8,128)(2,1)S(1)} %copy-done.2, s32[2,1024,1]{2,1,0:T(8,128)S(1)} %get-tuple-element.23.col_ref, bf16[768,768]{1,0:T(8,128)(2,1)} %rest_0_.1, bf16[768,768]{1,0:T(8,128)(2,1)} %rest_1_.1, ...), custom_call_target="tpu_custom_call" | custom-call | tf_op jit(solution)/shard_map/feed_forward/pallas_call | solution.py:343
  147.1 7.5 %all-to-all-start.4 = ((bf16[32,2,32,256]{3,2,1,0:T(8,128)(2,1)}), bf16[32,2,32,256]{3,2,1,0:T(8,128)(2,1)S(1)}, u32[]{:S(2)}, u32[]{:S(2)}) async-start(bf16[32,2,32,256]{3,2,1,0:T(8,128)(2,1)} %feed_forward.1), calls=%async_computation.4 | async-start | bytes 2097152 | tf_op jit(solution)/shard_map/all_to_all | solution.py:644
  154.8 15.5 %all-to-all-done.4.home_ref = bf16[32,2,32,256]{3,2,1,0:T(8,128)(2,1)S(1)} async-done(((bf16[32,2,32,256]{3,2,1,0:T(8,128)(2,1)}), bf16[32,2,32,256]{3,2,1,0:T(8,128)(2,1)S(1)}, u32[]{:S(2)}, u32[]{:S(2)}) %all-to-all-start.4) | async-done | bytes 1048608 | tf_op jit(solution)/shard_map/all_to_all | solution.py:644
  170.3 1.7 place.1
  175.0 1.3 select_convert_fusion
  178.8 2.3 %convolution_convert_fusion = bf16[2,16,32,128]{3,2,1,0:T(8,128)(2,1)} fusion(f32[2,16,32,256]{3,2,1,0:T(8,128)S(1)} %convolution_add_fusion.1, bf16[2,18,34,256]{3,2,1,0:T(8,128)(2,1)S(1)} %select_convert_fusion, bf16[2,9,256,256]{3,2,1,0:T(8,128)(2,1)} %param.21, bf16[256,128]{1,0:T(8,128)(2,1)S(1)} %copy-done), kind=kOutput, calls=%fused_computation.9 | convolution fusion | flops 203554816 | bytes 2555904 | tf_op jit(solution)/shard_map/dot_general | solution.py:62
  (75 shorter events, 9.8 us)
Async XLA Ops:
  0.0 178.8 %copy-start = (bf16[256,128]{1,0:T(8,128)(2,1)S(1)}, bf16[256,128]{1,0:T(8,128)(2,1)}, u32[]{:S(2)}) copy-start(bf16[256,128]{1,0:T(8,128)(2,1)} %param.22) | copy-start | bytes 196612
  2.6 14.7 %all-to-all-start = ((s32[32,1,372]{2,1,0:T(1,128)}), s32[32,1,372]{2,1,0:T(1,128)S(1)}, u32[]{:S(2)}, u32[]{:S(2)}) async-start(s32[32,1,372]{2,1,0:T(1,128)} %broadcast_in_dim.78), calls=%async_computation | async-start | bytes 98304 | tf_op jit(solution)/shard_map/all_to_all | solution.py:582
  21.6 5.9 %copy-start.3 = (bf16[768,768]{1,0:T(8,128)(2,1)S(1)}, bf16[768,768]{1,0:T(8,128)(2,1)}, u32[]{:S(2)}) copy-start(bf16[768,768]{1,0:T(8,128)(2,1)} %rest_1_.1) | copy-start | bytes 3538948
  21.6 26.8 %all-to-all-start.1 = ((bf16[32,2,16,768]{3,2,1,0:T(8,128)(2,1)}), bf16[32,2,16,768]{3,2,1,0:T(8,128)(2,1)S(1)}, u32[]{:S(2)}, u32[]{:S(2)}) async-start(bf16[32,2,16,768]{3,2,1,0:T(8,128)(2,1)} %dispatch.1), calls=%async_computation.1 | async-start | bytes 3145728 | tf_op jit(solution)/shard_map/all_to_all | solution.py:605
  53.1 5.3 %copy-start.4 = (bf16[768,768]{1,0:T(8,128)(2,1)S(1)}, bf16[768,768]{1,0:T(8,128)(2,1)}, u32[]{:S(2)}) copy-start(bf16[768,768]{1,0:T(8,128)(2,1)} %rest_2_.1) | copy-start | bytes 3538948
  53.1 26.8 %all-to-all-start.2 = ((bf16[32,192,128]{2,1,0:T(8,128)(2,1)}), bf16[32,192,128]{2,1,0:T(8,128)(2,1)S(1)}, u32[]{:S(2)}, u32[]{:S(2)}) async-start(bf16[32,192,128]{2,1,0:T(8,128)(2,1)} %get-tuple-element.18), calls=%async_computation.2 | async-start | bytes 3145728 | tf_op jit(solution)/shard_map/all_to_all | solution.py:628
  58.6 60.7 %collective-permute-start.2 = (bf16[1536,384]{1,0:T(8,128)(2,1)S(1)}, bf16[1536,384]{1,0:T(8,128)(2,1)}, u32[]{:S(2)}, u32[]{:S(2)}) collective-permute-start(bf16[1536,384]{1,0:T(8,128)(2,1)S(1)} %pad_maximum_fusion), channel_id=1, source_target_pairs={{0,96},{32,0},{64,32},{96,64},{1,97},{33,1},{65,33},{97,65},{2,98}... | collective-permute-start | bytes 3538952 | tf_op jit(solution)/shard_map/ppermute | solution.py:368
  61.7 57.6 %collective-permute-start.1 = (bf16[1536,384]{1,0:T(8,128)(2,1)S(1)}, bf16[1536,384]{1,0:T(8,128)(2,1)}, u32[]{:S(2)}, u32[]{:S(2)}) collective-permute-start(bf16[1536,384]{1,0:T(8,128)(2,1)S(1)} %pad_maximum_fusion), channel_id=1, source_target_pairs={{0,64},{32,96},{64,0},{96,32},{1,65},{33,97},{65,1},{97,33},{2,66}... | collective-permute-start | bytes 3538952 | tf_op jit(solution)/shard_map/ppermute | solution.py:368
  62.3 57.0 %collective-permute-start = (bf16[1536,384]{1,0:T(8,128)(2,1)S(1)}, bf16[1536,384]{1,0:T(8,128)(2,1)}, u32[]{:S(2)}, u32[]{:S(2)}) collective-permute-start(bf16[1536,384]{1,0:T(8,128)(2,1)S(1)} %pad_maximum_fusion), channel_id=1, source_target_pairs={{0,32},{32,64},{64,96},{96,0},{1,33},{33,65},{65,97},{97,1},{2,34}... | collective-permute-start | bytes 3538952 | tf_op jit(solution)/shard_map/ppermute | solution.py:368
  119.3 17.6 %collective-permute-start.3 = (bf16[1536,384]{1,0:T(8,128)(2,1)}, bf16[1536,384]{1,0:T(8,128)(2,1)}, u32[]{:S(2)}, u32[]{:S(2)}) collective-permute-start(bf16[1536,384]{1,0:T(8,128)(2,1)} %collective-permute-done.rest_3_), channel_id=1, source_target_pairs={{0,4},{4,0},{8,12},{12,8},{16,20},{20,16},{24,28},{28,24},{1,5},{5... | collective-permute-start | bytes 3538952 | tf_op jit(solution)/shard_map/ppermute | solution.py:374
  119.4 17.5 %collective-permute-start.4 = (bf16[1536,384]{1,0:T(8,128)(2,1)}, bf16[1536,384]{1,0:T(8,128)(2,1)}, u32[]{:S(2)}, u32[]{:S(2)}) collective-permute-start(bf16[1536,384]{1,0:T(8,128)(2,1)} %collective-permute-done.1.rest_4_), channel_id=1, source_target_pairs={{0,4},{4,0},{8,12},{12,8},{16,20},{20,16},{24,28},{28,24},{1,5},{5... | collective-permute-start | bytes 3538952 | tf_op jit(solution)/shard_map/ppermute | solution.py:374
  119.9 17.0 %collective-permute-start.5 = (bf16[1536,384]{1,0:T(8,128)(2,1)}, bf16[1536,384]{1,0:T(8,128)(2,1)}, u32[]{:S(2)}, u32[]{:S(2)}) collective-permute-start(bf16[1536,384]{1,0:T(8,128)(2,1)} %collective-permute-done.2.rest_5_), channel_id=1, source_target_pairs={{0,4},{4,0},{8,12},{12,8},{16,20},{20,16},{24,28},{28,24},{1,5},{5... | collective-permute-start | bytes 3538952 | tf_op jit(solution)/shard_map/ppermute | solution.py:374
  120.0 16.9 %all-to-all-start.3 = ((bf16[32,64,128]{2,1,0:T(8,128)(2,1)}), bf16[32,64,128]{2,1,0:T(8,128)(2,1)S(1)}, u32[]{:S(2)}, u32[]{:S(2)}) async-start(bf16[32,64,128]{2,1,0:T(8,128)(2,1)} %attention.1), calls=%async_computation.3 | async-start | bytes 1048576 | tf_op jit(solution)/shard_map/all_to_all | solution.py:632
  136.9 1.0 copy-start.2
  147.1 7.6 %copy-start.6 = (bf16[768]{0:T(1024)(128)(2,1)S(1)}, bf16[768]{0:T(1024)(128)(2,1)}, u32[]{:S(2)}) copy-start(bf16[768]{0:T(1024)(128)(2,1)} %param.15) | copy-start | bytes 4612
  147.1 23.2 %copy-start.1 = (bf16[768,256]{1,0:T(8,128)(2,1)S(1)}, bf16[768,256]{1,0:T(8,128)(2,1)}, u32[]{:S(2)}) copy-start(bf16[768,256]{1,0:T(8,128)(2,1)} %dec_ref.1) | copy-start | bytes 1179652
  147.1 23.2 %all-to-all-start.4 = ((bf16[32,2,32,256]{3,2,1,0:T(8,128)(2,1)}), bf16[32,2,32,256]{3,2,1,0:T(8,128)(2,1)S(1)}, u32[]{:S(2)}, u32[]{:S(2)}) async-start(bf16[32,2,32,256]{3,2,1,0:T(8,128)(2,1)} %feed_forward.1), calls=%async_computation.4 | async-start | bytes 2097152 | tf_op jit(solution)/shard_map/all_to_all | solution.py:644
  170.3 1.7 copy-start.5

commit v7 on v6

--- a/solution.py
+++ b/solution.py
@@ -88,33 +88,56 @@
     return pltpu.CompilerParams(vmem_limit_bytes=limit * MIB)
 
 
-def dispatch(my_start, cell_rank, tokens, peers):
+def compact(cell_rank, tokens, peers):
     samples, tile, width = tokens.shape
     cap = tile // peers
 
-    def kernel(start_ref, rank_ref, token_ref, out_ref):
-        start = start_ref[pl.program_id(0)]
+    def kernel(rank_ref, token_ref, out_ref):
         slot = lax.broadcasted_iota(jnp.int32, (tile, 1), 0)
-        rank = (slot % cap) * peers + ((slot // cap - start) & (peers - 1))
+        rank = (slot % cap) * peers + slot // cap
         chosen = one_hot(rank, rank_ref[...].reshape(1, tile))
         rows = dot(chosen, token_ref[...].reshape(tile, width)).astype(jnp.bfloat16)
-        out_ref[...] = rows.reshape(peers, 1, cap, width)
+        rows = rows.reshape(peers, 1, cap, width)
+        out_ref[:peers] = rows
+        out_ref[peers:] = rows
 
     return pl.pallas_call(
         kernel,
-        grid_spec=pltpu.PrefetchScalarGridSpec(
-            num_scalar_prefetch=1,
-            grid=(samples,),
-            in_specs=[
-                pl.BlockSpec((1, 1, tile), lambda s, _: (s, 0, 0)),
-                pl.BlockSpec((1, tile, width), lambda s, _: (s, 0, 0)),
-            ],
-            out_specs=pl.BlockSpec((peers, 1, cap, width), lambda s, _: (0, s, 0, 0)),
-        ),
-        out_shape=jax.ShapeDtypeStruct((peers, samples, cap, width), jnp.bfloat16),
-        compiler_params=params(32),
+        grid=(samples,),
+        in_specs=[
+            pl.BlockSpec((1, 1, tile), lambda s: (s, 0, 0)),
+            pl.BlockSpec((1, tile, width), lambda s: (s, 0, 0)),
+        ],
+        out_specs=pl.BlockSpec((2 * peers, 1, cap, width), lambda s: (0, s, 0, 0)),
+        out_shape=jax.ShapeDtypeStruct((2 * peers, samples, cap, width), jnp.bfloat16),
+        compiler_params=params(20),
+        name="compact",
+    )(cell_rank, in_hbm(tokens))
+
+
+def dispatch(my_start, twice):
+    peers, samples, cap, width = twice.shape
+    peers = peers // 2
+
+    def kernel(start_ref, twice_ref, out_hbm, sems):
+        copies = []
+        for sample in range(samples):
+            turn = (-start_ref[sample]) & (peers - 1)
+            source = twice_ref.at[pl.ds(turn, peers), sample]
+            copies.append(pltpu.make_async_copy(source, out_hbm.at[:, sample], sems.at[sample]))
+            copies[-1].start()
+        for copy in copies:
+            copy.wait()
+
+    return pl.pallas_call(
+        kernel,
+        in_specs=[pl.BlockSpec(memory_space=pltpu.SMEM), pl.BlockSpec(memory_space=pltpu.VMEM)],
+        out_specs=pl.BlockSpec(memory_space=pltpu.HBM),
+        out_shape=pltpu.HBM((peers, samples, cap, width), jnp.bfloat16),
+        scratch_shapes=[pltpu.SemaphoreType.DMA((samples,))],
+        compiler_params=params(8),
         name="dispatch",
-    )(my_start, cell_rank, in_hbm(tokens))
+    )(my_start, twice)
 
 
 def project(arrived, token_col, qkv_weight, kept):
@@ -277,22 +300,50 @@
     )(packed)
 
 
+def fetch(arrays):
+    count = len(arrays)
+
+    def kernel(*refs):
+        sources, held, sems = refs[:count], refs[count : 2 * count], refs[-1]
+        copies = [
+            pltpu.make_async_copy(source, kept, sems.at[at])
+            for at, (source, kept) in enumerate(zip(sources, held))
+        ]
+        for copy in copies:
+            copy.start()
+        for copy in copies:
+            copy.wait()
+
+    return pl.pallas_call(
+        kernel,
+        in_specs=[pl.BlockSpec(memory_space=pltpu.HBM)] * count,
+        out_specs=[pl.BlockSpec(memory_space=pltpu.VMEM)] * count,
+        out_shape=[pltpu.VMEM(one.shape, one.dtype) for one in arrays],
+        scratch_shapes=[pltpu.SemaphoreType.DMA((count,))],
+        compiler_params=params(2),
+        name="fetch",
+    )(*[in_hbm(one) for one in arrays])
+
+
 def feed_forward(mixed, x, token_col, out_weight, up, down, dec_proj, pieces, slots):
     peers, half, lanes = mixed.shape
     samples, kept, width = x.shape
     places = peers // samples
     narrow = dec_proj.shape[1]
 
-    weights = [in_hbm(one) for one in (out_weight, up, down, *pieces, dec_proj)]
+    weights = [in_hbm(one) for one in (down, *pieces, dec_proj)]
     count = len(weights)
 
-    def kernel(mixed_ref, x_ref, col_ref, *rest):
-        sources, out_ref, held, sems = rest[:count], rest[count], rest[count + 1 : -1], rest[-1]
+    def kernel(mixed_ref, x_ref, col_hbm, out_w, up_ref, *rest):
+        sources, out_ref, held = rest[:count], rest[count], rest[count + 1 : -2]
+        col_ref, sems = rest[-2:]
+        slots_in = pltpu.make_async_copy(col_hbm, col_ref, sems.at[count])
         copies = [
             pltpu.make_async_copy(source, held[at], sems.at[at])
             for at, source in enumerate(sources)
         ]
-        ahead = 3
+        slots_in.start()
+        ahead = 4
         for copy in copies[:ahead]:
             copy.start()
 
@@ -315,16 +366,16 @@
             attn.append(jnp.concatenate(parts, 1))
         attn = jnp.concatenate(attn, 0)
         rows = x_ref[...].reshape(samples * kept, width)
-        x_one = (rows.astype(jnp.float32) + dot(attn, ready(0)[...])).astype(jnp.bfloat16)
+        x_one = (rows.astype(jnp.float32) + dot(attn, out_w[...])).astype(jnp.bfloat16)
         normed = normalize(x_one.astype(jnp.float32))
-        raised = dot(normed, ready(1)[...])
+        raised = dot(normed, up_ref[...])
         total = jnp.zeros((samples * kept, width), jnp.float32)
-        lower = ready(2)
-        for at in range(3, count):
+        lower = ready(0)
+        for at in range(1, count):
             piece = ready(at)
             later = dot(normed, piece[:width]) if at < count - 1 else None
             inner = gelu(raised).astype(jnp.bfloat16)
-            if at == 3:
+            if at == 1:
                 total = total + dot(inner, lower[...])
             else:
                 part = lower.shape[1]
@@ -334,6 +385,7 @@
             raised, lower = later, piece
         encoded = (x_one.astype(jnp.float32) + total).astype(jnp.bfloat16)
         field = dot(encoded, held[count - 1][...]).astype(jnp.bfloat16)
+        slots_in.wait()
         for sample in range(samples):
             token = lax.broadcasted_iota(jnp.int32, (1, kept), 1)
             chosen = one_hot(col_ref[sample], token)
@@ -342,15 +394,17 @@
 
     return pl.pallas_call(
         kernel,
-        in_specs=[pl.BlockSpec(memory_space=pltpu.VMEM)] * 3
+        in_specs=[pl.BlockSpec(memory_space=pltpu.VMEM)] * 2
+        + [pl.BlockSpec(memory_space=pltpu.HBM)]
+        + [pl.BlockSpec(memory_space=pltpu.VMEM)] * 2
         + [pl.BlockSpec(memory_space=pltpu.HBM)] * count,
         out_specs=pl.BlockSpec(memory_space=pltpu.VMEM),
         out_shape=jax.ShapeDtypeStruct((peers, samples, slots, narrow), jnp.bfloat16),
         scratch_shapes=[pltpu.VMEM(one.shape, one.dtype) for one in weights]
-        + [pltpu.SemaphoreType.DMA((count,))],
+        + [pltpu.VMEM(token_col.shape, jnp.int32), pltpu.SemaphoreType.DMA((count + 1,))],
         compiler_params=params(32),
         name="feed_forward",
-    )(mixed, x, token_col, *weights)
+    )(mixed, x, in_hbm(token_col), out_weight, up, *weights)
 
 
 def share(up_weight, down_weight):
@@ -585,20 +639,22 @@
         split_axis=0,
         concat_axis=0,
         tiled=True,
-    ).reshape(peers, samples, marks + edge)
+    )
+    told_all = told_all.reshape(peers, samples, marks + edge)
     told = told_all[:, :, marks - 1]
     before = order[:, None] < order[None, :]
     running = dot(flat_mask.astype(jnp.bfloat16), before.astype(jnp.bfloat16)).astype(jnp.int32)
     cell_rank = jnp.where(flat_mask == 1, running, -1)
+    twice = compact(
+        cell_rank.reshape(samples, 1, tile), patches.reshape(samples, tile, width), peers
+    )
 
     ids = jnp.arange(peers, dtype=jnp.int32)
     earlier = ids[:, None] < ids[None, :]
     starts = jnp.sum(jnp.where(earlier[:, :, None], told[:, None, :], 0), 0)
     my_start = jnp.sum(jnp.where((ids < me)[:, None], told, 0), 0)
 
-    outgoing = dispatch(
-        my_start, cell_rank.reshape(samples, 1, tile), patches.reshape(samples, tile, width), peers
-    )
+    outgoing = dispatch(my_start, twice)
     outgoing, *halves = lax.optimization_barrier((outgoing, up_weight, down_weight))
     piece = share(*halves)
     pieces = from_dp(piece)
@@ -629,13 +685,14 @@
     mixed = attention(packed, kept)
     mixed, *pieces = lax.optimization_barrier((mixed, *pieces))
     pieces = pieces + [from_partner(one) for one in pieces]
+    out_near, up_near = fetch([out_weight, up_weight])
     mixed = lax.all_to_all(mixed, PLANE, split_axis=0, concat_axis=0, tiled=True)
     returning = feed_forward(
         mixed,
         x,
         back,
-        out_weight,
-        up_weight,
+        out_near,
+        up_near,
         down_weight,
         dec_proj,
         pieces,

time: 183 us -> 187 us (1.022)
  local copies, waits for them, and re-layouts: 3.39 us -> 6.72 us
  waiting for transfers between devices: 57.1 us -> 54.5 us
  Pallas kernels: 70 us -> 72.3 us
    unnamed x14 -> x20, local copies, waits for them, and re-layouts: 1.02 us -> 4.35 us
    all_to_all x1, waiting for transfers between devices: 4.28 us -> 1.76 us  [shards(): lax.all_to_all(jnp.broadcast_to(counts.reshape(1, 1, counts.size), (peers...]
    pallas_call x1 -> x3, Pallas kernels: 3.8 us -> 5.91 us  [the longest x1 2.52 us: compact(): pl.pallas_call(kernel, grid=(samples,), in_specs=[pl.BlockSpec((1, 1, til...]
  transfers between devices with their start and end apart: 11 -> 11, of which waited for: 4 -> 4; matrix products, arithmetic and copies ran while one was open for 2% -> 2% of each run, Pallas kernels for 28% -> 30%
where the time goes in v7:
time: 187 us; the launch traced here: 185 us
  Pallas kernels  72.3 us (39%)
  waiting for transfers between devices  54.5 us (29%)
  starting transfers between devices  37.5 us (20%)
  matrix products  11.1 us (6%)
  local copies, waits for them, and re-layouts  6.72 us (4%)
  other arithmetic  2.07 us (1%)
    pallas_call x1, Pallas kernels, attention(): pl.pallas_call(kernel, grid=(peers // step,), in_specs=[pl.BlockSpec(pack...  39.4 us
    all_to_all x1, waiting for transfers between devices, shards(): lax.all_to_all(outgoing, PLANE, split_axis=0, concat_axis=0, tiled=True)  20.6 us
    all_to_all x1, waiting for transfers between devices, shards(): lax.all_to_all(packed, PLANE, split_axis=0, concat_axis=0, tiled=True)  16.6 us
    all_to_all x1, waiting for transfers between devices, shards(): lax.all_to_all(returning, PLANE, split_axis=0, concat_axis=0, tiled=True)  15.5 us
    pallas_call x1, Pallas kernels, index(): pl.pallas_call(kernel, grid_spec=pltpu.PrefetchScalarGridSpec(num_scalar_...  11.3 us
    pallas_call x1, Pallas kernels, feed_forward(): pl.pallas_call(kernel, in_specs=[pl.BlockSpec(memory_space=pltpu.VMEM)] *...  9.37 us
    all_to_all x1, starting transfers between devices, shards(): lax.all_to_all(jnp.broadcast_to(counts.reshape(1, 1, counts.size), (peers...  8.46 us
    all_to_all x1, starting transfers between devices, shards(): lax.all_to_all(returning, PLANE, split_axis=0, concat_axis=0, tiled=True)  7.51 us
  transfers between devices with their start and end apart: 11, of which 4 were waited for; matrix products, arithmetic and copies ran while one was open for 2% of the time, Pallas kernels for 30%

profile of v7, /device:TPU:2, one launch (start us, length us, event | category | flops | bytes accessed | tf_op | source)
XLA Modules:
  0.0 184.7 jit_solution(2534040190940891171)
XLA Ops:
  0.8 1.0 fusion.2
  2.6 8.5 %all-to-all-start = ((s32[32,1,372]{2,1,0:T(1,128)}), s32[32,1,372]{2,1,0:T(1,128)S(1)}, u32[]{:S(2)}, u32[]{:S(2)}) async-start(s32[32,1,372]{2,1,0:T(1,128)} %broadcast_in_dim.78), calls=%async_computation | async-start | bytes 98304 | tf_op jit(solution)/shard_map/all_to_all | solution.py:636
  11.9 1.1 broadcast_add_fusion
  13.0 2.5 %compact.1.twice_ref = bf16[64,2,16,768]{3,2,1,0:T(8,128)(2,1)S(1)} custom-call(s32[2,1,512]{2,1,0:T(1,128)S(1)} %reshape.258.rank_ref, bf16[2,512,768]{2,1,0:T(8,128)(2,1)} %bitcast.162), custom_call_target="tpu_custom_call" | custom-call | tf_op jit(solution)/shard_map/compact/pallas_call | solution.py:104
  15.5 1.8 all-to-all-done
  17.8 1.7 dispatch.1
  19.6 5.8 %all-to-all-start.1 = ((bf16[32,2,16,768]{3,2,1,0:T(8,128)(2,1)}), bf16[32,2,16,768]{3,2,1,0:T(8,128)(2,1)S(1)}, u32[]{:S(2)}, u32[]{:S(2)}) async-start(bf16[32,2,16,768]{3,2,1,0:T(8,128)(2,1)} %dispatch.1), calls=%async_computation.1 | async-start | bytes 3145728 | tf_op jit(solution)/shard_map/all_to_all | solution.py:661
  26.2 20.6 %all-to-all-done.1.arrived_ref = bf16[32,2,16,768]{3,2,1,0:T(8,128)(2,1)S(1)} async-done(((bf16[32,2,16,768]{3,2,1,0:T(8,128)(2,1)}), bf16[32,2,16,768]{3,2,1,0:T(8,128)(2,1)S(1)}, u32[]{:S(2)}, u32[]{:S(2)}) %all-to-all-start.1) | async-done | bytes 1572896 | tf_op jit(solution)/shard_map/all_to_all | solution.py:661
  46.9 4.7 %project.1 = (bf16[2,128,768]{2,1,0:T(8,128)(2,1)}, bf16[32,192,128]{2,1,0:T(8,128)(2,1)}) custom-call(s32[2,1,512]{2,1,0:T(1,128)S(1)} %compare_select_fusion.col_ref, bf16[32,2,16,768]{3,2,1,0:T(8,128)(2,1)S(1)} %all-to-all-done.1.arrived_ref, bf16[768,2304]{1,0:T(8,128)(2,1)} %weight_hbm.1), custom_call_target="tpu_custom_call" | custom-call | tf_op jit(solution)/shard_map/project/pallas_call | solution.py:195
  51.6 5.2 %all-to-all-start.2 = ((bf16[32,192,128]{2,1,0:T(8,128)(2,1)}), bf16[32,192,128]{2,1,0:T(8,128)(2,1)S(1)}, u32[]{:S(2)}, u32[]{:S(2)}) async-start(bf16[32,192,128]{2,1,0:T(8,128)(2,1)} %get-tuple-element.20), calls=%async_computation.2 | async-start | bytes 3145728 | tf_op jit(solution)/shard_map/all_to_all | solution.py:684
  57.0 3.1 %collective-permute-start.2 = (bf16[1536,384]{1,0:T(8,128)(2,1)S(1)}, bf16[1536,384]{1,0:T(8,128)(2,1)}, u32[]{:S(2)}, u32[]{:S(2)}) collective-permute-start(bf16[1536,384]{1,0:T(8,128)(2,1)S(1)} %pad_maximum_fusion), channel_id=1, source_target_pairs={{0,96},{32,0},{64,32},{96,64},{1,97},{33,1},{65,33},{97,65},{2,98}... | collective-permute-start | bytes 3538952 | tf_op jit(solution)/shard_map/ppermute | solution.py:422
  61.7 16.6 %all-to-all-done.2.packed_ref = bf16[32,192,128]{2,1,0:T(8,128)(2,1)S(1)} async-done(((bf16[32,192,128]{2,1,0:T(8,128)(2,1)}), bf16[32,192,128]{2,1,0:T(8,128)(2,1)S(1)}, u32[]{:S(2)}, u32[]{:S(2)}) %all-to-all-start.2) | async-done | bytes 1572896 | tf_op jit(solution)/shard_map/all_to_all | solution.py:684
  78.3 39.4 %attention.1 = bf16[32,64,128]{2,1,0:T(8,128)(2,1)} custom-call(bf16[32,192,128]{2,1,0:T(8,128)(2,1)S(1)} %all-to-all-done.2.packed_ref), custom_call_target="tpu_custom_call" | custom-call | tf_op jit(solution)/shard_map/attention/pallas_call | solution.py:285
  118.3 5.1 %all-to-all-start.3 = ((bf16[32,64,128]{2,1,0:T(8,128)(2,1)}), bf16[32,64,128]{2,1,0:T(8,128)(2,1)S(1)}, u32[]{:S(2)}, u32[]{:S(2)}) async-start(bf16[32,64,128]{2,1,0:T(8,128)(2,1)} %attention.1), calls=%async_computation.3 | async-start | bytes 1048576 | tf_op jit(solution)/shard_map/all_to_all | solution.py:689
  123.9 1.6 fetch.1
  126.6 11.3 %index.1 = (s32[2,1024,1]{2,1,0:T(8,128)S(1)}, s32[2,800,1]{2,1,0:T(8,128)S(1)}) custom-call(s32[1]{0:T(128)} %bitcast.me_ref, s32[2,32,186]{2,1,0:T(8,128)S(1)} %bitcast.161, s32[2,800,1]{2,1,0:T(8,128)S(1)} %reshape.281.rank_ref), custom_call_target="tpu_custom_call" | custom-call | tf_op jit(solution)/shard_map/index/pallas_call | solution.py:577
  137.9 1.1 copy-done.4
  139.0 1.3 copy-done.3
  141.3 9.4 %feed_forward.1 = bf16[32,2,32,256]{3,2,1,0:T(8,128)(2,1)} custom-call(bf16[32,64,128]{2,1,0:T(8,128)(2,1)S(1)} %all-to-all-done.3.mixed_ref, bf16[2,128,768]{2,1,0:T(8,128)(2,1)S(1)} %copy-done.5, s32[2,1024,1]{2,1,0:T(8,128)} %copy-done.4, bf16[768,768]{1,0:T(8,128)(2,1)S(1)} %get-tuple-element.26.out_w, bf16[768,768]{1,0:T(8,128)(2,1)S(1)} %copy-done.3, ...), custom_call_target="tpu_custom_call" | custom-call | tf_op jit(solution)/shard_map/feed_forward/pallas_call | solution.py:395
  150.7 7.5 %all-to-all-start.4 = ((bf16[32,2,32,256]{3,2,1,0:T(8,128)(2,1)}), bf16[32,2,32,256]{3,2,1,0:T(8,128)(2,1)S(1)}, u32[]{:S(2)}, u32[]{:S(2)}) async-start(bf16[32,2,32,256]{3,2,1,0:T(8,128)(2,1)} %feed_forward.1), calls=%async_computation.4 | async-start | bytes 2097152 | tf_op jit(solution)/shard_map/all_to_all | solution.py:701
  158.3 15.5 %all-to-all-done.4.home_ref = bf16[32,2,32,256]{3,2,1,0:T(8,128)(2,1)S(1)} async-done(((bf16[32,2,32,256]{3,2,1,0:T(8,128)(2,1)}), bf16[32,2,32,256]{3,2,1,0:T(8,128)(2,1)S(1)}, u32[]{:S(2)}, u32[]{:S(2)}) %all-to-all-start.4) | async-done | bytes 1048608 | tf_op jit(solution)/shard_map/all_to_all | solution.py:701
  173.9 1.7 place.1
  178.5 1.3 select_convert_fusion
  182.4 2.3 %convolution_convert_fusion = bf16[2,16,32,128]{3,2,1,0:T(8,128)(2,1)} fusion(f32[2,16,32,256]{3,2,1,0:T(8,128)S(1)} %convolution_add_fusion.1, bf16[2,18,34,256]{3,2,1,0:T(8,128)(2,1)S(1)} %select_convert_fusion, bf16[2,9,256,256]{3,2,1,0:T(8,128)(2,1)} %param.21, bf16[256,128]{1,0:T(8,128)(2,1)S(1)} %copy-done), kind=kOutput, calls=%fused_computation.9 | convolution fusion | flops 203554816 | bytes 2555904 | tf_op jit(solution)/shard_map/dot_general | solution.py:62
  (83 shorter events, 14.2 us)
Async XLA Ops:
  0.0 182.4 %copy-start = (bf16[256,128]{1,0:T(8,128)(2,1)S(1)}, bf16[256,128]{1,0:T(8,128)(2,1)}, u32[]{:S(2)}) copy-start(bf16[256,128]{1,0:T(8,128)(2,1)} %param.22) | copy-start | bytes 196612
  2.6 14.7 %all-to-all-start = ((s32[32,1,372]{2,1,0:T(1,128)}), s32[32,1,372]{2,1,0:T(1,128)S(1)}, u32[]{:S(2)}, u32[]{:S(2)}) async-start(s32[32,1,372]{2,1,0:T(1,128)} %broadcast_in_dim.78), calls=%async_computation | async-start | bytes 98304 | tf_op jit(solution)/shard_map/all_to_all | solution.py:636
  19.6 6.5 %copy-start.6 = (bf16[768,768]{1,0:T(8,128)(2,1)S(1)}, bf16[768,768]{1,0:T(8,128)(2,1)}, u32[]{:S(2)}) copy-start(bf16[768,768]{1,0:T(8,128)(2,1)} %refs_1_.1) | copy-start | bytes 3538948
  19.6 27.3 %all-to-all-start.1 = ((bf16[32,2,16,768]{3,2,1,0:T(8,128)(2,1)}), bf16[32,2,16,768]{3,2,1,0:T(8,128)(2,1)S(1)}, u32[]{:S(2)}, u32[]{:S(2)}) async-start(bf16[32,2,16,768]{3,2,1,0:T(8,128)(2,1)} %dispatch.1), calls=%async_computation.1 | async-start | bytes 3145728 | tf_op jit(solution)/shard_map/all_to_all | solution.py:661
  51.5 5.2 %copy-start.7 = (bf16[768,768]{1,0:T(8,128)(2,1)S(1)}, bf16[768,768]{1,0:T(8,128)(2,1)}, u32[]{:S(2)}) copy-start(bf16[768,768]{1,0:T(8,128)(2,1)} %rest_0_.1) | copy-start | bytes 3538948
  51.6 26.7 %all-to-all-start.2 = ((bf16[32,192,128]{2,1,0:T(8,128)(2,1)}), bf16[32,192,128]{2,1,0:T(8,128)(2,1)S(1)}, u32[]{:S(2)}, u32[]{:S(2)}) async-start(bf16[32,192,128]{2,1,0:T(8,128)(2,1)} %get-tuple-element.20), calls=%async_computation.2 | async-start | bytes 3145728 | tf_op jit(solution)/shard_map/all_to_all | solution.py:684
  57.0 60.6 %collective-permute-start.2 = (bf16[1536,384]{1,0:T(8,128)(2,1)S(1)}, bf16[1536,384]{1,0:T(8,128)(2,1)}, u32[]{:S(2)}, u32[]{:S(2)}) collective-permute-start(bf16[1536,384]{1,0:T(8,128)(2,1)S(1)} %pad_maximum_fusion), channel_id=1, source_target_pairs={{0,96},{32,0},{64,32},{96,64},{1,97},{33,1},{65,33},{97,65},{2,98}... | collective-permute-start | bytes 3538952 | tf_op jit(solution)/shard_map/ppermute | solution.py:422
  60.1 57.6 %collective-permute-start.1 = (bf16[1536,384]{1,0:T(8,128)(2,1)S(1)}, bf16[1536,384]{1,0:T(8,128)(2,1)}, u32[]{:S(2)}, u32[]{:S(2)}) collective-permute-start(bf16[1536,384]{1,0:T(8,128)(2,1)S(1)} %pad_maximum_fusion), channel_id=1, source_target_pairs={{0,64},{32,96},{64,0},{96,32},{1,65},{33,97},{65,1},{97,33},{2,66}... | collective-permute-start | bytes 3538952 | tf_op jit(solution)/shard_map/ppermute | solution.py:422
  60.7 56.9 %collective-permute-start = (bf16[1536,384]{1,0:T(8,128)(2,1)S(1)}, bf16[1536,384]{1,0:T(8,128)(2,1)}, u32[]{:S(2)}, u32[]{:S(2)}) collective-permute-start(bf16[1536,384]{1,0:T(8,128)(2,1)S(1)} %pad_maximum_fusion), channel_id=1, source_target_pairs={{0,32},{32,64},{64,96},{96,0},{1,33},{33,65},{65,97},{97,1},{2,34}... | collective-permute-start | bytes 3538952 | tf_op jit(solution)/shard_map/ppermute | solution.py:422
  117.7 21.3 %collective-permute-start.3 = (bf16[1536,384]{1,0:T(8,128)(2,1)}, bf16[1536,384]{1,0:T(8,128)(2,1)}, u32[]{:S(2)}, u32[]{:S(2)}) collective-permute-start(bf16[1536,384]{1,0:T(8,128)(2,1)} %collective-permute-done.rest_1_), channel_id=1, source_target_pairs={{0,4},{4,0},{8,12},{12,8},{16,20},{20,16},{24,28},{28,24},{1,5},{5... | collective-permute-start | bytes 3538952 | tf_op jit(solution)/shard_map/ppermute | solution.py:428
  117.8 21.2 %collective-permute-start.4 = (bf16[1536,384]{1,0:T(8,128)(2,1)}, bf16[1536,384]{1,0:T(8,128)(2,1)}, u32[]{:S(2)}, u32[]{:S(2)}) collective-permute-start(bf16[1536,384]{1,0:T(8,128)(2,1)} %collective-permute-done.1.rest_2_), channel_id=1, source_target_pairs={{0,4},{4,0},{8,12},{12,8},{16,20},{20,16},{24,28},{28,24},{1,5},{5... | collective-permute-start | bytes 3538952 | tf_op jit(solution)/shard_map/ppermute | solution.py:428
  118.3 20.7 %collective-permute-start.5 = (bf16[1536,384]{1,0:T(8,128)(2,1)}, bf16[1536,384]{1,0:T(8,128)(2,1)}, u32[]{:S(2)}, u32[]{:S(2)}) collective-permute-start(bf16[1536,384]{1,0:T(8,128)(2,1)} %collective-permute-done.2.rest_3_), channel_id=1, source_target_pairs={{0,4},{4,0},{8,12},{12,8},{16,20},{20,16},{24,28},{28,24},{1,5},{5... | collective-permute-start | bytes 3538952 | tf_op jit(solution)/shard_map/ppermute | solution.py:428
  118.3 20.6 %all-to-all-start.3 = ((bf16[32,64,128]{2,1,0:T(8,128)(2,1)}), bf16[32,64,128]{2,1,0:T(8,128)(2,1)S(1)}, u32[]{:S(2)}, u32[]{:S(2)}) async-start(bf16[32,64,128]{2,1,0:T(8,128)(2,1)} %attention.1), calls=%async_computation.3 | async-start | bytes 1048576 | tf_op jit(solution)/shard_map/all_to_all | solution.py:689
  125.6 1.0 copy-start.2
  137.9 1.1 copy-start.4
  139.0 1.3 copy-start.3
  140.3 1.0 copy-start.5
  150.6 7.6 %copy-start.9 = (bf16[768]{0:T(1024)(128)(2,1)S(1)}, bf16[768]{0:T(1024)(128)(2,1)}, u32[]{:S(2)}) copy-start(bf16[768]{0:T(1024)(128)(2,1)} %param.15) | copy-start | bytes 4612
  150.7 23.2 %copy-start.1 = (bf16[768,256]{1,0:T(8,128)(2,1)S(1)}, bf16[768,256]{1,0:T(8,128)(2,1)}, u32[]{:S(2)}) copy-start(bf16[768,256]{1,0:T(8,128)(2,1)} %dec_ref.1) | copy-start | bytes 1179652
  150.7 23.2 %all-to-all-start.4 = ((bf16[32,2,32,256]{3,2,1,0:T(8,128)(2,1)}), bf16[32,2,32,256]{3,2,1,0:T(8,128)(2,1)S(1)}, u32[]{:S(2)}, u32[]{:S(2)}) async-start(bf16[32,2,32,256]{3,2,1,0:T(8,128)(2,1)} %feed_forward.1), calls=%async_computation.4 | async-start | bytes 2097152 | tf_op jit(solution)/shard_map/all_to_all | solution.py:701
  173.9 1.7 copy-start.8

commit v8 on v7

--- a/solution.py
+++ b/solution.py
@@ -140,7 +140,7 @@
     )(my_start, twice)
 
 
-def project(arrived, token_col, qkv_weight, kept):
+def project(arrived, token_col, q_weight, qkv_weight, kept):
     peers, samples, cap, width = arrived.shape
     tile = peers * cap
     lanes = 2 * HD
@@ -148,12 +148,12 @@
     places = peers // samples
     half = kept // 2
 
-    def kernel(col_ref, arrived_ref, weight_hbm, x_hbm, out_ref, weight, x_ref, sems):
+    def kernel(col_ref, arrived_ref, weight_ref, weight_hbm, x_hbm, out_ref, weight, x_ref, sems):
         copies = []
-        for third in range(3):
+        for third in (1, 2):
             cols = pl.ds(third * width, width)
             copies.append(
-                pltpu.make_async_copy(weight_hbm.at[:, cols], weight.at[third], sems.at[third])
+                pltpu.make_async_copy(weight_hbm.at[:, cols], weight.at[third - 1], sems.at[third])
             )
             copies[-1].start()
         token = lax.broadcasted_iota(jnp.int32, (kept, 1), 0)
@@ -162,13 +162,13 @@
             chosen = one_hot(token, col_ref[sample])
             rows.append(dot(chosen, arrived_ref[:, sample].reshape(tile, width)))
             x_ref[sample] = rows[-1].astype(jnp.bfloat16)
-        keep = pltpu.make_async_copy(x_ref, x_hbm, sems.at[3])
+        keep = pltpu.make_async_copy(x_ref, x_hbm, sems.at[0])
         keep.start()
         normed = normalize(jnp.concatenate(rows, 0))
-        qkv = []
-        for third in range(3):
-            copies[third].wait()
-            qkv.append(dot(normed, weight[third]))
+        qkv = [dot(normed, weight_ref[...])]
+        for at, copy in enumerate(copies):
+            copy.wait()
+            qkv.append(dot(normed, weight[at]))
         low = lax.broadcasted_iota(jnp.int32, (kept, lanes), 1) < HD
         low_half = lax.broadcasted_iota(jnp.int32, (half, lanes), 1) < HD
         for sample in range(samples):
@@ -194,20 +194,23 @@
 
     return pl.pallas_call(
         kernel,
-        in_specs=[pl.BlockSpec(memory_space=pltpu.VMEM)] * 2 + [pl.BlockSpec(memory_space=pltpu.HBM)],
-        out_specs=[pl.BlockSpec(memory_space=pltpu.HBM), pl.BlockSpec(memory_space=pltpu.VMEM)],
+        in_specs=[pl.BlockSpec(memory_space=pltpu.VMEM)] * 3 + [pl.BlockSpec(memory_space=pltpu.HBM)],
+        out_specs=[
+            pl.BlockSpec(memory_space=pltpu.HBM),
+            pl.BlockSpec((peers, kept + half, lanes), lambda: (0, 0, 0)),
+        ],
         out_shape=[
             pltpu.HBM((samples, kept, width), jnp.bfloat16),
-            jax.ShapeDtypeStruct((peers, kept + half, lanes), jnp.bfloat16),
+            pltpu.HBM((peers, kept + half, lanes), jnp.bfloat16),
         ],
         scratch_shapes=[
-            pltpu.VMEM((3, width, width), jnp.bfloat16),
+            pltpu.VMEM((2, width, width), jnp.bfloat16),
             pltpu.VMEM((samples, kept, width), jnp.bfloat16),
-            pltpu.SemaphoreType.DMA((4,)),
+            pltpu.SemaphoreType.DMA((3,)),
         ],
         compiler_params=params(20),
         name="project",
-    )(token_col, arrived, in_hbm(qkv_weight))
+    )(token_col, arrived, q_weight, in_hbm(qkv_weight))
 
 
 def attention(packed, kept):
@@ -300,13 +303,13 @@
     )(packed)
 
 
-def fetch(arrays):
+def fetch(arrays, columns):
     count = len(arrays)
 
     def kernel(*refs):
         sources, held, sems = refs[:count], refs[count : 2 * count], refs[-1]
         copies = [
-            pltpu.make_async_copy(source, kept, sems.at[at])
+            pltpu.make_async_copy(source.at[:, pl.ds(0, columns)], kept, sems.at[at])
             for at, (source, kept) in enumerate(zip(sources, held))
         ]
         for copy in copies:
@@ -318,7 +321,7 @@
         kernel,
         in_specs=[pl.BlockSpec(memory_space=pltpu.HBM)] * count,
         out_specs=[pl.BlockSpec(memory_space=pltpu.VMEM)] * count,
-        out_shape=[pltpu.VMEM(one.shape, one.dtype) for one in arrays],
+        out_shape=[pltpu.VMEM((one.shape[0], columns), one.dtype) for one in arrays],
         scratch_shapes=[pltpu.SemaphoreType.DMA((count,))],
         compiler_params=params(2),
         name="fetch",
@@ -334,16 +337,14 @@
     weights = [in_hbm(one) for one in (down, *pieces, dec_proj)]
     count = len(weights)
 
-    def kernel(mixed_ref, x_ref, col_hbm, out_w, up_ref, *rest):
-        sources, out_ref, held = rest[:count], rest[count], rest[count + 1 : -2]
-        col_ref, sems = rest[-2:]
-        slots_in = pltpu.make_async_copy(col_hbm, col_ref, sems.at[count])
+    def kernel(mixed_ref, x_ref, col_ref, out_w, up_ref, *rest):
+        sources, out_ref, held = rest[:count], rest[count], rest[count + 1 : -1]
+        sems = rest[-1]
         copies = [
             pltpu.make_async_copy(source, held[at], sems.at[at])
             for at, source in enumerate(sources)
         ]
-        slots_in.start()
-        ahead = 4
+        ahead = count
         for copy in copies[:ahead]:
             copy.start()
 
@@ -385,26 +386,24 @@
             raised, lower = later, piece
         encoded = (x_one.astype(jnp.float32) + total).astype(jnp.bfloat16)
         field = dot(encoded, held[count - 1][...]).astype(jnp.bfloat16)
-        slots_in.wait()
         for sample in range(samples):
             token = lax.broadcasted_iota(jnp.int32, (1, kept), 1)
-            chosen = one_hot(col_ref[sample], token)
+            turned = jnp.broadcast_to(col_ref[sample].astype(jnp.float32), (kept, peers * slots)).T
+            chosen = one_hot(turned.astype(jnp.int32), token)
             sent = dot(chosen, field[sample * kept : (sample + 1) * kept])
             out_ref[:, sample] = sent.astype(jnp.bfloat16).reshape(peers, slots, narrow)
 
     return pl.pallas_call(
         kernel,
-        in_specs=[pl.BlockSpec(memory_space=pltpu.VMEM)] * 2
-        + [pl.BlockSpec(memory_space=pltpu.HBM)]
-        + [pl.BlockSpec(memory_space=pltpu.VMEM)] * 2
+        in_specs=[pl.BlockSpec(memory_space=pltpu.VMEM)] * 5
         + [pl.BlockSpec(memory_space=pltpu.HBM)] * count,
         out_specs=pl.BlockSpec(memory_space=pltpu.VMEM),
         out_shape=jax.ShapeDtypeStruct((peers, samples, slots, narrow), jnp.bfloat16),
         scratch_shapes=[pltpu.VMEM(one.shape, one.dtype) for one in weights]
-        + [pltpu.VMEM(token_col.shape, jnp.int32), pltpu.SemaphoreType.DMA((count + 1,))],
+        + [pltpu.SemaphoreType.DMA((count,))],
         compiler_params=params(32),
         name="feed_forward",
-    )(mixed, x, in_hbm(token_col), out_weight, up, *weights)
+    )(mixed, x, token_col, out_weight, up, *weights)
 
 
 def share(up_weight, down_weight):
@@ -513,7 +512,9 @@
             return pick(which, rows)
 
         position = (spread(begins) - me + peers - 1) // peers + nth
-        back_ref[0] = jnp.where(position * peers + me < spread(ends), position, -1)
+        back = jnp.where(position * peers + me < spread(ends), position, -1)
+        back = jnp.broadcast_to(back.astype(jnp.float32), (peers * SLOTS, 128)).T
+        back_ref[0] = back[:1].astype(jnp.int32)
 
         cell = lax.broadcasted_iota(jnp.int32, (cells, 1), 0)
         row, col = cell // wide, cell % wide
@@ -584,12 +585,12 @@
                 pl.BlockSpec((1, cells, 1), lambda s, _: (s, 0, 0)),
             ],
             out_specs=[
-                pl.BlockSpec((1, peers * SLOTS, 1), lambda s, _: (s, 0, 0)),
+                pl.BlockSpec((1, 1, peers * SLOTS), lambda s, _: (s, 0, 0)),
                 pl.BlockSpec((1, cells, 1), lambda s, _: (s, 0, 0)),
             ],
         ),
         out_shape=[
-            jax.ShapeDtypeStruct((samples, peers * SLOTS, 1), jnp.int32),
+            jax.ShapeDtypeStruct((samples, 1, peers * SLOTS), jnp.int32),
             jax.ShapeDtypeStruct((samples, cells, 1), jnp.int32),
         ],
         compiler_params=params(16),
@@ -680,12 +681,13 @@
         wide,
     )
 
-    x, packed = project(arrived, token.reshape(samples, 1, tile), qkv_weight, kept)
+    (q_near,) = fetch([qkv_weight], width)
+    x, packed = project(arrived, token.reshape(samples, 1, tile), q_near, qkv_weight, kept)
     packed = lax.all_to_all(packed, PLANE, split_axis=0, concat_axis=0, tiled=True)
     mixed = attention(packed, kept)
     mixed, *pieces = lax.optimization_barrier((mixed, *pieces))
     pieces = pieces + [from_partner(one) for one in pieces]
-    out_near, up_near = fetch([out_weight, up_weight])
+    out_near, up_near = fetch([out_weight, up_weight], width)
     mixed = lax.all_to_all(mixed, PLANE, split_axis=0, concat_axis=0, tiled=True)
     returning = feed_forward(
         mixed,

time: 187 us -> 185 us (0.989)
  waiting for transfers between devices: 54.5 us -> 52.2 us
    all_to_all x1, waiting for transfers between devices: 20.6 us -> 18.3 us  [shards(): lax.all_to_all(outgoing, PLANE, split_axis=0, concat_axis=0, tiled=True)]
    unnamed x20 -> x16, local copies, waits for them, and re-layouts: 4.35 us -> 3.38 us
  transfers between devices with their start and end apart: 11 -> 11, of which waited for: 4 -> 4; matrix products, arithmetic and copies ran while one was open for 2% -> 2% of each run, Pallas kernels for 30% -> 31%
where the time goes in v8:
time: 185 us; the launch traced here: 183 us
  Pallas kernels  72.7 us (39%)
  waiting for transfers between devices  52.2 us (28%)
  starting transfers between devices  37.4 us (20%)
  matrix products  11.1 us (6%)
  local copies, waits for them, and re-layouts  6.82 us (4%)
  other arithmetic  2.07 us (1%)
    pallas_call x1, Pallas kernels, attention(): pl.pallas_call(kernel, grid=(peers // step,), in_specs=[pl.BlockSpec(pack...  39.4 us
    all_to_all x1, waiting for transfers between devices, shards(): lax.all_to_all(outgoing, PLANE, split_axis=0, concat_axis=0, tiled=True)  18.3 us
    all_to_all x1, waiting for transfers between devices, shards(): lax.all_to_all(packed, PLANE, split_axis=0, concat_axis=0, tiled=True)  16.6 us
    all_to_all x1, waiting for transfers between devices, shards(): lax.all_to_all(returning, PLANE, split_axis=0, concat_axis=0, tiled=True)  15.5 us
    pallas_call x1, Pallas kernels, index(): pl.pallas_call(kernel, grid_spec=pltpu.PrefetchScalarGridSpec(num_scalar_...  11.3 us
    pallas_call x1, Pallas kernels, feed_forward(): pl.pallas_call(kernel, in_specs=[pl.BlockSpec(memory_space=pltpu.VMEM)] *...  8.99 us
    all_to_all x1, starting transfers between devices, shards(): lax.all_to_all(jnp.broadcast_to(counts.reshape(1, 1, counts.size), (peers...  8.46 us
    all_to_all x1, starting transfers between devices, shards(): lax.all_to_all(returning, PLANE, split_axis=0, concat_axis=0, tiled=True)  7.52 us
  transfers between devices with their start and end apart: 11, of which 4 were waited for; matrix products, arithmetic and copies ran while one was open for 2% of the time, Pallas kernels for 31%

profile of v8, /device:TPU:2, one launch (start us, length us, event | category | flops | bytes accessed | tf_op | source)
XLA Modules:
  0.0 182.8 jit_solution(10853759551596798891)
XLA Ops:
  2.6 8.5 %all-to-all-start = ((s32[32,1,372]{2,1,0:T(1,128)}), s32[32,1,372]{2,1,0:T(1,128)S(1)}, u32[]{:S(2)}, u32[]{:S(2)}) async-start(s32[32,1,372]{2,1,0:T(1,128)} %broadcast_in_dim.78), calls=%async_computation | async-start | bytes 98304 | tf_op jit(solution)/shard_map/all_to_all | solution.py:637
  13.0 2.5 %compact.1.twice_ref = bf16[64,2,16,768]{3,2,1,0:T(8,128)(2,1)S(1)} custom-call(s32[2,1,512]{2,1,0:T(1,128)S(1)} %reshape.258.rank_ref, bf16[2,512,768]{2,1,0:T(8,128)(2,1)} %bitcast.162), custom_call_target="tpu_custom_call" | custom-call | tf_op jit(solution)/shard_map/compact/pallas_call | solution.py:104
  15.5 1.8 all-to-all-done
  17.8 1.8 dispatch.1
  19.6 5.6 %all-to-all-start.1 = ((bf16[32,2,16,768]{3,2,1,0:T(8,128)(2,1)}), bf16[32,2,16,768]{3,2,1,0:T(8,128)(2,1)S(1)}, u32[]{:S(2)}, u32[]{:S(2)}) async-start(bf16[32,2,16,768]{3,2,1,0:T(8,128)(2,1)} %dispatch.1), calls=%async_computation.1 | async-start | bytes 3145728 | tf_op jit(solution)/shard_map/all_to_all | solution.py:662
  25.4 1.3 fetch.2.weight_ref
  27.3 1.1 constant_dynamic-slice_fusion
  28.5 18.3 %all-to-all-done.1.arrived_ref = bf16[32,2,16,768]{3,2,1,0:T(8,128)(2,1)S(1)} async-done(((bf16[32,2,16,768]{3,2,1,0:T(8,128)(2,1)}), bf16[32,2,16,768]{3,2,1,0:T(8,128)(2,1)S(1)}, u32[]{:S(2)}, u32[]{:S(2)}) %all-to-all-start.1) | async-done | bytes 1572896 | tf_op jit(solution)/shard_map/all_to_all | solution.py:662
  46.8 4.1 %project.1 = (bf16[2,128,768]{2,1,0:T(8,128)(2,1)}, bf16[32,192,128]{2,1,0:T(8,128)(2,1)}) custom-call(s32[2,1,512]{2,1,0:T(1,128)S(1)} %compare_select_fusion.col_ref, bf16[32,2,16,768]{3,2,1,0:T(8,128)(2,1)S(1)} %all-to-all-done.1.arrived_ref, bf16[768,768]{1,0:T(8,128)(2,1)S(1)} %fetch.2.weight_ref, bf16[768,2304]{1,0:T(8,128)(2,1)} %weight_hbm.1), custom_call_target="tpu_custom_call" | custom-call | tf_op jit(solution)/shard_map/project/pallas_call | solution.py:195
  50.9 5.2 %all-to-all-start.2 = ((bf16[32,192,128]{2,1,0:T(8,128)(2,1)}), bf16[32,192,128]{2,1,0:T(8,128)(2,1)S(1)}, u32[]{:S(2)}, u32[]{:S(2)}) async-start(bf16[32,192,128]{2,1,0:T(8,128)(2,1)} %get-tuple-element.20), calls=%async_computation.2 | async-start | bytes 3145728 | tf_op jit(solution)/shard_map/all_to_all | solution.py:686
  56.4 3.1 %collective-permute-start.2 = (bf16[1536,384]{1,0:T(8,128)(2,1)S(1)}, bf16[1536,384]{1,0:T(8,128)(2,1)}, u32[]{:S(2)}, u32[]{:S(2)}) collective-permute-start(bf16[1536,384]{1,0:T(8,128)(2,1)S(1)} %pad_maximum_fusion), channel_id=1, source_target_pairs={{0,96},{32,0},{64,32},{96,64},{1,97},{33,1},{65,33},{97,65},{2,98}... | collective-permute-start | bytes 3538952 | tf_op jit(solution)/shard_map/ppermute | solution.py:421
  61.1 16.6 %all-to-all-done.2.packed_ref = bf16[32,192,128]{2,1,0:T(8,128)(2,1)S(1)} async-done(((bf16[32,192,128]{2,1,0:T(8,128)(2,1)}), bf16[32,192,128]{2,1,0:T(8,128)(2,1)S(1)}, u32[]{:S(2)}, u32[]{:S(2)}) %all-to-all-start.2) | async-done | bytes 1572896 | tf_op jit(solution)/shard_map/all_to_all | solution.py:686
  77.6 39.4 %attention.1 = bf16[32,64,128]{2,1,0:T(8,128)(2,1)} custom-call(bf16[32,192,128]{2,1,0:T(8,128)(2,1)S(1)} %all-to-all-done.2.packed_ref), custom_call_target="tpu_custom_call" | custom-call | tf_op jit(solution)/shard_map/attention/pallas_call | solution.py:288
  117.7 5.1 %all-to-all-start.3 = ((bf16[32,64,128]{2,1,0:T(8,128)(2,1)}), bf16[32,64,128]{2,1,0:T(8,128)(2,1)S(1)}, u32[]{:S(2)}, u32[]{:S(2)}) async-start(bf16[32,64,128]{2,1,0:T(8,128)(2,1)} %attention.1), calls=%async_computation.3 | async-start | bytes 1048576 | tf_op jit(solution)/shard_map/all_to_all | solution.py:691
  123.3 1.6 fetch.3
  125.0 1.1 copy-done.2
  126.1 11.3 %index.1 = (s32[2,1,1024]{2,1,0:T(1,128)S(1)}, s32[2,800,1]{2,1,0:T(8,128)S(1)}) custom-call(s32[1]{0:T(128)} %bitcast.me_ref, s32[2,32,186]{2,1,0:T(8,128)S(1)} %bitcast.161, s32[2,800,1]{2,1,0:T(8,128)S(1)} %reshape.281.rank_ref), custom_call_target="tpu_custom_call" | custom-call | tf_op jit(solution)/shard_map/index/pallas_call | solution.py:578
  137.5 1.3 copy-done.3
  139.8 9.0 %feed_forward.1 = bf16[32,2,32,256]{3,2,1,0:T(8,128)(2,1)} custom-call(bf16[32,64,128]{2,1,0:T(8,128)(2,1)S(1)} %all-to-all-done.3.mixed_ref, bf16[2,128,768]{2,1,0:T(8,128)(2,1)S(1)} %copy-done.4, s32[2,1,1024]{2,1,0:T(1,128)S(1)} %get-tuple-element.25.col_ref, bf16[768,768]{1,0:T(8,128)(2,1)S(1)} %get-tuple-element.26.out_w, ...), custom_call_target="tpu_custom_call" | custom-call | tf_op jit(solution)/shard_map/feed_forward/pallas_call | solution.py:396
  148.8 7.5 %all-to-all-start.4 = ((bf16[32,2,32,256]{3,2,1,0:T(8,128)(2,1)}), bf16[32,2,32,256]{3,2,1,0:T(8,128)(2,1)S(1)}, u32[]{:S(2)}, u32[]{:S(2)}) async-start(bf16[32,2,32,256]{3,2,1,0:T(8,128)(2,1)} %feed_forward.1), calls=%async_computation.4 | async-start | bytes 2097152 | tf_op jit(solution)/shard_map/all_to_all | solution.py:703
  156.4 15.5 %all-to-all-done.4.home_ref = bf16[32,2,32,256]{3,2,1,0:T(8,128)(2,1)S(1)} async-done(((bf16[32,2,32,256]{3,2,1,0:T(8,128)(2,1)}), bf16[32,2,32,256]{3,2,1,0:T(8,128)(2,1)S(1)}, u32[]{:S(2)}, u32[]{:S(2)}) %all-to-all-start.4) | async-done | bytes 1048608 | tf_op jit(solution)/shard_map/all_to_all | solution.py:703
  172.0 1.7 place.1
  176.6 1.3 select_convert_fusion
  180.5 2.3 %convolution_convert_fusion = bf16[2,16,32,128]{3,2,1,0:T(8,128)(2,1)} fusion(f32[2,16,32,256]{3,2,1,0:T(8,128)S(1)} %convolution_add_fusion.1, bf16[2,18,34,256]{3,2,1,0:T(8,128)(2,1)S(1)} %select_convert_fusion, bf16[2,9,256,256]{3,2,1,0:T(8,128)(2,1)} %param.21, bf16[256,128]{1,0:T(8,128)(2,1)S(1)} %copy-done), kind=kOutput, calls=%fused_computation.9 | convolution fusion | flops 203554816 | bytes 2555904 | tf_op jit(solution)/shard_map/dot_general | solution.py:62
  (80 shorter events, 15.2 us)
Async XLA Ops:
  0.0 180.5 %copy-start = (bf16[256,128]{1,0:T(8,128)(2,1)S(1)}, bf16[256,128]{1,0:T(8,128)(2,1)}, u32[]{:S(2)}) copy-start(bf16[256,128]{1,0:T(8,128)(2,1)} %param.22) | copy-start | bytes 196612
  2.6 14.7 %all-to-all-start = ((s32[32,1,372]{2,1,0:T(1,128)}), s32[32,1,372]{2,1,0:T(1,128)S(1)}, u32[]{:S(2)}, u32[]{:S(2)}) async-start(s32[32,1,372]{2,1,0:T(1,128)} %broadcast_in_dim.78), calls=%async_computation | async-start | bytes 98304 | tf_op jit(solution)/shard_map/all_to_all | solution.py:637
  19.6 27.1 %all-to-all-start.1 = ((bf16[32,2,16,768]{3,2,1,0:T(8,128)(2,1)}), bf16[32,2,16,768]{3,2,1,0:T(8,128)(2,1)S(1)}, u32[]{:S(2)}, u32[]{:S(2)}) async-start(bf16[32,2,16,768]{3,2,1,0:T(8,128)(2,1)} %dispatch.1), calls=%async_computation.1 | async-start | bytes 3145728 | tf_op jit(solution)/shard_map/all_to_all | solution.py:662
  50.9 5.3 %copy-start.5 = (bf16[768,768]{1,0:T(8,128)(2,1)S(1)}, bf16[768,768]{1,0:T(8,128)(2,1)}, u32[]{:S(2)}) copy-start(bf16[768,768]{1,0:T(8,128)(2,1)} %rest_0_.1) | copy-start | bytes 3538948
  50.9 26.7 %all-to-all-start.2 = ((bf16[32,192,128]{2,1,0:T(8,128)(2,1)}), bf16[32,192,128]{2,1,0:T(8,128)(2,1)S(1)}, u32[]{:S(2)}, u32[]{:S(2)}) async-start(bf16[32,192,128]{2,1,0:T(8,128)(2,1)} %get-tuple-element.20), calls=%async_computation.2 | async-start | bytes 3145728 | tf_op jit(solution)/shard_map/all_to_all | solution.py:686
  56.4 60.7 %collective-permute-start.2 = (bf16[1536,384]{1,0:T(8,128)(2,1)S(1)}, bf16[1536,384]{1,0:T(8,128)(2,1)}, u32[]{:S(2)}, u32[]{:S(2)}) collective-permute-start(bf16[1536,384]{1,0:T(8,128)(2,1)S(1)} %pad_maximum_fusion), channel_id=1, source_target_pairs={{0,96},{32,0},{64,32},{96,64},{1,97},{33,1},{65,33},{97,65},{2,98}... | collective-permute-start | bytes 3538952 | tf_op jit(solution)/shard_map/ppermute | solution.py:421
  59.5 57.6 %collective-permute-start.1 = (bf16[1536,384]{1,0:T(8,128)(2,1)S(1)}, bf16[1536,384]{1,0:T(8,128)(2,1)}, u32[]{:S(2)}, u32[]{:S(2)}) collective-permute-start(bf16[1536,384]{1,0:T(8,128)(2,1)S(1)} %pad_maximum_fusion), channel_id=1, source_target_pairs={{0,64},{32,96},{64,0},{96,32},{1,65},{33,97},{65,1},{97,33},{2,66}... | collective-permute-start | bytes 3538952 | tf_op jit(solution)/shard_map/ppermute | solution.py:421
  60.1 57.0 %collective-permute-start = (bf16[1536,384]{1,0:T(8,128)(2,1)S(1)}, bf16[1536,384]{1,0:T(8,128)(2,1)}, u32[]{:S(2)}, u32[]{:S(2)}) collective-permute-start(bf16[1536,384]{1,0:T(8,128)(2,1)S(1)} %pad_maximum_fusion), channel_id=1, source_target_pairs={{0,32},{32,64},{64,96},{96,0},{1,33},{33,65},{65,97},{97,1},{2,34}... | collective-permute-start | bytes 3538952 | tf_op jit(solution)/shard_map/ppermute | solution.py:421
  117.0 20.4 %collective-permute-start.3 = (bf16[1536,384]{1,0:T(8,128)(2,1)}, bf16[1536,384]{1,0:T(8,128)(2,1)}, u32[]{:S(2)}, u32[]{:S(2)}) collective-permute-start(bf16[1536,384]{1,0:T(8,128)(2,1)} %collective-permute-done.rest_1_), channel_id=1, source_target_pairs={{0,4},{4,0},{8,12},{12,8},{16,20},{20,16},{24,28},{28,24},{1,5},{5... | collective-permute-start | bytes 3538952 | tf_op jit(solution)/shard_map/ppermute | solution.py:427
  117.1 20.3 %collective-permute-start.4 = (bf16[1536,384]{1,0:T(8,128)(2,1)}, bf16[1536,384]{1,0:T(8,128)(2,1)}, u32[]{:S(2)}, u32[]{:S(2)}) collective-permute-start(bf16[1536,384]{1,0:T(8,128)(2,1)} %collective-permute-done.1.rest_2_), channel_id=1, source_target_pairs={{0,4},{4,0},{8,12},{12,8},{16,20},{20,16},{24,28},{28,24},{1,5},{5... | collective-permute-start | bytes 3538952 | tf_op jit(solution)/shard_map/ppermute | solution.py:427
  117.6 19.8 %collective-permute-start.5 = (bf16[1536,384]{1,0:T(8,128)(2,1)}, bf16[1536,384]{1,0:T(8,128)(2,1)}, u32[]{:S(2)}, u32[]{:S(2)}) collective-permute-start(bf16[1536,384]{1,0:T(8,128)(2,1)} %collective-permute-done.2.rest_3_), channel_id=1, source_target_pairs={{0,4},{4,0},{8,12},{12,8},{16,20},{20,16},{24,28},{28,24},{1,5},{5... | collective-permute-start | bytes 3538952 | tf_op jit(solution)/shard_map/ppermute | solution.py:427
  117.7 19.7 %all-to-all-start.3 = ((bf16[32,64,128]{2,1,0:T(8,128)(2,1)}), bf16[32,64,128]{2,1,0:T(8,128)(2,1)S(1)}, u32[]{:S(2)}, u32[]{:S(2)}) async-start(bf16[32,64,128]{2,1,0:T(8,128)(2,1)} %attention.1), calls=%async_computation.3 | async-start | bytes 1048576 | tf_op jit(solution)/shard_map/all_to_all | solution.py:691
  125.0 1.1 copy-start.2
  137.5 1.3 copy-start.3
  138.8 1.0 copy-start.4
  148.7 7.6 %copy-start.7 = (bf16[768]{0:T(1024)(128)(2,1)S(1)}, bf16[768]{0:T(1024)(128)(2,1)}, u32[]{:S(2)}) copy-start(bf16[768]{0:T(1024)(128)(2,1)} %param.15) | copy-start | bytes 4612
  148.8 23.2 %copy-start.1 = (bf16[768,256]{1,0:T(8,128)(2,1)S(1)}, bf16[768,256]{1,0:T(8,128)(2,1)}, u32[]{:S(2)}) copy-start(bf16[768,256]{1,0:T(8,128)(2,1)} %dec_ref.1) | copy-start | bytes 1179652
  148.8 23.2 %all-to-all-start.4 = ((bf16[32,2,32,256]{3,2,1,0:T(8,128)(2,1)}), bf16[32,2,32,256]{3,2,1,0:T(8,128)(2,1)S(1)}, u32[]{:S(2)}, u32[]{:S(2)}) async-start(bf16[32,2,32,256]{3,2,1,0:T(8,128)(2,1)} %feed_forward.1), calls=%async_computation.4 | async-start | bytes 2097152 | tf_op jit(solution)/shard_map/all_to_all | solution.py:703
  172.0 1.7 copy-start.6
